TPU v7x, 128 devices: a whole 4x4x4 slice. The times are simulated.
128 devices in a mesh: ep: 32 (over z, y, core), dp: 4 (over x).
Axes of the slice: x: 4, y: 4, z: 4, core: 2. Of those that a mesh axis runs over, the one named last changes fastest.
Arguments:
- tokens: bfloat16 [16384, 7168], P(('dp', 'ep')), parts along dimension 0, may hold values from -18 to 18
- expert_ids: int32 [16384, 2], P(('dp', 'ep')), parts along dimension 0, may hold values from 0 to 15, all different within a row; in each aligned block of 128 rows (0 to 127, 128 to 255, ...) at most 32 rows name the same one
- affinity: float32 [16384, 2], P(('dp', 'ep')), parts along dimension 0, may hold values from 0.05 to 1
- w_gate: bfloat16 [32, 7168, 512], P('ep'), may hold values from -0.0625 to 0.0625
- w_up: bfloat16 [32, 7168, 512], P('ep'), may hold values from -0.0625 to 0.0625
- w_down: bfloat16 [32, 512, 7168], P('ep'), may hold values from -0.1875 to 0.1875
Outputs:
- mixed: bfloat16 [16384, 7168], P(('dp', 'ep')), parts along dimension 0
There are 4 independent parts, one for each index of `dp`. A program takes and returns all parts, laid end to end along the dimension named above; an argument that names none is the same for every part. Nothing has to cross between parts.
Inputs may be any that keep to these rules, and one draw needn't show every extreme that they name: `expert_ids`: each row names 2 different experts; among the rows of one index of ep no expert is named by more than 32 rows.
All inputs are finite; a program needn't handle non-finite values.
Results may differ from a plain program's by a relative error of at most 0.019.
Values may be sent and summed in bfloat16 or wider, within the bound.
No kernel may reach another device: no remote copies, remote signals or barrier semaphores. Data moves between devices by JAX's collectives and lax.ppermute only.
A program may use at most 256 MiB of HBM per device.

v0:
```python
import jax
import jax.numpy as jnp
from jax import lax
from jax.sharding import PartitionSpec as P

TOP = 2
TOK_DEV = 128


def side_by_side(arrays, axis, split_dim, concat_dim, along):
    both = jnp.concatenate(arrays, axis=along)
    result, at, done = (
        lax.all_to_all(both, axis, split_axis=split_dim, concat_axis=concat_dim, tiled=True),
        0,
        [],
    )
    for a in arrays:
        done.append(lax.slice_in_dim(result, at, at + a.shape[along], axis=along))
        at += a.shape[along]
    return tuple(done)


def from_partner(value, axis, distance):
    mask = 2**distance
    pairs = [(source, source ^ mask) for source in range(lax.axis_size(axis))]
    return lax.ppermute(value, axis, pairs)


def quantize(tokens):
    count_rows = tokens.shape[0]
    blocks = tokens.astype(jnp.float32).reshape(count_rows, -1, 16)
    largest = jnp.max(jnp.abs(blocks), axis=2)
    scales = (jnp.maximum(largest, 0.25) / 9.0).astype(jnp.bfloat16)
    divided = blocks / scales.astype(jnp.float32)[:, :, None]
    payload = jnp.clip(divided, -6.0, 6.0).astype(jnp.bfloat16).reshape(count_rows, -1)
    return (payload, scales)


def restore(payload, scales):
    count_rows = payload.shape[0]
    values = (
        payload.astype(jnp.float32).reshape(count_rows, -1, 16)
        * scales.astype(jnp.float32)[:, :, None]
    )
    return values.astype(jnp.bfloat16).reshape(count_rows, -1)


def half_expert(restored, gate_half, up_half, down_half):
    gate = jnp.dot(restored, gate_half, preferred_element_type=jnp.float32)
    upward = jnp.dot(restored, up_half, preferred_element_type=jnp.float32)
    hidden = (jax.nn.silu(gate) * upward).astype(jnp.bfloat16)
    return jnp.dot(hidden, down_half, preferred_element_type=jnp.float32).astype(jnp.bfloat16)


def filled_rows(payload, scales, gate_half, up_half, down_half):
    count_rows = payload.shape[0]
    row_width = payload.shape[1]
    block_rows = 256
    padded_rows = -(-count_rows // block_rows) * block_rows
    empty_slot = (scales[:, 0] <= 0.0).astype(jnp.int32)
    ordering = jnp.argsort(empty_slot, stable=True)
    live_rows = count_rows - jnp.sum(empty_slot)
    packed = payload[ordering]
    packed_scales = scales[ordering]
    blocks_live = (live_rows + block_rows - 1) // block_rows

    def one_block(number, result):
        offset = number * block_rows
        block_payload = lax.dynamic_slice_in_dim(packed, offset, block_rows, 0)
        block_scales = lax.dynamic_slice_in_dim(packed_scales, offset, block_rows, 0)
        computed = half_expert(restore(block_payload, block_scales), gate_half, up_half, down_half)
        return lax.dynamic_update_slice_in_dim(result, computed, offset, 0)

    result = lax.fori_loop(
        0, blocks_live, one_block, jnp.zeros((padded_rows, row_width), jnp.bfloat16)
    )
    return jnp.zeros((count_rows, row_width), jnp.bfloat16).at[ordering].set(result)


def expert_rows(payload, scales, gate_half, up_half, down_half):
    return filled_rows(payload, scales, gate_half, up_half, down_half)


def on_device(tokens, expert_ids, affinity, w_gate, w_up, w_down):
    ep_count = lax.axis_size("ep")
    experts = ep_count // 2
    capacity = 2 * TOK_DEV * TOP // experts
    tok_rows = tokens.shape[0]
    row_width = tokens.shape[1]
    scale_width = row_width // 16
    gate_half = w_gate[0]
    up_half = w_up[0]
    down_half = w_down[0]
    payload, scales = quantize(tokens)
    flat_ids = expert_ids.reshape(-1)
    assigned = flat_ids.shape[0]
    one_hot = (flat_ids[:, None] == jnp.arange(experts, dtype=jnp.int32)[None, :]).astype(jnp.int32)
    running = jnp.cumsum(one_hot, axis=0) - 1
    within = jnp.sum(running * one_hot, axis=1)
    slot_index = flat_ids * capacity + within
    slot_total = experts * capacity
    source_row = (
        jnp.zeros((slot_total,), jnp.int32)
        .at[slot_index]
        .set(jnp.arange(assigned, dtype=jnp.int32) // TOP)
    )
    filled = jnp.zeros((slot_total,), jnp.int32).at[slot_index].set(1) > 0
    send_payload = jnp.where(filled[:, None], payload[source_row], jnp.zeros((), jnp.bfloat16))
    send_scales = jnp.where(filled[:, None], scales[source_row], jnp.zeros((), jnp.bfloat16))
    half_cap = capacity // 2
    split_payload = send_payload.reshape(ep_count, half_cap, row_width)
    split_scales = send_scales.reshape(ep_count, half_cap, scale_width)
    got_payload, got_scales = side_by_side((split_payload, split_scales), "ep", 0, 0, 2)
    mate_payload, mate_scales = from_partner((got_payload, got_scales), "ep", 0)
    upper_half = lax.axis_index("ep") % 2 == 1
    lower_payload = jnp.where(upper_half, mate_payload, got_payload)
    higher_payload = jnp.where(upper_half, got_payload, mate_payload)
    lower_scales = jnp.where(upper_half, mate_scales, got_scales)
    higher_scales = jnp.where(upper_half, got_scales, mate_scales)
    full_payload = jnp.concatenate([lower_payload, higher_payload], axis=1)
    full_scales = jnp.concatenate([lower_scales, higher_scales], axis=1)
    computed = expert_rows(
        full_payload.reshape(-1, row_width),
        full_scales.reshape(-1, scale_width),
        gate_half,
        up_half,
        down_half,
    )
    computed = computed.reshape(ep_count, capacity, row_width)
    lower_part = computed[:, :half_cap]
    higher_part = computed[:, half_cap:]
    own_part = jnp.where(upper_half, higher_part, lower_part)
    mate_part = jnp.where(upper_half, lower_part, higher_part)
    received = from_partner(mate_part, "ep", 0)
    summed = (own_part.astype(jnp.float32) + received.astype(jnp.float32)).astype(jnp.bfloat16)
    expert_out = lax.all_to_all(summed, "ep", split_axis=0, concat_axis=0, tiled=True).reshape(
        slot_total, row_width
    )
    per_slot = expert_out[slot_index].astype(jnp.float32).reshape(tok_rows, TOP, row_width)
    weights = affinity / jnp.sum(affinity, axis=1, keepdims=True)
    return jnp.sum(weights[:, :, None] * per_slot, axis=1).astype(jnp.bfloat16)


def solution(mesh):
    in_specs = (
        P(("dp", "ep"), None),
        P(("dp", "ep"), None),
        P(("dp", "ep"), None),
        P("ep", None, None),
        P("ep", None, None),
        P("ep", None, None),
    )
    out_specs = P(("dp", "ep"), None)
    return jax.shard_map(
        on_device, mesh=mesh, in_specs=in_specs, out_specs=out_specs, check_vma=False
    )
```

profile of v0, /device:TPU:0, one launch (start us, length us, event | category | flops | bytes accessed | tf_op | source)
XLA Modules:
  0.0 513.5 jit_solution(1612174605001306442)
XLA Ops:
  8.1 5.3 %copy.34 = f32[128,7168]{0,1:T(8,128)} copy(f32[128,7168]{1,0:T(8,128)} %convert_abs_fusion) | data formatting | bytes 7340032 | tf_op jit(solution)/shard_map/abs | solution.py:32
  18.2 5.2 %copy.35 = f32[128,7168]{1,0:T(8,128)} copy(f32[128,7168]{0,1:T(8,128)} %bitcast.65) | data formatting | bytes 7340032 | tf_op jit(solution)/shard_map/div | solution.py:34
  28.2 7.0 %gather_fusion = bf16[512,7168]{1,0:T(8,128)(2,1)} fusion(bf16[128,7168]{1,0:T(8,128)(2,1)S(1)} %fusion.6, s32[1024]{0:T(1024)S(1)} %pad_clamp_fusion.1), kind=kCustom, calls=%fused_computation | custom fusion | bytes 14682112 | tf_op jit(solution)/shard_map/gather | solution.py:108
  37.2 6.6 %broadcast_select_fusion = bf16[32,16,7168]{2,1,0:T(8,128)(2,1)} fusion(bf16[32,16,7168]{2,1,0:T(8,128)(2,1)} %bitcast.63, pred[32,16]{1,0:T(8,128)(4,1)S(1)} %broadcast_in_dim.49), kind=kLoop, calls=%fused_computation.22 | loop fusion | flops 3670016 | bytes 14680576 | tf_op jit(solution)/shard_map/jit(_where)/select_n | solution.py:108
  43.9 6.8 %pad_maximum_fusion.1 = bf16[32,16,7616]{2,1,0:T(8,128)(2,1)} fusion(bf16[32,16,448]{2,1,0:T(8,128)(2,1)S(1)} %broadcast_select_fusion.4, bf16[32,16,7168]{2,1,0:T(8,128)(2,1)} %broadcast_select_fusion), kind=kLoop, calls=%fused_computation.18 | loop fusion | flops 15597568 | bytes 15597568 | tf_op jit(solution)/shard_map/concatenate | solution.py:11
  50.8 98.8 %all_to_all.10 = bf16[32,16,7616]{2,1,0:T(8,128)(2,1)S(1)} all-to-all(bf16[32,16,7616]{2,1,0:T(8,128)(2,1)} %pad_maximum_fusion.1), channel_id=1, replica_groups=mesh['ep'=32,'dp'=4] {'ep'}, dimensions={0} | all-to-all | bytes 15597568 | tf_op jit(solution)/shard_map/all_to_all | solution.py:13
  149.6 4.4 slice.41
  155.3 11.1 %collective-permute-done = bf16[32,16,448]{2,1,0:T(8,128)(2,1)S(1)} collective-permute-done((bf16[32,16,448]{2,1,0:T(8,128)(2,1)S(1)}, bf16[32,16,448]{2,1,0:T(8,128)(2,1)S(1)}, u32[]{:S(2)}, u32[]{:S(2)}) %collective-permute-start) | collective-permute-done | bytes 458784 | tf_op jit(solution)/shard_map/ppermute | solution.py:26
  169.2 4.4 sort.17
  179.4 5.9 %broadcast_select_fusion.3 = (bf16[32,16,7168]{2,1,0:T(8,128)(2,1)S(1)}, bf16[32,16,7168]{2,1,0:T(8,128)(2,1)S(1)}) fusion(bf16[32,16,7168]{2,1,0:T(8,128)(2,1)} %collective-permute-done.1, pred[]{:T(512)S(6)} %eq.30, bf16[32,16,7616]{2,1,0:T(8,128)(2,1)} %copy-done), kind=kLoop, calls=%fused_computation.25 | loop fusion | flops 7340032 | bytes 29360128 | tf_op jit(solution)/shard_map/jit(_where)/select_n | solution.py:116
  185.3 6.7 %pad_maximum_fusion = bf16[32,32,7168]{2,1,0:T(8,128)(2,1)} fusion(bf16[32,16,7168]{2,1,0:T(8,128)(2,1)S(1)} %get-tuple-element.94, bf16[32,16,7168]{2,1,0:T(8,128)(2,1)S(1)} %get-tuple-element.93), kind=kLoop, calls=%fused_computation.16 | loop fusion | flops 29360128 | bytes 29360128 | tf_op jit(solution)/shard_map/concatenate | solution.py:120
  192.0 31.8 %gather_fusion.2 = bf16[1024,7168]{1,0:T(8,128)(2,1)} fusion(bf16[1024,7168]{1,0:T(8,128)(2,1)} %bitcast.52, s32[1024]{0:T(1024)S(1)} %get-tuple-element.97), kind=kCustom, calls=%fused_computation.2 | custom fusion | bytes 29364224 | tf_op jit(solution)/shard_map/gather | solution.py:63
  223.8 7.0 %broadcast.104 = bf16[1024,7168]{1,0:T(8,128)(2,1)} broadcast(bf16[]{:T(256)} %constant.84.clone.1), dimensions={} | broadcast | bytes 14680066 | tf_op jit(solution)/shard_map/broadcast.9
  230.8 23.6 %while.10 = (s32[]{:T(128)}, bf16[1024,7168]{1,0:T(8,128)(2,1)}, s32[]{:T(128)}, bf16[1024,7168]{1,0:T(8,128)(2,1)}, bf16[1024,448]{0,1:T(8,128)(2,1)}, /*index=...) while((s32[]{:T(128)}, bf16[1024,7168]{1,0:T(8,128)(2,1)}, ...), condition=%wide.region_10.11_spmd, body=%wide.region_9.10_spmd.sunk | while | flops 5645385728 | bytes 123830584 | solution.py:74
  235.3 6.1 %copy.43 = bf16[256,7168]{0,1:T(8,128)(2,1)} copy(bf16[256,7168]{1,0:T(8,128)(2,1)} %constant_dynamic-slice_fusion.2) | data formatting | bytes 7340032 | tf_op jit(solution)/shard_map/while/body/dynamic_slice | solution.py:69
  254.4 29.3 %scatter_custom_fusion.2 = bf16[1024,7168]{1,0:T(8,128)(2,1)} fusion(s32[1024]{0:T(1024)} %get-tuple-element.98, bf16[1024,7168]{1,0:T(8,128)(2,1)} %get-tuple-element.50, bf16[]{:T(256)} %constant.84.clone.1), kind=kCustom, calls=%fused_computation.20 | custom fusion | bytes 14680576 | tf_op jit(solution)/shard_map/scatter | solution.py:77
  283.7 8.9 %broadcast_select_fusion.1 = bf16[32,16,7168]{2,1,0:T(8,128)(2,1)} fusion(pred[]{:T(512)S(6)} %eq.30, bf16[32,32,7168]{2,1,0:T(8,128)(2,1)} %bitcast.59), kind=kLoop, calls=%fused_computation.23 | loop fusion | flops 3670016 | bytes 22020096 | tf_op jit(solution)/shard_map/jit(_where)/select_n | solution.py:133
  292.7 11.7 %collective-permute-done.2 = bf16[32,16,7168]{2,1,0:T(8,128)(2,1)S(1)} collective-permute-done((bf16[32,16,7168]{2,1,0:T(8,128)(2,1)}, bf16[32,16,7168]{2,1,0:T(8,128)(2,1)S(1)}, u32[]{:S(2)}, u32[]{:S(2)}) %collective-permute-start.2) | collective-permute-done | bytes 7340064 | tf_op jit(solution)/shard_map/ppermute | solution.py:26
  304.4 9.6 %add_convert_fusion = bf16[32,16,7168]{2,1,0:T(8,128)(2,1)} fusion(bf16[32,16,7168]{2,1,0:T(8,128)(2,1)S(1)} %collective-permute-done.2, pred[]{:T(512)S(6)} %eq.30, bf16[32,32,7168]{2,1,0:T(8,128)(2,1)} %bitcast.60), kind=kLoop, calls=%fused_computation.17 | loop fusion | flops 18350080 | bytes 29360128 | tf_op jit(solution)/shard_map/convert_element_type | solution.py:135
  314.1 73.6 %all-to-all-start.1 = ((bf16[32,16,7168]{2,1,0:T(8,128)(2,1)}), bf16[32,16,7168]{2,1,0:T(8,128)(2,1)}, u32[]{:S(2)}, u32[]{:S(2)}) async-start(bf16[32,16,7168]{2,1,0:T(8,128)(2,1)} %add_convert_fusion), calls=%async_computation.1 | async-start | bytes 14680064 | tf_op jit(solution)/shard_map/all_to_all | solution.py:136
  387.9 92.1 %all-to-all-done.1 = bf16[32,16,7168]{2,1,0:T(8,128)(2,1)} async-done(((bf16[32,16,7168]{2,1,0:T(8,128)(2,1)}), bf16[32,16,7168]{2,1,0:T(8,128)(2,1)}, u32[]{:S(2)}, u32[]{:S(2)}) %all-to-all-start.1) | async-done | bytes 7340064 | tf_op jit(solution)/shard_map/all_to_all | solution.py:136
  480.0 12.1 %gather_fusion.4 = bf16[256,7168]{1,0:T(8,128)(2,1)} fusion(bf16[512,7168]{1,0:T(8,128)(2,1)} %bitcast.14, s32[1024]{0:T(1024)S(1)} %pad_clamp_fusion), kind=kCustom, calls=%fused_computation.4 | custom fusion | bytes 7341056 | tf_op jit(solution)/shard_map/gather | solution.py:139
  492.1 8.6 %reshape.102 = f32[128,2,7168]{2,1,0:T(2,128)} reshape(bf16[256,7168]{1,0:T(8,128)(2,1)} %gather_fusion.4) | data formatting | bytes 11010048 | tf_op jit(solution)/shard_map/convert_element_type | solution.py:139
  500.7 12.4 %multiply_reduce_fusion = bf16[128,7168]{1,0:T(8,128)(2,1)} fusion(f32[128,2,7168]{2,1,0:T(2,128)} %reshape.102, f32[128,2]{1,0:T(8,128)S(1)} %copy.29), kind=kLoop, calls=%fused_computation.19 | loop fusion | flops 2752512 | bytes 9176064 | tf_op jit(solution)/shard_map/reduce_sum | solution.py:141
  (74 shorter events, 46.0 us)
Async XLA Ops:
  2.9 23.7 %copy-start.1 = (s32[256,1]{0,1:T(1,128)}, s32[256,1]{0,1:T(1,128)S(1)}, u32[]{:S(2)}) copy-start(s32[256,1]{0,1:T(1,128)S(1)} %compare_select_fusion.1) | copy-start | bytes 3076
  149.6 5.3 %copy-start = (bf16[32,16,7616]{2,1,0:T(8,128)(2,1)}, bf16[32,16,7616]{2,1,0:T(8,128)(2,1)S(1)}, u32[]{:S(2)}) copy-start(bf16[32,16,7616]{2,1,0:T(8,128)(2,1)S(1)} %all_to_all.10) | copy-start | bytes 23396356
  154.0 25.3 %collective-permute-start.1 = (bf16[32,16,7168]{2,1,0:T(8,128)(2,1)}, bf16[32,16,7168]{2,1,0:T(8,128)(2,1)}, u32[]{:S(2)}, u32[]{:S(2)}) collective-permute-start(bf16[32,16,7168]{2,1,0:T(8,128)(2,1)} %slice.41), channel_id=1, source_target_pairs={{0,4},{4,0},{8,12},{12,8},{16,20},{20,16},{24,28},{28,24},{32,36},... | collective-permute-start | bytes 22020104 | tf_op jit(solution)/shard_map/ppermute | solution.py:26
  155.0 11.5 %collective-permute-start = (bf16[32,16,448]{2,1,0:T(8,128)(2,1)S(1)}, bf16[32,16,448]{2,1,0:T(8,128)(2,1)S(1)}, u32[]{:S(2)}, u32[]{:S(2)}) collective-permute-start(bf16[32,16,448]{2,1,0:T(8,128)(2,1)S(1)} %slice.39), channel_id=1, source_target_pairs={{0,4},{4,0},{8,12},{12,8},{16,20},{20,16},{24,28},{28,24},{32,36},... | collective-permute-start | bytes 1376264 | tf_op jit(solution)/shard_map/ppermute | solution.py:26
  235.3 10.2 %slice-start = ((s8[7340032]{0:T(1024)(128)(4,1)}), s8[3145728]{0:T(1024)(128)(4,1)S(1)}, s32[]{:S(2)}) async-start(s8[7340032]{0:T(1024)(128)(4,1)} %bitcast.54), calls=%async_computation.2 | async-start | bytes 6291456 | tf_op jit(solution)/shard_map/while
  241.4 4.2 slice-start.1
  242.5 5.2 %slice-start.2 = ((s8[7340032]{0:T(1024)(128)(4,1)}), s8[4194304]{0:T(1024)(128)(4,1)S(1)}, s32[]{:S(2)}) async-start(s8[7340032]{0:T(1024)(128)(4,1)} %bitcast.57), calls=%async_computation.4 | async-start | bytes 8388608 | tf_op jit(solution)/shard_map/while
  242.5 8.0 %slice-start.4 = ((s8[7340032]{0:T(1024)(128)(4,1)}), s8[4194304]{0:T(1024)(128)(4,1)S(1)}, s32[]{:S(2)}) async-start(s8[7340032]{0:T(1024)(128)(4,1)} %bitcast.72), calls=%async_computation.6 | async-start | bytes 8388608 | tf_op jit(solution)/shard_map/while
  245.6 2.8 slice-start.3
  245.6 4.9 slice-start.5
  292.6 11.9 %collective-permute-start.2 = (bf16[32,16,7168]{2,1,0:T(8,128)(2,1)}, bf16[32,16,7168]{2,1,0:T(8,128)(2,1)S(1)}, u32[]{:S(2)}, u32[]{:S(2)}) collective-permute-start(bf16[32,16,7168]{2,1,0:T(8,128)(2,1)} %broadcast_select_fusion.1), channel_id=1, source_target_pairs={{0,4},{4,0},{8,12},{12,8},{16,20},{20,16},{24,28},{28,24},{32,36},... | collective-permute-start | bytes 22020104 | tf_op jit(solution)/shard_map/ppermute | solution.py:26
  314.1 73.6 %copy-start.3 = (f32[128,2]{0,1:T(2,128)S(1)}, f32[128,2]{0,1:T(2,128)}, u32[]{:S(2)}) copy-start(f32[128,2]{0,1:T(2,128)} %param.10) | copy-start | bytes 3076
  314.1 73.8 %copy-start.2 = (s32[256,1]{0,1:T(1,128)S(1)}, s32[256,1]{0,1:T(1,128)}, u32[]{:S(2)}) copy-start(s32[256,1]{0,1:T(1,128)} %copy-done.1) | copy-start | bytes 3076
  314.1 165.9 %all-to-all-start.1 = ((bf16[32,16,7168]{2,1,0:T(8,128)(2,1)}), bf16[32,16,7168]{2,1,0:T(8,128)(2,1)}, u32[]{:S(2)}, u32[]{:S(2)}) async-start(bf16[32,16,7168]{2,1,0:T(8,128)(2,1)} %add_convert_fusion), calls=%async_computation.1 | async-start | bytes 14680064 | tf_op jit(solution)/shard_map/all_to_all | solution.py:136
where the time goes:
time: 523 us; the launch traced here: 513 us
  local copies, waits for them, and re-layouts  137 us (26%)
  waiting for transfers between devices  115 us (22%)
  blocking collectives  98.8 us (19%)
  other arithmetic  79.2 us (15%)
  starting transfers between devices  74.2 us (14%)
  matrix products  8.03 us (2%)
    all_to_all x1, blocking collectives, side_by_side(): lax.all_to_all(both, axis, split_axis=split_dim, concat_axis=concat_dim,...  98.8 us
    all_to_all x1, waiting for transfers between devices, on_device(): lax.all_to_all(summed, 'ep', split_axis=0, concat_axis=0, tiled=True)  92.1 us
    all_to_all x1, starting transfers between devices, on_device(): lax.all_to_all(summed, 'ep', split_axis=0, concat_axis=0, tiled=True)  73.6 us
    gather x1, local copies, waits for them, and re-layouts, filled_rows(): packed = payload[ordering]  31.8 us
    scatter x1, local copies, waits for them, and re-layouts, filled_rows(): jnp.zeros((count_rows, row_width), jnp.bfloat16).at[ordering].set(result)  29.3 us
    ppermute x3, waiting for transfers between devices, from_partner(): return lax.ppermute(value, axis, pairs)  22.9 us
    reduce_sum x1, other arithmetic, on_device(): return jnp.sum(weights[:, :, None] * per_slot, axis=1).astype(jnp.bfloat16)  12.4 us
    gather x1, local copies, waits for them, and re-layouts, on_device(): expert_out[slot_index].astype(jnp.float32).reshape(tok_rows, TOP, row_width)  12.1 us
  transfers between devices with their start and end apart: 4, of which 3 were waited for; matrix products, arithmetic and copies ran while one was open for 2% of the time, Pallas kernels for 0%

commit v1 on v0

v1 whole, which is shorter than its diff:
```python
import functools
import jax
import jax.numpy as jnp
from jax import lax
from jax.experimental import pallas as pl
from jax.experimental.pallas import tpu as pltpu
from jax.sharding import PartitionSpec as P

TOP = 2
BLOCK = 16
LANES = 128
VMEM_BYTES = 56 * 1024 * 1024


def iota(shape, dim):
    return lax.broadcasted_iota(jnp.int32, shape, dim)


def named(ids_ref, experts):
    ids = ids_ref[...]
    lanes = iota((ids.shape[0], experts), 1)
    hit = ids[:, 0:1] == lanes
    for k in range(1, TOP):
        hit = hit | (ids[:, k : k + 1] == lanes)
    return hit.astype(jnp.float32).astype(jnp.bfloat16)


def restored_lanes(values):
    x = values.astype(jnp.float32)
    lane = iota(x.shape, 1)
    top = jnp.abs(x)
    for bit in (1, 2, 4, 8):
        low = pltpu.roll(top, bit, 1)
        high = pltpu.roll(top, LANES - bit, 1)
        top = jnp.maximum(top, jnp.where((lane & bit) != 0, low, high))
    scale = (jnp.maximum(top, 0.25) / 9.0).astype(jnp.bfloat16).astype(jnp.float32)
    payload = jnp.clip(x / scale, -6.0, 6.0).astype(jnp.bfloat16).astype(jnp.float32)
    return (payload * scale).astype(jnp.bfloat16)


def send_kernel(experts, chunks, ids_ref, tokens_ref, *rest):
    out_refs, pick, restored = rest[:chunks], rest[chunks], rest[chunks + 1]
    count = tokens_ref.shape[0]
    rows = out_refs[0].shape[0]
    each = rows // experts

    @pl.when(pl.program_id(0) == 0)
    def _():
        mask = named(ids_ref, experts)
        before = (iota((count, count), 0) < iota((count, count), 1)).astype(jnp.float32)
        same = (iota((count, count), 0) == iota((count, count), 1)).astype(jnp.float32)
        dims = (((0,), (0,)), ((), ()))
        rank = lax.dot_general(
            mask, before.astype(jnp.bfloat16), dims, preferred_element_type=jnp.float32
        )
        turned = lax.dot_general(
            mask, same.astype(jnp.bfloat16), dims, preferred_element_type=jnp.float32
        )
        key = jnp.where(turned > 0.5, rank, -1.0).astype(jnp.bfloat16)
        spread = (iota((rows, experts), 0) // each == iota((rows, experts), 1)).astype(jnp.float32)
        wide = jnp.dot(spread.astype(jnp.bfloat16), key, preferred_element_type=jnp.float32)
        place = (iota((rows, count), 0) % each).astype(jnp.float32)
        for j in range(chunks):
            hit = (wide == place + float(each * j)).astype(jnp.float32)
            pick[j * rows : (j + 1) * rows, :] = hit.astype(jnp.bfloat16)

    for at in range(0, tokens_ref.shape[1], LANES):
        restored[:, at : at + LANES] = restored_lanes(tokens_ref[:, at : at + LANES])
    for j in range(chunks):
        out_refs[j][...] = jnp.dot(
            pick[j * rows : (j + 1) * rows, :],
            restored[...],
            preferred_element_type=jnp.float32,
        ).astype(jnp.bfloat16)


def slots_of_tokens(tokens, expert_ids, experts, slots, chunks):
    count, width = tokens.shape
    rows = experts * slots // chunks
    wide = 1024
    return pl.pallas_call(
        functools.partial(send_kernel, experts, chunks),
        name="send_slots",
        out_shape=[jax.ShapeDtypeStruct((rows, width), jnp.bfloat16)] * chunks,
        grid=(width // wide,),
        in_specs=[
            pl.BlockSpec((count, TOP), lambda d: (0, 0)),
            pl.BlockSpec((count, wide), lambda d: (0, d)),
        ],
        out_specs=[pl.BlockSpec((rows, wide), lambda d: (0, d))] * chunks,
        scratch_shapes=[
            pltpu.VMEM((rows * chunks, count), jnp.bfloat16),
            pltpu.VMEM((count, wide), jnp.bfloat16),
        ],
        compiler_params=pltpu.CompilerParams(
            dimension_semantics=("arbitrary",), vmem_limit_bytes=VMEM_BYTES
        ),
    )(expert_ids, tokens)


def expert_kernel(
    steps, x_ref, g0, g1, u0, u1, d0, d1, out_ref, gate0, gate1, up0, up1, hid0, hid1
):
    step = pl.program_id(0)
    pairs = ((gate0, g0), (gate1, g1), (up0, u0), (up1, u1))

    @pl.when(step == 0)
    def _():
        for total, _w in pairs:
            total[...] = jnp.zeros_like(total)

    @pl.when(step < steps)
    def _():
        x = x_ref[...]
        for total, w in pairs:
            total[...] += jnp.dot(x, w[...], preferred_element_type=jnp.float32)

    @pl.when(step == steps - 1)
    def _():
        for hid, gate, up in ((hid0, gate0, up0), (hid1, gate1, up1)):
            v = gate[...]
            hid[...] = (v / (1.0 + jnp.exp(-v)) * up[...]).astype(jnp.bfloat16)

    @pl.when(step >= steps)
    def _():
        out_ref[...] = (
            jnp.dot(hid0[...], d0[...], preferred_element_type=jnp.float32)
            + jnp.dot(hid1[...], d1[...], preferred_element_type=jnp.float32)
        ).astype(jnp.bfloat16)


def expert(rows, gates, ups, downs):
    count, width = rows.shape
    half = gates[0].shape[-1]
    wide = 1024
    steps = width // wide
    first = lambda s: jnp.minimum(s, steps - 1)
    second = lambda s: jnp.maximum(s - steps, 0)
    into = pl.BlockSpec((None, wide, half), lambda s: (0, first(s), 0))
    out_of = pl.BlockSpec((None, half, wide), lambda s: (0, 0, second(s)))
    return pl.pallas_call(
        functools.partial(expert_kernel, steps),
        name="expert_rows",
        out_shape=jax.ShapeDtypeStruct((count, width), jnp.bfloat16),
        grid=(2 * steps,),
        in_specs=[pl.BlockSpec((count, wide), lambda s: (0, first(s)))] + [into] * 4 + [out_of] * 2,
        out_specs=pl.BlockSpec((count, wide), lambda s: (0, second(s))),
        scratch_shapes=[pltpu.VMEM((count, half), jnp.float32)] * 4
        + [pltpu.VMEM((count, half), jnp.bfloat16)] * 2,
        compiler_params=pltpu.CompilerParams(
            dimension_semantics=("arbitrary",), vmem_limit_bytes=VMEM_BYTES
        ),
        cost_estimate=pl.CostEstimate(
            flops=count * width * half * 12,
            transcendentals=count * half * 2,
            bytes_accessed=width * half * 12 + count * width * 4,
        ),
    )(rows, *gates, *ups, *downs)


def mix_kernel(experts, chunks, ids_ref, affinity_ref, *rest):
    in_refs, out_ref, high, low = rest[:chunks], rest[chunks], rest[chunks + 1], rest[chunks + 2]
    count = out_ref.shape[0]
    rows = in_refs[0].shape[0]
    each = rows // experts

    @pl.when(pl.program_id(0) == 0)
    def _():
        mask = named(ids_ref, experts)
        after = (iota((count, count), 1) < iota((count, count), 0)).astype(jnp.float32)
        rank = jnp.dot(after.astype(jnp.bfloat16), mask, preferred_element_type=jnp.float32)
        key = jnp.where(mask.astype(jnp.float32) > 0.5, rank, -1.0).astype(jnp.bfloat16)
        affinity = affinity_ref[...]
        total = affinity[:, 0:1]
        for k in range(1, TOP):
            total = total + affinity[:, k : k + 1]
        lanes = iota((count, experts), 1)
        weight = jnp.zeros((count, experts), jnp.float32)
        for k in range(TOP):
            weight = jnp.where(
                ids_ref[:, k : k + 1] == lanes, affinity[:, k : k + 1] / total, weight
            )
        upper = weight.astype(jnp.bfloat16)
        lower = (weight - upper.astype(jnp.float32)).astype(jnp.bfloat16)
        spread = (iota((experts, rows), 1) // each == iota((experts, rows), 0)).astype(jnp.float32)
        spread = spread.astype(jnp.bfloat16)
        wide = jnp.dot(key, spread, preferred_element_type=jnp.float32)
        upper = jnp.dot(upper, spread, preferred_element_type=jnp.float32)
        lower = jnp.dot(lower, spread, preferred_element_type=jnp.float32)
        place = (iota((count, rows), 1) % each).astype(jnp.float32)
        for j in range(chunks):
            hit = wide == place + float(each * j)
            high[j] = jnp.where(hit, upper, 0.0).astype(jnp.bfloat16)
            low[j] = jnp.where(hit, lower, 0.0).astype(jnp.bfloat16)

    total = None
    for j in range(chunks):
        values = in_refs[j][...]
        part = jnp.dot(high[j], values, preferred_element_type=jnp.float32) + jnp.dot(
            low[j], values, preferred_element_type=jnp.float32
        )
        total = part if total is None else total + part
    out_ref[...] = total.astype(jnp.bfloat16)


def mix(expert_ids, affinity, parts, experts):
    count = expert_ids.shape[0]
    rows, width = parts[0].shape
    chunks = len(parts)
    wide = 1024
    return pl.pallas_call(
        functools.partial(mix_kernel, experts, chunks),
        name="mix_slots",
        out_shape=jax.ShapeDtypeStruct((count, width), jnp.bfloat16),
        grid=(width // wide,),
        in_specs=[pl.BlockSpec((count, TOP), lambda d: (0, 0))] * 2
        + [pl.BlockSpec((rows, wide), lambda d: (0, d))] * chunks,
        out_specs=pl.BlockSpec((count, wide), lambda d: (0, d)),
        scratch_shapes=[pltpu.VMEM((chunks, count, rows), jnp.bfloat16)] * 2,
        compiler_params=pltpu.CompilerParams(
            dimension_semantics=("arbitrary",), vmem_limit_bytes=VMEM_BYTES
        ),
    )(expert_ids, affinity, *parts)


def exchange(rows, devices):
    count, width = rows.shape
    split = rows.reshape(devices, count // devices, width)
    return lax.all_to_all(split, "ep", split_axis=0, concat_axis=0, tiled=True).reshape(
        count, width
    )


CHUNKS = 2


def on_device(tokens, expert_ids, affinity, w_gate, w_up, w_down):
    devices = lax.axis_size("ep")
    experts = devices // 2
    slots = 2 * tokens.shape[0] * TOP // experts
    pairs = [(s, s ^ 1) for s in range(devices)]
    gates, ups, downs = [(w, lax.ppermute(w, "ep", pairs)) for w in (w_gate, w_up, w_down)]
    sent = slots_of_tokens(tokens, expert_ids, experts, slots, CHUNKS)
    parts = []
    for rows in sent:
        computed = expert(exchange(rows, devices), gates, ups, downs)
        parts.append(exchange(computed, devices))
    return mix(expert_ids, affinity, parts, experts)


def solution(mesh):
    rows = P(("dp", "ep"), None)
    weights = P("ep", None, None)
    return jax.shard_map(
        on_device,
        mesh=mesh,
        in_specs=(rows, rows, rows, weights, weights, weights),
        out_specs=rows,
        check_vma=False,
    )
```

time: 523 us -> 236 us (0.45); the launches traced: 513 us -> 235 us
  local copies, waits for them, and re-layouts: 137 us -> 2.14 us
  other arithmetic: 79.2 us -> 0 us
  Pallas kernels: 0 us -> 71.9 us
  starting transfers between devices: 74.2 us -> 15.2 us
  blocking collectives: 98.8 us -> 54.1 us
  waiting for transfers between devices: 115 us -> 91.9 us
  matrix products: 8.03 us -> 0 us
    pallas_call x0 -> x4, Pallas kernels: none -> 71.9 us  [the longest x2 50.3 us: expert(): pl.pallas_call(functools.partial(expert_kernel, steps), name='expert_rows...]
    all_to_all x1 -> x3, starting transfers between devices: 73.6 us -> 14.6 us  [exchange(): lax.all_to_all(split, 'ep', split_axis=0, concat_axis=0, tiled=True)]
    gather x5 -> x0, local copies, waits for them, and re-layouts: 56.9 us -> none  [the longest x1 31.8 us: filled_rows(): packed = payload[ordering]]
    all_to_all x1, blocking collectives: 98.8 us -> 54.1 us  [exchange(): lax.all_to_all(split, 'ep', split_axis=0, concat_axis=0, tiled=True)]
    scatter x3 -> x0, local copies, waits for them, and re-layouts: 32.1 us -> none  [the longest x1 29.3 us: filled_rows(): jnp.zeros((count_rows, row_width), jnp.bfloat16).at[ordering].set(result)]
    ppermute x3, waiting for transfers between devices: 22.9 us -> 0.01 us  [on_device(): lax.ppermute(w, 'ep', pairs)]
    select_n x8 -> x0, other arithmetic: 22.7 us -> none  [the longest x1 8.87 us: on_device(): mate_part = jnp.where(upper_half, lower_part, higher_part)]
    convert_element_type x6 -> x0, other arithmetic: 17 us -> none  [the longest x1 9.63 us: on_device(): (own_part.astype(jnp.float32) + received.astype(jnp.float32)).astype(jnp....]
  transfers between devices with their start and end apart: 4 -> 6, of which waited for: 3 -> 3; matrix products, arithmetic and copies ran while one was open for 2% -> 1% of each run, Pallas kernels for 0% -> 27%
where the time goes in v1:
time: 236 us; the launch traced here: 235 us
  waiting for transfers between devices  91.9 us (39%)
  Pallas kernels  71.9 us (30%)
  blocking collectives  54.1 us (23%)
  starting transfers between devices  15.2 us (6%)
    all_to_all x3, waiting for transfers between devices, exchange(): lax.all_to_all(split, 'ep', split_axis=0, concat_axis=0, tiled=True)  91.9 us
    all_to_all x1, blocking collectives, exchange(): lax.all_to_all(split, 'ep', split_axis=0, concat_axis=0, tiled=True)  54.1 us
    pallas_call x2, Pallas kernels, expert(): pl.pallas_call(functools.partial(expert_kernel, steps), name='expert_rows...  50.3 us
    all_to_all x3, starting transfers between devices, exchange(): lax.all_to_all(split, 'ep', split_axis=0, concat_axis=0, tiled=True)  14.6 us
    pallas_call x1, Pallas kernels, slots_of_tokens(): pl.pallas_call(functools.partial(send_kernel, experts, chunks), name='sen...  13.4 us
    pallas_call x1, Pallas kernels, mix(): pl.pallas_call(functools.partial(mix_kernel, experts, chunks), name='mix_...  8.16 us
  transfers between devices with their start and end apart: 6, of which 3 were waited for; matrix products, arithmetic and copies ran while one was open for 1% of the time, Pallas kernels for 27%

profile of v1, /device:TPU:0, one launch (start us, length us, event | category | flops | bytes accessed | tf_op | source)
XLA Modules:
  0.0 235.3 jit_solution(16450166185828799421)
XLA Ops:
  0.0 0.0 collective-permute-start
  0.0 0.5 collective-permute-start.1
  0.5 0.0 collective-permute-start.2
  0.5 1.4 copy.8.ids_ref
  1.9 13.4 %send_slots.1 = (bf16[256,7168]{1,0:T(8,128)(2,1)}, bf16[256,7168]{1,0:T(8,128)(2,1)}) custom-call(s32[128,2]{1,0:T(8,128)} %copy.8.ids_ref, bf16[128,7168]{1,0:T(8,128)(2,1)} %tokens_ref.1), custom_call_target="tpu_custom_call" | custom-call | tf_op jit(solution)/shard_map/send_slots/pallas_call | solution.py:81
  15.3 54.1 %all_to_all.20 = bf16[32,8,7168]{2,1,0:T(8,128)(2,1)} all-to-all(bf16[32,8,7168]{2,1,0:T(8,128)(2,1)} %bitcast.12), channel_id=1, replica_groups=mesh['ep'=32,'dp'=4] {'ep'}, dimensions={0} | all-to-all | bytes 7340032 | tf_op jit(solution)/shard_map/all_to_all | solution.py:229
  69.4 4.8 %all-to-all-start.2 = ((bf16[32,8,7168]{2,1,0:T(8,128)(2,1)}), bf16[32,8,7168]{2,1,0:T(8,128)(2,1)}, u32[]{:S(2)}, u32[]{:S(2)}) async-start(bf16[32,8,7168]{2,1,0:T(8,128)(2,1)} %bitcast.11), calls=%async_computation.2 | async-start | bytes 7340032 | tf_op jit(solution)/shard_map/all_to_all | solution.py:229
  74.3 0.0 collective-permute-done.g1
  74.3 0.0 collective-permute-done.1.u1
  74.3 0.0 collective-permute-done.2.d1
  74.3 25.2 %expert_rows.2 = bf16[256,7168]{1,0:T(8,128)(2,1)} custom-call(bf16[256,7168]{1,0:T(8,128)(2,1)} %bitcast.8, bf16[1,7168,512]{2,1,0:T(8,128)(2,1)} %g0.3, bf16[1,7168,512]{2,1,0:T(8,128)(2,1)} %collective-permute-done.g1, bf16[1,7168,512]{2,1,0:T(8,128)(2,1)} %u0.3, bf16[1,7168,512]{2,1,0:T(8,128)(2,1)} %collective-permute-done.1.u1, ...), custom_call_target="tpu_custom_call" | custom-call | flops 11274289152 | bytes 51380224 | tf_op jit(solution)/shard_map/expert_rows/pallas_call | solution.py:141
  99.5 22.5 %all-to-all-done.2 = bf16[32,8,7168]{2,1,0:T(8,128)(2,1)} async-done(((bf16[32,8,7168]{2,1,0:T(8,128)(2,1)}), bf16[32,8,7168]{2,1,0:T(8,128)(2,1)}, u32[]{:S(2)}, u32[]{:S(2)}) %all-to-all-start.2) | async-done | bytes 3670048 | tf_op jit(solution)/shard_map/all_to_all | solution.py:229
  122.0 4.8 %all-to-all-start.1 = ((bf16[32,8,7168]{2,1,0:T(8,128)(2,1)}), bf16[32,8,7168]{2,1,0:T(8,128)(2,1)}, u32[]{:S(2)}, u32[]{:S(2)}) async-start(bf16[32,8,7168]{2,1,0:T(8,128)(2,1)} %bitcast.9), calls=%async_computation.1 | async-start | bytes 7340032 | tf_op jit(solution)/shard_map/all_to_all | solution.py:229
  126.8 25.2 %expert_rows.3 = bf16[256,7168]{1,0:T(8,128)(2,1)} custom-call(bf16[256,7168]{1,0:T(8,128)(2,1)} %bitcast.5.x_ref, bf16[1,7168,512]{2,1,0:T(8,128)(2,1)} %g0.3, bf16[1,7168,512]{2,1,0:T(8,128)(2,1)} %collective-permute-done.g1, bf16[1,7168,512]{2,1,0:T(8,128)(2,1)} %u0.3, bf16[1,7168,512]{2,1,0:T(8,128)(2,1)} %collective-permute-done.1.u1, ...), custom_call_target="tpu_custom_call" | custom-call | flops 11274289152 | bytes 51380224 | tf_op jit(solution)/shard_map/expert_rows/pallas_call | solution.py:141
  152.0 22.5 %all-to-all-done.1 = bf16[32,8,7168]{2,1,0:T(8,128)(2,1)} async-done(((bf16[32,8,7168]{2,1,0:T(8,128)(2,1)}), bf16[32,8,7168]{2,1,0:T(8,128)(2,1)}, u32[]{:S(2)}, u32[]{:S(2)}) %all-to-all-start.1) | async-done | bytes 3670048 | tf_op jit(solution)/shard_map/all_to_all | solution.py:229
  174.5 0.0 copy-start
  174.5 5.0 %all-to-all-start.3 = ((bf16[32,8,7168]{2,1,0:T(8,128)(2,1)}), bf16[32,8,7168]{2,1,0:T(8,128)(2,1)}, u32[]{:S(2)}, u32[]{:S(2)}) async-start(bf16[32,8,7168]{2,1,0:T(8,128)(2,1)} %bitcast.10), calls=%async_computation.3 | async-start | bytes 7340032 | tf_op jit(solution)/shard_map/all_to_all | solution.py:229
  179.5 0.0 copy-done
  179.5 0.7 copy.9.affinity_ref
  180.2 46.9 %all-to-all-done.3 = bf16[32,8,7168]{2,1,0:T(8,128)(2,1)} async-done(((bf16[32,8,7168]{2,1,0:T(8,128)(2,1)}), bf16[32,8,7168]{2,1,0:T(8,128)(2,1)}, u32[]{:S(2)}, u32[]{:S(2)}) %all-to-all-start.3) | async-done | bytes 3670048 | tf_op jit(solution)/shard_map/all_to_all | solution.py:229
  227.1 8.2 %mix_slots.1 = bf16[128,7168]{1,0:T(8,128)(2,1)} custom-call(s32[128,2]{1,0:T(8,128)} %copy.8.ids_ref, f32[128,2]{1,0:T(8,128)} %copy.9.affinity_ref, bf16[256,7168]{1,0:T(8,128)(2,1)} %bitcast.3.rest_0_, bf16[256,7168]{1,0:T(8,128)(2,1)} %bitcast.7.rest_1_), custom_call_target="tpu_custom_call" | custom-call | tf_op jit(solution)/shard_map/mix_slots/pallas_call | solution.py:211
Async XLA Ops:
  0.0 74.3 %collective-permute-start = (bf16[1,7168,512]{2,1,0:T(8,128)(2,1)}, bf16[1,7168,512]{2,1,0:T(8,128)(2,1)}, u32[]{:S(2)}, u32[]{:S(2)}) collective-permute-start(bf16[1,7168,512]{2,1,0:T(8,128)(2,1)} %g0.3), channel_id=1, source_target_pairs={{0,4},{4,0},{8,12},{12,8},{16,20},{20,16},{24,28},{28,24},{32,36},... | collective-permute-start | bytes 22020104 | tf_op jit(solution)/shard_map/ppermute | solution.py:242
  0.0 74.3 %collective-permute-start.1 = (bf16[1,7168,512]{2,1,0:T(8,128)(2,1)}, bf16[1,7168,512]{2,1,0:T(8,128)(2,1)}, u32[]{:S(2)}, u32[]{:S(2)}) collective-permute-start(bf16[1,7168,512]{2,1,0:T(8,128)(2,1)} %u0.3), channel_id=1, source_target_pairs={{0,4},{4,0},{8,12},{12,8},{16,20},{20,16},{24,28},{28,24},{32,36},... | collective-permute-start | bytes 22020104 | tf_op jit(solution)/shard_map/ppermute | solution.py:242
  0.5 73.8 %collective-permute-start.2 = (bf16[1,512,7168]{2,1,0:T(8,128)(2,1)}, bf16[1,512,7168]{2,1,0:T(8,128)(2,1)}, u32[]{:S(2)}, u32[]{:S(2)}) collective-permute-start(bf16[1,512,7168]{2,1,0:T(8,128)(2,1)} %d0.3), channel_id=1, source_target_pairs={{0,4},{4,0},{8,12},{12,8},{16,20},{20,16},{24,28},{28,24},{32,36},... | collective-permute-start | bytes 22020104 | tf_op jit(solution)/shard_map/ppermute | solution.py:242
  69.4 52.5 %all-to-all-start.2 = ((bf16[32,8,7168]{2,1,0:T(8,128)(2,1)}), bf16[32,8,7168]{2,1,0:T(8,128)(2,1)}, u32[]{:S(2)}, u32[]{:S(2)}) async-start(bf16[32,8,7168]{2,1,0:T(8,128)(2,1)} %bitcast.11), calls=%async_computation.2 | async-start | bytes 7340032 | tf_op jit(solution)/shard_map/all_to_all | solution.py:229
  122.0 52.5 %all-to-all-start.1 = ((bf16[32,8,7168]{2,1,0:T(8,128)(2,1)}), bf16[32,8,7168]{2,1,0:T(8,128)(2,1)}, u32[]{:S(2)}, u32[]{:S(2)}) async-start(bf16[32,8,7168]{2,1,0:T(8,128)(2,1)} %bitcast.9), calls=%async_computation.1 | async-start | bytes 7340032 | tf_op jit(solution)/shard_map/all_to_all | solution.py:229
  174.5 5.0 %copy-start = (f32[128,2]{0,1:T(2,128)S(1)}, f32[128,2]{0,1:T(2,128)}, u32[]{:S(2)}) copy-start(f32[128,2]{0,1:T(2,128)} %param.8) | copy-start | bytes 3076
  174.5 52.6 %all-to-all-start.3 = ((bf16[32,8,7168]{2,1,0:T(8,128)(2,1)}), bf16[32,8,7168]{2,1,0:T(8,128)(2,1)}, u32[]{:S(2)}, u32[]{:S(2)}) async-start(bf16[32,8,7168]{2,1,0:T(8,128)(2,1)} %bitcast.10), calls=%async_computation.3 | async-start | bytes 7340032 | tf_op jit(solution)/shard_map/all_to_all | solution.py:229

commit v2 on v1

v2 whole, which is shorter than its diff:
```python
import functools
import jax
import jax.numpy as jnp
from jax import lax
from jax.experimental import pallas as pl
from jax.experimental.pallas import tpu as pltpu
from jax.sharding import PartitionSpec as P

TOP = 2
BLOCK = 16
LANES = 128
VMEM_BYTES = 56 * 1024 * 1024


def iota(shape, dim):
    return lax.broadcasted_iota(jnp.int32, shape, dim)


def halves(value):
    upper = value.astype(jnp.bfloat16)
    return upper, (value - upper.astype(jnp.float32)).astype(jnp.bfloat16)


def ones_where(hit):
    return hit.astype(jnp.float32).astype(jnp.bfloat16)


def times(a, b):
    return jnp.dot(a, b, preferred_element_type=jnp.float32)


def slot_keys(turned_ids_ref, experts):
    count = turned_ids_ref.shape[1]
    row = iota((experts, count), 0)
    hit = turned_ids_ref[0:1, :] == row
    for k in range(1, TOP):
        hit = hit | (turned_ids_ref[k : k + 1, :] == row)
    earlier = ones_where(iota((count, count), 0) < iota((count, count), 1))
    rank = times(ones_where(hit), earlier)
    return jnp.where(hit, rank, -1.0).astype(jnp.bfloat16)


def restored_rows(tokens, gather, spread, spread3):
    x = tokens.astype(jnp.float32)
    width = x.shape[1]
    tops = []
    for at in range(0, width, LANES):
        top = jnp.abs(x[:, at : at + LANES])
        for step in (1, 2, 4, 8):
            top = jnp.maximum(top, pltpu.roll(top, LANES - step, 1))
        tops.append(top.astype(jnp.bfloat16))
    largest = times(jnp.concatenate(tops, axis=1), gather)
    scale = (jnp.maximum(largest, 0.25) / 9.0).astype(jnp.bfloat16)
    inverse = 1.0 / scale.astype(jnp.float32)
    first, rest = halves(inverse)
    second, third = halves(inverse - first.astype(jnp.float32))
    inverse = times(jnp.concatenate([first, second, third], axis=1), spread3)
    scale = times(scale, spread)
    payload = jnp.clip(x * inverse, -6.0, 6.0).astype(jnp.bfloat16).astype(jnp.float32)
    return (payload * scale).astype(jnp.bfloat16)


def send_kernel(experts, chunks, ids_ref, tokens_ref, *rest):
    out_refs, (pick, gather, spread, spread3) = rest[:chunks], rest[chunks:]
    count, width = tokens_ref.shape
    rows = out_refs[0].shape[0]
    each = rows // experts
    blocks = width // BLOCK

    @pl.when(pl.program_id(0) == 0)
    def _():
        key = slot_keys(ids_ref, experts)
        wide = times(ones_where(iota((rows, experts), 0) // each == iota((rows, experts), 1)), key)
        place = (iota((rows, count), 0) % each).astype(jnp.float32)
        for j in range(chunks):
            pick[j * rows : (j + 1) * rows, :] = ones_where(wide == place + float(each * j))
        gather[...] = ones_where(iota((width, blocks), 0) == BLOCK * iota((width, blocks), 1))
        spread[...] = ones_where(iota((blocks, width), 1) // BLOCK == iota((blocks, width), 0))
        for j in range(3):
            spread3[j * blocks : (j + 1) * blocks, :] = spread[...]

    restored = restored_rows(tokens_ref[...], gather[...], spread[...], spread3[...])
    for j in range(chunks):
        out_refs[j][...] = times(pick[j * rows : (j + 1) * rows, :], restored).astype(jnp.bfloat16)


def slots_of_tokens(tokens, turned_ids, experts, slots, chunks):
    count, width = tokens.shape
    rows = experts * slots // chunks
    wide = 1024
    blocks = wide // BLOCK
    return pl.pallas_call(
        functools.partial(send_kernel, experts, chunks),
        name="send_slots",
        out_shape=[jax.ShapeDtypeStruct((rows, width), jnp.bfloat16)] * chunks,
        grid=(width // wide,),
        in_specs=[
            pl.BlockSpec((TOP, count), lambda d: (0, 0)),
            pl.BlockSpec((count, wide), lambda d: (0, d)),
        ],
        out_specs=[pl.BlockSpec((rows, wide), lambda d: (0, d))] * chunks,
        scratch_shapes=[
            pltpu.VMEM((rows * chunks, count), jnp.bfloat16),
            pltpu.VMEM((wide, blocks), jnp.bfloat16),
            pltpu.VMEM((blocks, wide), jnp.bfloat16),
            pltpu.VMEM((3 * blocks, wide), jnp.bfloat16),
        ],
        compiler_params=pltpu.CompilerParams(
            dimension_semantics=("arbitrary",), vmem_limit_bytes=VMEM_BYTES
        ),
    )(turned_ids, tokens)


def expert_kernel(
    steps, x_ref, g0, g1, u0, u1, d0, d1, out_ref, gate0, gate1, up0, up1, hid0, hid1
):
    step = pl.program_id(0)
    pairs = ((gate0, g0), (gate1, g1), (up0, u0), (up1, u1))

    @pl.when(step == 0)
    def _():
        for total, _w in pairs:
            total[...] = jnp.zeros_like(total)

    @pl.when(step < steps)
    def _():
        x = x_ref[...]
        for total, w in pairs:
            total[...] += jnp.dot(x, w[...], preferred_element_type=jnp.float32)

    @pl.when(step == steps - 1)
    def _():
        for hid, gate, up in ((hid0, gate0, up0), (hid1, gate1, up1)):
            v = gate[...]
            hid[...] = (v / (1.0 + jnp.exp(-v)) * up[...]).astype(jnp.bfloat16)

    @pl.when(step >= steps)
    def _():
        out_ref[...] = (
            jnp.dot(hid0[...], d0[...], preferred_element_type=jnp.float32)
            + jnp.dot(hid1[...], d1[...], preferred_element_type=jnp.float32)
        ).astype(jnp.bfloat16)


def expert(rows, gates, ups, downs):
    count, width = rows.shape
    half = gates[0].shape[-1]
    wide = 1024
    steps = width // wide
    first = lambda s: jnp.minimum(s, steps - 1)
    second = lambda s: jnp.maximum(s - steps, 0)
    into = pl.BlockSpec((None, wide, half), lambda s: (0, first(s), 0))
    out_of = pl.BlockSpec((None, half, wide), lambda s: (0, 0, second(s)))
    return pl.pallas_call(
        functools.partial(expert_kernel, steps),
        name="expert_rows",
        out_shape=jax.ShapeDtypeStruct((count, width), jnp.bfloat16),
        grid=(2 * steps,),
        in_specs=[pl.BlockSpec((count, wide), lambda s: (0, first(s)))] + [into] * 4 + [out_of] * 2,
        out_specs=pl.BlockSpec((count, wide), lambda s: (0, second(s))),
        scratch_shapes=[pltpu.VMEM((count, half), jnp.float32)] * 4
        + [pltpu.VMEM((count, half), jnp.bfloat16)] * 2,
        compiler_params=pltpu.CompilerParams(
            dimension_semantics=("arbitrary",), vmem_limit_bytes=VMEM_BYTES
        ),
        cost_estimate=pl.CostEstimate(
            flops=count * width * half * 12,
            transcendentals=count * half * 2,
            bytes_accessed=width * half * 12 + count * width * 4,
        ),
    )(rows, *gates, *ups, *downs)


def table_kernel(experts, chunks, ids_ref, affinity_ref, out_ref):
    count = ids_ref.shape[1]
    rows = out_ref.shape[2]
    each = rows // experts
    key = slot_keys(ids_ref, experts)
    total = affinity_ref[0:1, :]
    for k in range(1, TOP):
        total = total + affinity_ref[k : k + 1, :]
    row = iota((experts, count), 0)
    weight = jnp.zeros((experts, count), jnp.float32)
    for k in range(TOP):
        share = affinity_ref[k : k + 1, :] / total
        weight = jnp.where(ids_ref[k : k + 1, :] == row, share, weight)
    same = ones_where(iota((count, count), 0) == iota((count, count), 1))
    spread = ones_where(iota((experts, rows), 1) // each == iota((experts, rows), 0))

    def by_token(value):
        turned = lax.dot_general(
            same, value, (((1,), (1,)), ((), ())), preferred_element_type=jnp.float32
        )
        return times(turned.astype(jnp.bfloat16), spread)

    wide = by_token(key)
    upper, lower = [by_token(part) for part in halves(weight)]
    place = (iota((count, rows), 1) % each).astype(jnp.float32)
    for j in range(chunks):
        hit = wide == place + float(each * j)
        out_ref[j, 0:count, :] = jnp.where(hit, upper, 0.0).astype(jnp.bfloat16)
        out_ref[j, count : 2 * count, :] = jnp.where(hit, lower, 0.0).astype(jnp.bfloat16)


def weights_of_slots(turned_ids, turned_affinity, experts, slots, chunks):
    count = turned_ids.shape[1]
    rows = experts * slots // chunks
    return pl.pallas_call(
        functools.partial(table_kernel, experts, chunks),
        name="slot_weights",
        out_shape=jax.ShapeDtypeStruct((chunks, 2 * count, rows), jnp.bfloat16),
    )(turned_ids, turned_affinity)


def mix_kernel(chunks, table_ref, *rest):
    in_refs, out_ref = rest[:chunks], rest[chunks]
    count = out_ref.shape[0]
    total = times(table_ref[0], in_refs[0][...])
    for j in range(1, chunks):
        total = total + times(table_ref[j], in_refs[j][...])
    out_ref[...] = (total[:count] + total[count:]).astype(jnp.bfloat16)


def mix(table, parts):
    chunks, count, rows = table.shape
    count //= 2
    width = parts[0].shape[1]
    wide = 1024
    return pl.pallas_call(
        functools.partial(mix_kernel, chunks),
        name="mix_slots",
        out_shape=jax.ShapeDtypeStruct((count, width), jnp.bfloat16),
        grid=(width // wide,),
        in_specs=[pl.BlockSpec(table.shape, lambda d: (0, 0, 0))]
        + [pl.BlockSpec((rows, wide), lambda d: (0, d))] * chunks,
        out_specs=pl.BlockSpec((count, wide), lambda d: (0, d)),
        compiler_params=pltpu.CompilerParams(
            dimension_semantics=("arbitrary",), vmem_limit_bytes=VMEM_BYTES
        ),
    )(table, *parts)


def exchange(rows, devices):
    count, width = rows.shape
    split = rows.reshape(devices, count // devices, width)
    return lax.all_to_all(split, "ep", split_axis=0, concat_axis=0, tiled=True).reshape(
        count, width
    )


CHUNKS = 2


def on_device(tokens, expert_ids, affinity, w_gate, w_up, w_down):
    devices = lax.axis_size("ep")
    experts = devices // 2
    slots = 2 * tokens.shape[0] * TOP // experts
    pairs = [(s, s ^ 1) for s in range(devices)]
    gates, ups, downs = [(w, lax.ppermute(w, "ep", pairs)) for w in (w_gate, w_up, w_down)]
    turned_ids = expert_ids.T
    table = weights_of_slots(turned_ids, affinity.T, experts, slots, CHUNKS)
    sent = slots_of_tokens(tokens, turned_ids, experts, slots, CHUNKS)
    parts = []
    for rows in sent:
        computed = expert(exchange(rows, devices), gates, ups, downs)
        parts.append(exchange(computed, devices))
    return mix(table, parts)


def solution(mesh):
    rows = P(("dp", "ep"), None)
    weights = P("ep", None, None)
    return jax.shard_map(
        on_device,
        mesh=mesh,
        in_specs=(rows, rows, rows, weights, weights, weights),
        out_specs=rows,
        check_vma=False,
    )
```

time: 236 us -> 232 us (0.983)
    pallas_call x1, Pallas kernels: 13.4 us -> 10.8 us  [slots_of_tokens(): pl.pallas_call(functools.partial(send_kernel, experts, chunks), name='sen...]
    pallas_call x1 -> x2, Pallas kernels: 8.16 us -> 9.73 us  [the longest x1 7.77 us: mix(): pl.pallas_call(functools.partial(mix_kernel, chunks), name='mix_slots', o...]
  transfers between devices with their start and end apart: 6 -> 6, of which waited for: 3 -> 3; matrix products, arithmetic and copies ran while one was open for 1% -> 0% of each run, Pallas kernels for 27% -> 27%
where the time goes in v2:
time: 232 us; the launch traced here: 231 us
  waiting for transfers between devices  90.7 us (39%)
  Pallas kernels  70.9 us (31%)
  blocking collectives  54.1 us (23%)
  starting transfers between devices  15 us (6%)
    all_to_all x3, waiting for transfers between devices, exchange(): lax.all_to_all(split, 'ep', split_axis=0, concat_axis=0, tiled=True)  90.7 us
    all_to_all x1, blocking collectives, exchange(): lax.all_to_all(split, 'ep', split_axis=0, concat_axis=0, tiled=True)  54.1 us
    pallas_call x2, Pallas kernels, expert(): pl.pallas_call(functools.partial(expert_kernel, steps), name='expert_rows...  50.4 us
    all_to_all x3, starting transfers between devices, exchange(): lax.all_to_all(split, 'ep', split_axis=0, concat_axis=0, tiled=True)  14.5 us
    pallas_call x1, Pallas kernels, slots_of_tokens(): pl.pallas_call(functools.partial(send_kernel, experts, chunks), name='sen...  10.8 us
    pallas_call x1, Pallas kernels, mix(): pl.pallas_call(functools.partial(mix_kernel, chunks), name='mix_slots', o...  7.77 us
  transfers between devices with their start and end apart: 6, of which 3 were waited for; matrix products, arithmetic and copies ran while one was open for 0% of the time, Pallas kernels for 27%

profile of v2, /device:TPU:0, one launch (start us, length us, event | category | flops | bytes accessed | tf_op | source)
XLA Modules:
  0.0 230.8 jit_solution(10530466746418616167)
XLA Ops:
  0.0 0.0 collective-permute-start
  0.0 0.5 collective-permute-start.1
  0.5 0.0 collective-permute-start.2
  0.5 10.8 %send_slots.1 = (bf16[256,7168]{1,0:T(8,128)(2,1)}, bf16[256,7168]{1,0:T(8,128)(2,1)}) custom-call(s32[2,128]{1,0:T(2,128)} %bitcast.15, bf16[128,7168]{1,0:T(8,128)(2,1)} %tokens_ref.1), custom_call_target="tpu_custom_call" | custom-call | tf_op jit(solution)/shard_map/send_slots/pallas_call | solution.py:92
  11.3 54.1 %all_to_all.20 = bf16[32,8,7168]{2,1,0:T(8,128)(2,1)} all-to-all(bf16[32,8,7168]{2,1,0:T(8,128)(2,1)} %bitcast.14), channel_id=1, replica_groups=mesh['ep'=32,'dp'=4] {'ep'}, dimensions={0} | all-to-all | bytes 7340032 | tf_op jit(solution)/shard_map/all_to_all | solution.py:246
  65.4 4.8 %all-to-all-start.2 = ((bf16[32,8,7168]{2,1,0:T(8,128)(2,1)}), bf16[32,8,7168]{2,1,0:T(8,128)(2,1)}, u32[]{:S(2)}, u32[]{:S(2)}) async-start(bf16[32,8,7168]{2,1,0:T(8,128)(2,1)} %bitcast.13), calls=%async_computation.2 | async-start | bytes 7340032 | tf_op jit(solution)/shard_map/all_to_all | solution.py:246
  70.3 0.0 collective-permute-done.g1
  70.3 0.0 collective-permute-done.1.u1
  70.3 0.0 collective-permute-done.2.d1
  70.3 25.2 %expert_rows.2 = bf16[256,7168]{1,0:T(8,128)(2,1)} custom-call(bf16[256,7168]{1,0:T(8,128)(2,1)} %bitcast.10, bf16[1,7168,512]{2,1,0:T(8,128)(2,1)} %g0.3, bf16[1,7168,512]{2,1,0:T(8,128)(2,1)} %collective-permute-done.g1, bf16[1,7168,512]{2,1,0:T(8,128)(2,1)} %u0.3, bf16[1,7168,512]{2,1,0:T(8,128)(2,1)} %collective-permute-done.1.u1, ...), custom_call_target="tpu_custom_call" | custom-call | flops 11274289152 | bytes 51380224 | tf_op jit(solution)/shard_map/expert_rows/pallas_call | solution.py:154
  95.5 22.5 %all-to-all-done.2 = bf16[32,8,7168]{2,1,0:T(8,128)(2,1)} async-done(((bf16[32,8,7168]{2,1,0:T(8,128)(2,1)}), bf16[32,8,7168]{2,1,0:T(8,128)(2,1)}, u32[]{:S(2)}, u32[]{:S(2)}) %all-to-all-start.2) | async-done | bytes 3670048 | tf_op jit(solution)/shard_map/all_to_all | solution.py:246
  117.9 4.8 %all-to-all-start.1 = ((bf16[32,8,7168]{2,1,0:T(8,128)(2,1)}), bf16[32,8,7168]{2,1,0:T(8,128)(2,1)}, u32[]{:S(2)}, u32[]{:S(2)}) async-start(bf16[32,8,7168]{2,1,0:T(8,128)(2,1)} %bitcast.11), calls=%async_computation.1 | async-start | bytes 7340032 | tf_op jit(solution)/shard_map/all_to_all | solution.py:246
  122.8 25.2 %expert_rows.3 = bf16[256,7168]{1,0:T(8,128)(2,1)} custom-call(bf16[256,7168]{1,0:T(8,128)(2,1)} %bitcast.7.x_ref, bf16[1,7168,512]{2,1,0:T(8,128)(2,1)} %g0.3, bf16[1,7168,512]{2,1,0:T(8,128)(2,1)} %collective-permute-done.g1, bf16[1,7168,512]{2,1,0:T(8,128)(2,1)} %u0.3, bf16[1,7168,512]{2,1,0:T(8,128)(2,1)} %collective-permute-done.1.u1, ...), custom_call_target="tpu_custom_call" | custom-call | flops 11274289152 | bytes 51380224 | tf_op jit(solution)/shard_map/expert_rows/pallas_call | solution.py:154
  148.0 22.5 %all-to-all-done.1 = bf16[32,8,7168]{2,1,0:T(8,128)(2,1)} async-done(((bf16[32,8,7168]{2,1,0:T(8,128)(2,1)}), bf16[32,8,7168]{2,1,0:T(8,128)(2,1)}, u32[]{:S(2)}, u32[]{:S(2)}) %all-to-all-start.1) | async-done | bytes 3670048 | tf_op jit(solution)/shard_map/all_to_all | solution.py:246
  170.5 4.8 %all-to-all-start.3 = ((bf16[32,8,7168]{2,1,0:T(8,128)(2,1)}), bf16[32,8,7168]{2,1,0:T(8,128)(2,1)}, u32[]{:S(2)}, u32[]{:S(2)}) async-start(bf16[32,8,7168]{2,1,0:T(8,128)(2,1)} %bitcast.12), calls=%async_computation.3 | async-start | bytes 7340032 | tf_op jit(solution)/shard_map/all_to_all | solution.py:246
  175.3 2.0 slot_weights.1.table_ref
  177.3 45.7 %all-to-all-done.3 = bf16[32,8,7168]{2,1,0:T(8,128)(2,1)} async-done(((bf16[32,8,7168]{2,1,0:T(8,128)(2,1)}), bf16[32,8,7168]{2,1,0:T(8,128)(2,1)}, u32[]{:S(2)}, u32[]{:S(2)}) %all-to-all-start.3) | async-done | bytes 3670048 | tf_op jit(solution)/shard_map/all_to_all | solution.py:246
  223.0 7.8 %mix_slots.1 = bf16[128,7168]{1,0:T(8,128)(2,1)} custom-call(bf16[2,256,256]{2,1,0:T(8,128)(2,1)} %slot_weights.1.table_ref, bf16[256,7168]{1,0:T(8,128)(2,1)} %bitcast.5.rest_0_, bf16[256,7168]{1,0:T(8,128)(2,1)} %bitcast.9.rest_1_), custom_call_target="tpu_custom_call" | custom-call | tf_op jit(solution)/shard_map/mix_slots/pallas_call | solution.py:229
Async XLA Ops:
  0.0 70.3 %collective-permute-start = (bf16[1,7168,512]{2,1,0:T(8,128)(2,1)}, bf16[1,7168,512]{2,1,0:T(8,128)(2,1)}, u32[]{:S(2)}, u32[]{:S(2)}) collective-permute-start(bf16[1,7168,512]{2,1,0:T(8,128)(2,1)} %g0.3), channel_id=1, source_target_pairs={{0,4},{4,0},{8,12},{12,8},{16,20},{20,16},{24,28},{28,24},{32,36},... | collective-permute-start | bytes 22020104 | tf_op jit(solution)/shard_map/ppermute | solution.py:259
  0.0 70.3 %collective-permute-start.1 = (bf16[1,7168,512]{2,1,0:T(8,128)(2,1)}, bf16[1,7168,512]{2,1,0:T(8,128)(2,1)}, u32[]{:S(2)}, u32[]{:S(2)}) collective-permute-start(bf16[1,7168,512]{2,1,0:T(8,128)(2,1)} %u0.3), channel_id=1, source_target_pairs={{0,4},{4,0},{8,12},{12,8},{16,20},{20,16},{24,28},{28,24},{32,36},... | collective-permute-start | bytes 22020104 | tf_op jit(solution)/shard_map/ppermute | solution.py:259
  0.5 69.8 %collective-permute-start.2 = (bf16[1,512,7168]{2,1,0:T(8,128)(2,1)}, bf16[1,512,7168]{2,1,0:T(8,128)(2,1)}, u32[]{:S(2)}, u32[]{:S(2)}) collective-permute-start(bf16[1,512,7168]{2,1,0:T(8,128)(2,1)} %d0.3), channel_id=1, source_target_pairs={{0,4},{4,0},{8,12},{12,8},{16,20},{20,16},{24,28},{28,24},{32,36},... | collective-permute-start | bytes 22020104 | tf_op jit(solution)/shard_map/ppermute | solution.py:259
  65.4 52.5 %all-to-all-start.2 = ((bf16[32,8,7168]{2,1,0:T(8,128)(2,1)}), bf16[32,8,7168]{2,1,0:T(8,128)(2,1)}, u32[]{:S(2)}, u32[]{:S(2)}) async-start(bf16[32,8,7168]{2,1,0:T(8,128)(2,1)} %bitcast.13), calls=%async_computation.2 | async-start | bytes 7340032 | tf_op jit(solution)/shard_map/all_to_all | solution.py:246
  117.9 52.5 %all-to-all-start.1 = ((bf16[32,8,7168]{2,1,0:T(8,128)(2,1)}), bf16[32,8,7168]{2,1,0:T(8,128)(2,1)}, u32[]{:S(2)}, u32[]{:S(2)}) async-start(bf16[32,8,7168]{2,1,0:T(8,128)(2,1)} %bitcast.11), calls=%async_computation.1 | async-start | bytes 7340032 | tf_op jit(solution)/shard_map/all_to_all | solution.py:246
  170.5 52.5 %all-to-all-start.3 = ((bf16[32,8,7168]{2,1,0:T(8,128)(2,1)}), bf16[32,8,7168]{2,1,0:T(8,128)(2,1)}, u32[]{:S(2)}, u32[]{:S(2)}) async-start(bf16[32,8,7168]{2,1,0:T(8,128)(2,1)} %bitcast.12), calls=%async_computation.3 | async-start | bytes 7340032 | tf_op jit(solution)/shard_map/all_to_all | solution.py:246

commit v3 on v2

v3 whole, which is shorter than its diff:
```python
import functools
import math
import jax
import jax.numpy as jnp
import numpy as np
from jax import lax
from jax.experimental import pallas as pl
from jax.experimental.pallas import tpu as pltpu
from jax.sharding import PartitionSpec as P

TOP = 2
BLOCK = 16
LANES = 128
CHUNKS = 2
VMEM_BYTES = 56 * 1024 * 1024
OFFSETS = (0, 1, -1, 2)
PARAMS = pltpu.CompilerParams(
    dimension_semantics=("arbitrary",), vmem_limit_bytes=VMEM_BYTES
)


def iota(shape, dim):
    return lax.broadcasted_iota(jnp.int32, shape, dim)


def halves(value):
    upper = value.astype(jnp.bfloat16)
    return upper, (value - upper.astype(jnp.float32)).astype(jnp.bfloat16)


def ones_where(hit):
    return hit.astype(jnp.float32).astype(jnp.bfloat16)


def times(a, b):
    return jnp.dot(a, b, preferred_element_type=jnp.float32)


def times_turned(a, b):
    return lax.dot_general(a, b, (((1,), (1,)), ((), ())), preferred_element_type=jnp.float32)


def restored_rows(tokens, gather, spread, spread3):
    x = tokens.astype(jnp.float32)
    tops = []
    for at in range(0, x.shape[1], LANES):
        top = jnp.abs(x[:, at : at + LANES])
        for step in (1, 2, 4, 8):
            top = jnp.maximum(top, pltpu.roll(top, LANES - step, 1))
        tops.append(top.astype(jnp.bfloat16))
    largest = times(jnp.concatenate(tops, axis=1), gather)
    scale = (jnp.maximum(largest, 0.25) / 9.0).astype(jnp.bfloat16)
    inverse = 1.0 / scale.astype(jnp.float32)
    first, rest = halves(inverse)
    second, third = halves(inverse - first.astype(jnp.float32))
    inverse = times(jnp.concatenate([first, second, third], axis=1), spread3)
    scale = times(scale, spread)
    payload = jnp.clip(x * inverse, -6.0, 6.0).astype(jnp.bfloat16).astype(jnp.float32)
    return (payload * scale).astype(jnp.bfloat16)


def restore_kernel(wide, ids_ref, affinity_ref, tokens_ref, a_ref, b_ref):
    count, half = tokens_ref.shape
    blocks = wide // BLOCK
    gather = ones_where(iota((wide, blocks), 0) == BLOCK * iota((wide, blocks), 1))
    spread = ones_where(iota((blocks, wide), 1) // BLOCK == iota((blocks, wide), 0))
    spread3 = jnp.concatenate([spread] * 3, axis=0)

    def fill(out_ref):
        for at in range(0, half, wide):
            out_ref[:, at : at + wide] = restored_rows(
                tokens_ref[:, at : at + wide], gather, spread, spread3
            )
        ids = ids_ref[...].astype(jnp.float32)
        affinity = affinity_ref[...]
        total = affinity[0:1, :]
        for k in range(1, TOP):
            total = total + affinity[k : k + 1, :]
        lines = [ids[k : k + 1, :].astype(jnp.bfloat16) for k in range(TOP)]
        for k in range(TOP):
            lines.extend(halves(affinity[k : k + 1, :] / total))
        row = iota((BLOCK, count), 0)
        turned = jnp.zeros((BLOCK, count), jnp.float32)
        for j, line in enumerate(lines):
            turned = jnp.where(row == j, line.astype(jnp.float32), turned)
        same = ones_where(iota((count, count), 0) == iota((count, count), 1))
        by_token = times_turned(same, turned.astype(jnp.bfloat16)).astype(jnp.bfloat16)
        place = ones_where(iota((BLOCK, LANES), 0) == iota((BLOCK, LANES), 1))
        out_ref[:, half : half + LANES] = times(by_token, place).astype(jnp.bfloat16)

    @pl.when(pl.program_id(0) == 0)
    def _():
        fill(a_ref)

    @pl.when(pl.program_id(0) == 1)
    def _():
        fill(b_ref)


def restore(tokens, turned_ids, turned_affinity):
    count, width = tokens.shape
    half = width // 2
    wide = half // 4
    small = pl.BlockSpec((TOP, count), lambda h: (0, 0))
    out = jax.ShapeDtypeStruct((count, half + LANES), jnp.bfloat16)
    return pl.pallas_call(
        functools.partial(restore_kernel, wide),
        name="restore_tokens",
        out_shape=[out, out],
        grid=(2,),
        in_specs=[small, small, pl.BlockSpec((count, half), lambda h: (0, h))],
        out_specs=[pl.BlockSpec((count, half + LANES), lambda h: (0, 0))] * 2,
        compiler_params=PARAMS,
    )(turned_ids, turned_affinity, tokens)


def slot_tables(meta, targets, side):
    count = meta.shape[0]
    each = count * TOP * 2 // (side * side) // CHUNKS
    rows = side * each
    pickers = ones_where(iota((BLOCK, LANES), 0) == iota((BLOCK, LANES), 1))
    lines = times_turned(pickers, meta)
    hit = None
    upper = lower = jnp.zeros((side, count), jnp.float32)
    for k in range(TOP):
        this = lines[k : k + 1, :] == targets
        upper = jnp.where(this, lines[TOP + 2 * k : TOP + 2 * k + 1, :], upper)
        lower = jnp.where(this, lines[TOP + 2 * k + 1 : TOP + 2 * k + 2, :], lower)
        hit = this if hit is None else hit | this
    earlier = ones_where(iota((count, count), 0) < iota((count, count), 1))
    rank = times(ones_where(hit), earlier)
    key = jnp.where(hit, rank, -1.0).astype(jnp.bfloat16)
    row = iota((CHUNKS * rows, side), 0)
    spread = ones_where((row % rows) // each == iota((CHUNKS * rows, side), 1))
    place = iota((CHUNKS * rows, count), 0)
    place = ((place // rows) * each + place % each).astype(jnp.float32)
    hits = times(spread, key) == place
    return hits, times(spread, upper.astype(jnp.bfloat16)), times(spread, lower.astype(jnp.bfloat16))


def pick_kernel(side, targets_ref, *rest):
    ins, outs, picks = rest[:18], rest[18:-1], rest[-1]
    step = pl.program_id(0)
    rows = picks.shape[2] // CHUNKS
    each = rows // side

    @pl.when(step == 0)
    def _():
        for h in range(2):
            own = ins[9 * h : 9 * h + 9]
            notes = (own[3], own[4], own[5], own[8])
            targets = targets_ref[side * h : side * h + side, :]
            for i, note in enumerate(notes):
                hits, _u, _l = slot_tables(note[...], targets, side)
                picks[h, i] = ones_where(hits)

    for h in range(2):
        own = ins[9 * h : 9 * h + 9]
        opposite = jnp.where(step < 2, own[6][...], own[7][...])
        for i, block in enumerate((own[0][...], own[1][...], own[2][...], opposite)):
            found = times(picks[h, i], block).astype(jnp.bfloat16)
            for j in range(CHUNKS):
                for o in range(side):
                    at = j * rows + o * each
                    outs[(j * 2 + h) * side + o][i * each : (i + 1) * each, :] = found[
                        at : at + each
                    ]


def pick_slots(targets, gathered, side):
    count, padded = gathered[0][0].shape
    half = padded - LANES
    wide = half // 4
    each = count * TOP * 2 // (side * side) // CHUNKS
    rows = side * each
    note = pl.BlockSpec((count, LANES), lambda q: (0, half // LANES))
    late_note = pl.BlockSpec((count, LANES), lambda q: (0, half // 2 // LANES))
    data = pl.BlockSpec((count, wide), lambda q: (0, q))
    first = pl.BlockSpec((count, wide), lambda q: (0, jnp.minimum(q, 1)))
    second = pl.BlockSpec((count, wide), lambda q: (0, jnp.maximum(q - 2, 0)))
    specs, args = [pl.BlockSpec(targets.shape, lambda q: (0, 0))], [targets]
    for own, back, ahead, piece1, piece2 in gathered:
        specs += [data] * 3 + [note] * 3 + [first, second, late_note]
        args += [own, back, ahead, own, back, ahead, piece1, piece2, piece2]
    outs = pl.pallas_call(
        functools.partial(pick_kernel, side),
        name="pick_slots",
        out_shape=[jax.ShapeDtypeStruct((rows, half), jnp.bfloat16)] * (CHUNKS * 2 * side),
        grid=(4,),
        in_specs=specs,
        out_specs=[pl.BlockSpec((rows, wide), lambda q: (0, q))] * (CHUNKS * 2 * side),
        scratch_shapes=[pltpu.VMEM((2, side, CHUNKS * rows, count), jnp.bfloat16)],
        compiler_params=PARAMS,
    )(*args)
    return [
        [[outs[(j * 2 + h) * side + o] for o in range(side)] for h in range(2)]
        for j in range(CHUNKS)
    ]


def expert_kernel(side, steps, *refs):
    a_in, b_in = refs[:side], refs[side : 2 * side]
    g0, g1, u0, u1, d0, d1 = refs[2 * side : 2 * side + 6]
    a_out, b_out = refs[2 * side + 6 : 3 * side + 6], refs[3 * side + 6 : 4 * side + 6]
    x, gate0, gate1, up0, up1, hid0, hid1 = refs[4 * side + 6 :]
    step = pl.program_id(0)
    rows = a_in[0].shape[0]
    each = rows // side
    pairs = ((gate0, g0), (gate1, g1), (up0, u0), (up1, u1))

    @pl.when(step == 0)
    def _():
        for total, _w in pairs:
            total[...] = jnp.zeros_like(total)

    @pl.when(step < steps // 2)
    def _():
        for p in range(side):
            x[p * rows : (p + 1) * rows, :] = a_in[p][...]

    @pl.when((step >= steps // 2) & (step < steps))
    def _():
        for p in range(side):
            for q in range(side):
                at = p * rows + q * each
                x[at : at + each, :] = b_in[q][p * each : (p + 1) * each, :]

    @pl.when(step < steps)
    def _():
        for total, w in pairs:
            total[...] += times(x[...], w[...])

    @pl.when(step == steps - 1)
    def _():
        for hid, gate, up in ((hid0, gate0, up0), (hid1, gate1, up1)):
            v = gate[...]
            hid[...] = (v / (1.0 + jnp.exp(-v)) * up[...]).astype(jnp.bfloat16)

    def down():
        return (times(hid0[...], d0[...]) + times(hid1[...], d1[...])).astype(jnp.bfloat16)

    @pl.when((step >= steps) & (step < steps + steps // 2))
    def _():
        y = down()
        for p in range(side):
            a_out[p][...] = y[p * rows : (p + 1) * rows]

    @pl.when(step >= steps + steps // 2)
    def _():
        y = down()
        for p in range(side):
            for q in range(side):
                at = p * rows + q * each
                b_out[q][p * each : (p + 1) * each, :] = y[at : at + each]


def expert(parts, gates, ups, downs):
    a_rows, b_rows = parts
    side = len(a_rows)
    rows, half = a_rows[0].shape
    hidden = gates.shape[-1]
    count = side * rows
    wide = half // 4
    steps = 2 * half // wide
    clamp = lambda s, start: jnp.clip(s - start, 0, steps // 2 - 1)
    block = lambda start: pl.BlockSpec((rows, wide), lambda s: (0, clamp(s, start)))
    into = [
        pl.BlockSpec((None, wide, hidden), lambda s, c=c: (c, jnp.minimum(s, steps - 1), 0))
        for c in range(2)
    ]
    out_of = [
        pl.BlockSpec((None, hidden, wide), lambda s, c=c: (c, 0, jnp.maximum(s - steps, 0)))
        for c in range(2)
    ]
    outs = pl.pallas_call(
        functools.partial(expert_kernel, side, steps),
        name="expert_rows",
        out_shape=[jax.ShapeDtypeStruct((rows, half), jnp.bfloat16)] * (2 * side),
        grid=(2 * steps,),
        in_specs=[block(0)] * side + [block(steps // 2)] * side + into * 2 + out_of,
        out_specs=[block(steps)] * side + [block(steps + steps // 2)] * side,
        scratch_shapes=[pltpu.VMEM((count, wide), jnp.bfloat16)]
        + [pltpu.VMEM((count, hidden), jnp.float32)] * 4
        + [pltpu.VMEM((count, hidden), jnp.bfloat16)] * 2,
        compiler_params=PARAMS,
        cost_estimate=pl.CostEstimate(
            flops=count * half * hidden * 24,
            transcendentals=count * hidden * 2,
            bytes_accessed=half * hidden * 24 + count * half * 8,
        ),
    )(*a_rows, *b_rows, gates, gates, ups, ups, downs, downs)
    return outs[:side], outs[side:]


def weight_kernel(side, targets_ref, *rest):
    notes, out_ref = rest[:-1], rest[-1]
    count = notes[0].shape[0]
    same = ones_where(iota((count, count), 0) == iota((count, count), 1))
    for h in range(2):
        targets = targets_ref[side * h : side * h + side, :]
        for i in range(side):
            hits, upper, lower = slot_tables(notes[h * side + i][...], targets, side)
            for j, part in enumerate((upper, lower)):
                turned = times_turned(same, jnp.where(hits, part, 0.0).astype(jnp.bfloat16))
                out_ref[h, i, j * count : (j + 1) * count, :] = turned.astype(jnp.bfloat16)


def weights_of_slots(targets, gathered, side):
    count, padded = gathered[0][0].shape
    half = padded - LANES
    slots = side * count * TOP * 2 // (side * side)
    note = pl.BlockSpec((count, LANES), lambda q: (0, half // LANES))
    late_note = pl.BlockSpec((count, LANES), lambda q: (0, half // 2 // LANES))
    args = [targets]
    for own, back, ahead, piece1, piece2 in gathered:
        args += [own, back, ahead, piece2]
    shape = (2, side, 2 * count, slots)
    return pl.pallas_call(
        functools.partial(weight_kernel, side),
        name="slot_weights",
        out_shape=jax.ShapeDtypeStruct(shape, jnp.bfloat16),
        grid=(1,),
        in_specs=[pl.BlockSpec(targets.shape, lambda q: (0, 0))]
        + ([note] * 3 + [late_note]) * 2,
        out_specs=pl.BlockSpec(shape, lambda q: (0, 0, 0, 0)),
        compiler_params=PARAMS,
    )(*args)


def partial_kernel(side, table_ref, *rest):
    ins = rest[: CHUNKS * 2 * side]
    outs = rest[CHUNKS * 2 * side :]
    count = table_ref.shape[2] // 2
    rows = ins[0].shape[0]
    each = rows // side
    step = pl.program_id(0)
    for h in range(2):
        own, back, ahead, piece1, piece2 = outs[5 * h : 5 * h + 5]
        for i in range(side):
            values = jnp.concatenate(
                [
                    ins[(j * 2 + h) * side + o][i * each : (i + 1) * each, :]
                    for j in range(CHUNKS)
                    for o in range(side)
                ],
                axis=0,
            )
            both = times(table_ref[h, i], values)
            total = both[:count] + both[count:]
            if i == 0:
                own[...] = total
            elif i < 3:
                (back, ahead)[i - 1][...] = total.astype(jnp.bfloat16)
            else:
                pl.when(step < 2)(
                    lambda r=piece1, t=total: r.__setitem__(Ellipsis, t.astype(jnp.bfloat16))
                )
                pl.when(step >= 2)(
                    lambda r=piece2, t=total: r.__setitem__(Ellipsis, t.astype(jnp.bfloat16))
                )


def partial_sums(table, parts):
    side = table.shape[1]
    count = table.shape[2] // 2
    rows, half = parts[0][0][0].shape
    wide = half // 4
    data = pl.BlockSpec((rows, wide), lambda q: (0, q))
    whole = pl.BlockSpec((count, wide), lambda q: (0, q))
    first = pl.BlockSpec((count, wide), lambda q: (0, jnp.minimum(q, 1)))
    second = pl.BlockSpec((count, wide), lambda q: (0, jnp.maximum(q - 2, 0)))
    shape = lambda w, t: jax.ShapeDtypeStruct((count, w), t)
    bf16 = jnp.bfloat16
    outs = pl.pallas_call(
        functools.partial(partial_kernel, side),
        name="partial_sums",
        out_shape=[
            shape(half, jnp.float32),
            shape(half, bf16),
            shape(half, bf16),
            shape(half // 2, bf16),
            shape(half // 2, bf16),
        ]
        * 2,
        grid=(4,),
        in_specs=[pl.BlockSpec(table.shape, lambda q: (0, 0, 0, 0))]
        + [data] * (CHUNKS * 2 * side),
        out_specs=[whole, whole, whole, first, second] * 2,
        compiler_params=PARAMS,
    )(table, *[p for chunk in parts for ring in chunk for p in ring])
    return outs[:5], outs[5:]


def add_kernel(*refs):
    step = pl.program_id(0)
    for h in range(2):
        back, ahead, piece1, piece2 = refs[4 * h : 4 * h + 4]
        back_out, ahead_out = refs[8 + 2 * h : 10 + 2 * h]

        def joined(base, piece):
            return (base[...].astype(jnp.float32) + piece[...].astype(jnp.float32)).astype(
                jnp.bfloat16
            )

        @pl.when(step == 0)
        def _():
            ahead_out[...] = joined(ahead, piece1)
            back_out[...] = back[...]

        @pl.when(step == 1)
        def _():
            back_out[...] = joined(back, piece2)
            ahead_out[...] = ahead[...]


def add_pieces(groups):
    count, half = groups[0][0].shape
    data = pl.BlockSpec((count, half // 2), lambda q: (0, q))
    piece = pl.BlockSpec((count, half // 2), lambda q: (0, 0))
    outs = pl.pallas_call(
        add_kernel,
        name="add_pieces",
        out_shape=[jax.ShapeDtypeStruct((count, half), jnp.bfloat16)] * 4,
        grid=(2,),
        in_specs=[data, data, piece, piece] * 2,
        out_specs=[data] * 4,
        compiler_params=PARAMS,
    )(*groups[0], *groups[1])
    return outs[:2], outs[2:]


def sum_kernel(steps, *refs):
    out_ref = refs[-1]
    step = pl.program_id(0)
    for h in range(2):

        @pl.when(step // steps == h)
        def _():
            own, one, two = refs[3 * h : 3 * h + 3]
            out_ref[...] = (
                own[...] + one[...].astype(jnp.float32) + two[...].astype(jnp.float32)
            ).astype(jnp.bfloat16)


def final_sum(groups):
    count, half = groups[0][0].shape
    steps = 2
    wide = half // steps
    first = pl.BlockSpec((count, wide), lambda q: (0, jnp.minimum(q, steps - 1)))
    second = pl.BlockSpec((count, wide), lambda q: (0, jnp.maximum(q - steps, 0)))
    return pl.pallas_call(
        functools.partial(sum_kernel, steps),
        name="final_sum",
        out_shape=jax.ShapeDtypeStruct((count, 2 * half), jnp.bfloat16),
        grid=(2 * steps,),
        in_specs=[first] * 3 + [second] * 3,
        out_specs=pl.BlockSpec((count, wide), lambda q: (0, q)),
        compiler_params=PARAMS,
    )(*groups[0], *groups[1])


def on_device(tokens, expert_ids, affinity, w_gate, w_up, w_down):
    devices = lax.axis_size("ep")
    side = math.isqrt(devices // 2)
    half = tokens.shape[1] // 2

    def move(value, ring, offset):
        pairs = []
        for s in range(devices):
            z, y, core = s // 2 // side, s // 2 % side, s % 2
            z, y = ((z, (y + offset) % side), ((z + offset) % side, y))[ring]
            pairs.append((s, (z * side + y) * 2 + core))
        return lax.ppermute(value, "ep", pairs)

    experts = np.zeros((devices, 2 * side), np.float32)
    for s in range(devices):
        z, y = s // 2 // side, s // 2 % side
        experts[s, :side] = [(z + o) % side * side + y for o in OFFSETS]
        experts[s, side:] = [z * side + (y + o) % side for o in OFFSETS]
    targets = jnp.asarray(experts)[lax.axis_index("ep")]
    targets = jnp.broadcast_to(targets[:, None], (2 * side, tokens.shape[0]))

    mates = [[s, s + 1] for s in range(0, devices, 2)]
    gates, ups, downs = [
        lax.all_gather(w, "ep", axis_index_groups=mates, axis=0, tiled=True)
        for w in (w_gate, w_up, w_down)
    ]

    own = restore(tokens, expert_ids.T, affinity.T)
    near = [(move(own[h], h, 1), move(own[h], h, -1)) for h in range(2)]
    gathered = []
    for h in range(2):
        back, ahead = near[h]
        piece1 = move(back[:, : half // 2], h, 1)
        piece2 = move(ahead[:, half // 2 :], h, -1)
        gathered.append((own[h], back, ahead, piece1, piece2))
    sent = pick_slots(targets, gathered, side)
    table = weights_of_slots(targets, gathered, side)

    def across(rings, sign):
        return [
            [v if o == 0 else move(v, 1 - h, sign * o) for o, v in zip(OFFSETS, rings[h])]
            for h in range(2)
        ]

    parts = [across(expert(across(rings, 1), gates, ups, downs), -1) for rings in sent]
    sums = partial_sums(table, parts)
    joined = add_pieces(
        [
            (back, ahead, move(piece1, h, 1), move(piece2, h, -1))
            for h, (_own, back, ahead, piece1, piece2) in enumerate(sums)
        ]
    )
    return final_sum(
        [
            (sums[h][0], move(joined[h][0], h, -1), move(joined[h][1], h, 1))
            for h in range(2)
        ]
    )


def solution(mesh):
    rows = P(("dp", "ep"), None)
    weights = P("ep", None, None)
    return jax.shard_map(
        on_device,
        mesh=mesh,
        in_specs=(rows, rows, rows, weights, weights, weights),
        out_specs=rows,
        check_vma=False,
    )
```

time: 232 us -> 274 us (1.18)
  blocking collectives: 54.1 us -> 0 us
  starting transfers between devices: 15 us -> 61.3 us
  Pallas kernels: 70.9 us -> 98.3 us
  between operations: 0.05 us -> 13.5 us
  local copies, waits for them, and re-layouts: 0 us -> 11.6 us
    all_to_all x3 -> x0, waiting for transfers between devices: 90.7 us -> none  [exchange(): lax.all_to_all(split, 'ep', split_axis=0, concat_axis=0, tiled=True)]
    ppermute x3 -> x40, waiting for transfers between devices: 0.01 us -> 86.3 us  [move(): return lax.ppermute(value, 'ep', pairs)]
    ppermute x3 -> x40, starting transfers between devices: 0.51 us -> 61.2 us  [move(): return lax.ppermute(value, 'ep', pairs)]
    all_to_all x1 -> x0, blocking collectives: 54.1 us -> none  [exchange(): lax.all_to_all(split, 'ep', split_axis=0, concat_axis=0, tiled=True)]
    pallas_call x5 -> x8, Pallas kernels: 70.9 us -> 98.3 us  [the longest x2 55.6 us: expert(): pl.pallas_call(functools.partial(expert_kernel, side, steps), name='exper...]
    all_to_all x3 -> x0, starting transfers between devices: 14.5 us -> none  [exchange(): lax.all_to_all(split, 'ep', split_axis=0, concat_axis=0, tiled=True)]
    unnamed x0 -> x74, local copies, waits for them, and re-layouts: none -> 6.73 us
    slice x0 -> x4, local copies, waits for them, and re-layouts: none -> 3.42 us  [the longest x2 1.77 us: on_device(): piece2 = move(ahead[:, half // 2:], h, -1)]
  transfers between devices with their start and end apart: 6 -> 43, of which waited for: 3 -> 16; matrix products, arithmetic and copies ran while one was open for 0% -> 2% of each run, Pallas kernels for 27% -> 29%
where the time goes in v3:
time: 274 us; the launch traced here: 273 us
  Pallas kernels  98.3 us (36%)
  waiting for transfers between devices  88.4 us (32%)
  starting transfers between devices  61.3 us (22%)
  between operations  13.5 us (5%)
  local copies, waits for them, and re-layouts  11.6 us (4%)
    ppermute x40, waiting for transfers between devices, move(): return lax.ppermute(value, 'ep', pairs)  86.3 us
    ppermute x40, starting transfers between devices, move(): return lax.ppermute(value, 'ep', pairs)  61.2 us
    pallas_call x2, Pallas kernels, expert(): pl.pallas_call(functools.partial(expert_kernel, side, steps), name='exper...  55.6 us
    pallas_call x1, Pallas kernels, pick_slots(): pl.pallas_call(functools.partial(pick_kernel, side), name='pick_slots', o...  9.91 us
    pallas_call x1, Pallas kernels, partial_sums(): pl.pallas_call(functools.partial(partial_kernel, side), name='partial_sum...  9.8 us
    pallas_call x1, Pallas kernels, restore(): pl.pallas_call(functools.partial(restore_kernel, wide), name='restore_tok...  8.09 us
    unnamed x74, local copies, waits for them, and re-layouts  6.73 us
  transfers between devices with their start and end apart: 43, of which 16 were waited for; matrix products, arithmetic and copies ran while one was open for 2% of the time, Pallas kernels for 29%

profile of v3, /device:TPU:0, one launch (start us, length us, event | category | flops | bytes accessed | tf_op | source)
XLA Modules:
  0.0 273.0 jit_solution(3268341635270560964)
XLA Ops:
  8.7 8.1 %restore_tokens.1 = (bf16[128,3712]{1,0:T(8,128)(2,1)}, bf16[128,3712]{1,0:T(8,128)(2,1)}) custom-call(s32[2,128]{1,0:T(2,128)} %bitcast.4, f32[2,128]{1,0:T(2,128)} %bitcast.5, bf16[128,7168]{1,0:T(8,128)(2,1)} %tokens_ref.1), custom_call_target="tpu_custom_call" | custom-call | tf_op jit(solution)/shard_map/restore_tokens/pallas_call | solution.py:106
  19.9 4.0 %collective-permute-start.4 = (bf16[128,3712]{1,0:T(8,128)(2,1)}, bf16[128,3712]{1,0:T(8,128)(2,1)S(1)}, u32[]{:S(2)}, u32[]{:S(2)}) collective-permute-start(bf16[128,3712]{1,0:T(8,128)(2,1)} %get-tuple-element.54.rest_4_.rest_9_.rest_12_), channel_id=1, source_target_pairs={{0,96},{4,100},{8,104},{12,108},{16,112},{20,116},{24,120},{28,124... | collective-permute-start | bytes 2850824 | tf_op jit(solution)/shard_map/ppermute | solution.py:473
  24.0 16.6 %collective-permute-done.1.rest_2_.rest_5_ = bf16[128,3712]{1,0:T(8,128)(2,1)S(1)} collective-permute-done((bf16[128,3712]{1,0:T(8,128)(2,1)}, bf16[128,3712]{1,0:T(8,128)(2,1)S(1)}, u32[]{:S(2)}, u32[]{:S(2)}) %collective-permute-start.1) | collective-permute-done | bytes 950304 | tf_op jit(solution)/shard_map/ppermute | solution.py:473
  41.4 3.6 %collective-permute-start.2 = (bf16[128,1920]{1,0:T(8,128)(2,1)}, bf16[128,1920]{1,0:T(8,128)(2,1)S(1)}, u32[]{:S(2)}, u32[]{:S(2)}) collective-permute-start(bf16[128,1920]{1,0:T(8,128)(2,1)} %slice.16), channel_id=1, source_target_pairs={{0,24},{4,28},{8,0},{12,4},{16,8},{20,12},{24,16},{28,20},{32,56},... | collective-permute-start | bytes 1474568 | tf_op jit(solution)/shard_map/ppermute | solution.py:473
  45.9 4.0 %collective-permute-start.5 = (bf16[128,1920]{1,0:T(8,128)(2,1)}, bf16[128,1920]{1,0:T(8,128)(2,1)}, u32[]{:S(2)}, u32[]{:S(2)}) collective-permute-start(bf16[128,1920]{1,0:T(8,128)(2,1)} %slice.17), channel_id=1, source_target_pairs={{0,96},{4,100},{8,104},{12,108},{16,112},{20,116},{24,120},{28,124... | collective-permute-start | bytes 1474568 | tf_op jit(solution)/shard_map/ppermute | solution.py:473
  53.3 9.9 %collective-permute-done.6.rest_6_ = bf16[128,1792]{1,0:T(8,128)(2,1)} collective-permute-done((bf16[128,1792]{1,0:T(8,128)(2,1)}, bf16[128,1792]{1,0:T(8,128)(2,1)}, u32[]{:S(2)}, u32[]{:S(2)}) %collective-permute-start.6) | collective-permute-done | bytes 458784 | tf_op jit(solution)/shard_map/ppermute | solution.py:473
  65.7 9.9 %pick_slots.1 = (bf16[64,3584]{1,0:T(8,128)(2,1)}, bf16[64,3584]{1,0:T(8,128)(2,1)}, bf16[64,3584]{1,0:T(8,128)(2,1)}, bf16[64,3584]{1,0:T(8,128)(2,1)}, bf16[64...) custom-call(f32[8,128]{1,0:T(8,128)} %broadcast_in_dim.8.targets_ref, ...), custom_call_target="tpu_custom_call" | custom-call | tf_op jit(solution)/shard_map/pick_slots/pallas_call | solution.py:185
  75.7 3.2 %collective-permute-start.9 = (bf16[64,3584]{1,0:T(8,128)(2,1)}, bf16[64,3584]{1,0:T(8,128)(2,1)S(1)}, u32[]{:S(2)}, u32[]{:S(2)}) collective-permute-start(bf16[64,3584]{1,0:T(8,128)(2,1)} %get-tuple-element.57), channel_id=1, source_target_pairs={{0,96},{4,100},{8,104},{12,108},{16,112},{20,116},{24,120},{28,124... | collective-permute-start | bytes 1376264 | tf_op jit(solution)/shard_map/ppermute | solution.py:473
  79.0 3.2 %collective-permute-start.12 = (bf16[64,3584]{1,0:T(8,128)(2,1)}, bf16[64,3584]{1,0:T(8,128)(2,1)S(1)}, u32[]{:S(2)}, u32[]{:S(2)}) collective-permute-start(bf16[64,3584]{1,0:T(8,128)(2,1)} %get-tuple-element.61), channel_id=1, source_target_pairs={{0,24},{4,28},{8,0},{12,4},{16,8},{20,12},{24,16},{28,20},{32,56},... | collective-permute-start | bytes 1376264 | tf_op jit(solution)/shard_map/ppermute | solution.py:473
  82.2 16.8 %collective-permute-done.8.refs_1_ = bf16[64,3584]{1,0:T(8,128)(2,1)S(1)} collective-permute-done((bf16[64,3584]{1,0:T(8,128)(2,1)}, bf16[64,3584]{1,0:T(8,128)(2,1)S(1)}, u32[]{:S(2)}, u32[]{:S(2)}) %collective-permute-start.8) | collective-permute-done | bytes 458784 | tf_op jit(solution)/shard_map/ppermute | solution.py:473
  100.4 3.2 %collective-permute-start.21 = (bf16[64,3584]{1,0:T(8,128)(2,1)}, bf16[64,3584]{1,0:T(8,128)(2,1)S(1)}, u32[]{:S(2)}, u32[]{:S(2)}) collective-permute-start(bf16[64,3584]{1,0:T(8,128)(2,1)} %get-tuple-element.73), channel_id=1, source_target_pairs={{0,96},{4,100},{8,104},{12,108},{16,112},{20,116},{24,120},{28,124... | collective-permute-start | bytes 1376264 | tf_op jit(solution)/shard_map/ppermute | solution.py:473
  108.0 6.1 %collective-permute-done.13.refs_7_ = bf16[64,3584]{1,0:T(8,128)(2,1)S(1)} collective-permute-done((bf16[64,3584]{1,0:T(8,128)(2,1)}, bf16[64,3584]{1,0:T(8,128)(2,1)S(1)}, u32[]{:S(2)}, u32[]{:S(2)}) %collective-permute-start.13) | collective-permute-done | bytes 458784 | tf_op jit(solution)/shard_map/ppermute | solution.py:473
  118.3 27.8 %expert_rows.2 = (bf16[64,3584]{1,0:T(8,128)(2,1)}, bf16[64,3584]{1,0:T(8,128)(2,1)}, bf16[64,3584]{1,0:T(8,128)(2,1)}, bf16[64,3584]{1,0:T(8,128)(2,1)}, bf16[6...) custom-call(bf16[64,3584]{1,0:T(8,128)(2,1)} %get-tuple-element.55.refs_0_, ...), custom_call_target="tpu_custom_call" | custom-call | flops 11274289152 | bytes 51380224 | tf_op jit(solution)/shard_map/expert_rows/pallas_call | solution.py:275
  150.6 27.8 %expert_rows.3 = (bf16[64,3584]{1,0:T(8,128)(2,1)}, bf16[64,3584]{1,0:T(8,128)(2,1)}, bf16[64,3584]{1,0:T(8,128)(2,1)}, bf16[64,3584]{1,0:T(8,128)(2,1)}, bf16[6...) custom-call(bf16[64,3584]{1,0:T(8,128)(2,1)} %get-tuple-element.71.refs_0_, ...), custom_call_target="tpu_custom_call" | custom-call | flops 11274289152 | bytes 51380224 | tf_op jit(solution)/shard_map/expert_rows/pallas_call | solution.py:275
  188.6 4.5 %collective-permute-done.19.rest_7_ = bf16[64,3584]{1,0:T(8,128)(2,1)S(1)} collective-permute-done((bf16[64,3584]{1,0:T(8,128)(2,1)S(1)}, bf16[64,3584]{1,0:T(8,128)(2,1)S(1)}, u32[]{:S(2)}, u32[]{:S(2)}) %collective-permute-start.19) | collective-permute-done | bytes 458784 | tf_op jit(solution)/shard_map/ppermute | solution.py:473
  197.4 5.2 %slot_weights.1.table_ref = bf16[2,4,256,128]{3,2,1,0:T(8,128)(2,1)} custom-call(f32[8,128]{1,0:T(8,128)} %broadcast_in_dim.8.targets_ref, bf16[128,3712]{1,0:T(8,128)(2,1)} %get-tuple-element.53.rest_0_.rest_3_, bf16[128,3712]{1,0:T(8,128)(2,1)} %copy-done.2, bf16[128,3712]{1,0:T(8,128)(2,1)} %copy-done, bf16[128,1920]{1,0:T(8,128)(2,1)} %copy-done.4, ...), custom_call_target="tpu_custom_call" | custom-call | tf_op jit(solution)/shard_map/slot_weights/pallas_call | solution.py:318
  203.2 5.7 %collective-permute-done.31.rest_15_ = bf16[64,3584]{1,0:T(8,128)(2,1)S(1)} collective-permute-done((bf16[64,3584]{1,0:T(8,128)(2,1)}, bf16[64,3584]{1,0:T(8,128)(2,1)S(1)}, u32[]{:S(2)}, u32[]{:S(2)}) %collective-permute-start.31) | collective-permute-done | bytes 458784 | tf_op jit(solution)/shard_map/ppermute | solution.py:473
  209.7 9.8 %partial_sums.1 = (f32[128,3584]{1,0:T(8,128)}, bf16[128,3584]{1,0:T(8,128)(2,1)}, bf16[128,3584]{1,0:T(8,128)(2,1)}, bf16[128,1792]{1,0:T(8,128)(2,1)}, bf16[12...) custom-call(bf16[2,4,256,128]{3,2,1,0:T(8,128)(2,1)} %slot_weights.1, ...), custom_call_target="tpu_custom_call" | custom-call | tf_op jit(solution)/shard_map/partial_sums/pallas_call | solution.py:374
  219.6 3.2 %collective-permute-start.33 = (bf16[128,1792]{1,0:T(8,128)(2,1)}, bf16[128,1792]{1,0:T(8,128)(2,1)S(1)}, u32[]{:S(2)}, u32[]{:S(2)}) collective-permute-start(bf16[128,1792]{1,0:T(8,128)(2,1)} %get-tuple-element.91), channel_id=1, source_target_pairs={{0,24},{4,28},{8,0},{12,4},{16,8},{20,12},{24,16},{28,20},{32,56},... | collective-permute-start | bytes 1376264 | tf_op jit(solution)/shard_map/ppermute | solution.py:473
  226.1 3.4 %collective-permute-done.32.refs_2_ = bf16[128,1792]{1,0:T(8,128)(2,1)S(1)} collective-permute-done((bf16[128,1792]{1,0:T(8,128)(2,1)}, bf16[128,1792]{1,0:T(8,128)(2,1)S(1)}, u32[]{:S(2)}, u32[]{:S(2)}) %collective-permute-start.32) | collective-permute-done | bytes 458784 | tf_op jit(solution)/shard_map/ppermute | solution.py:473
  236.4 4.3 %add_pieces.1 = (bf16[128,3584]{1,0:T(8,128)(2,1)}, bf16[128,3584]{1,0:T(8,128)(2,1)}, bf16[128,3584]{1,0:T(8,128)(2,1)}, bf16[128,3584]{1,0:T(8,128)(2,1)}) custom-call(bf16[128,3584]{1,0:T(8,128)(2,1)} %get-tuple-element.88.refs_0_, bf16[128,3584]{1,0:T(8,128)(2,1)} %get-tuple-element.89.refs_1_, bf16[128,1792]{1,0:T(8,128)(2,1)} %copy-done.9, ...), custom_call_target="tpu_custom_call" | custom-call | tf_op jit(solution)/shard_map/add_pieces/pallas_call | solution.py:420
  245.2 9.1 %collective-permute-done.36.refs_1_ = bf16[128,3584]{1,0:T(8,128)(2,1)S(1)} collective-permute-done((bf16[128,3584]{1,0:T(8,128)(2,1)}, bf16[128,3584]{1,0:T(8,128)(2,1)S(1)}, u32[]{:S(2)}, u32[]{:S(2)}) %collective-permute-start.36) | collective-permute-done | bytes 917536 | tf_op jit(solution)/shard_map/ppermute | solution.py:473
  256.5 3.6 %collective-permute-done.39.refs_5_ = bf16[128,3584]{1,0:T(8,128)(2,1)S(1)} collective-permute-done((bf16[128,3584]{1,0:T(8,128)(2,1)}, bf16[128,3584]{1,0:T(8,128)(2,1)S(1)}, u32[]{:S(2)}, u32[]{:S(2)}) %collective-permute-start.39) | collective-permute-done | bytes 917536 | tf_op jit(solution)/shard_map/ppermute | solution.py:473
  261.1 5.4 %final_sum.1 = bf16[128,7168]{1,0:T(8,128)(2,1)} custom-call(f32[128,3584]{1,0:T(8,128)} %get-tuple-element.87.refs_0_, bf16[128,3584]{1,0:T(8,128)(2,1)} %copy-done.5, bf16[128,3584]{1,0:T(8,128)(2,1)} %copy-done.6, f32[128,3584]{1,0:T(8,128)} %get-tuple-element.98.refs_3_, bf16[128,3584]{1,0:T(8,128)(2,1)} %copy-done.7, bf16[128,3584]{1,0:T(8,128)(2,1)} %copy-done.8), custom_call_target="tpu_custom_call" | custom-call | tf_op jit(solution)/shard_map/final_sum/pallas_call | solution.py:451
  (153 shorter events, 61.0 us)
Async XLA Ops:
  6.5 111.7 %all-gather.4.cloned.1.call-start = ((), (), s32[]{:S(2)}) async-start(), calls=%async_computation | async-start | bytes 22020096 | tf_op jit(solution)/shard_map/all_gather | solution.py:485
  7.3 111.0 %all-gather.6.cloned.1.call-start = ((), (), s32[]{:S(2)}) async-start(), calls=%async_computation.1 | async-start | bytes 22020096 | tf_op jit(solution)/shard_map/all_gather | solution.py:485
  8.0 110.3 %all-gather.8.cloned.1.call-start = ((), (), s32[]{:S(2)}) async-start(), calls=%async_computation.2 | async-start | bytes 22020096 | tf_op jit(solution)/shard_map/all_gather | solution.py:485
  16.8 23.7 %collective-permute-start.1 = (bf16[128,3712]{1,0:T(8,128)(2,1)}, bf16[128,3712]{1,0:T(8,128)(2,1)S(1)}, u32[]{:S(2)}, u32[]{:S(2)}) collective-permute-start(bf16[128,3712]{1,0:T(8,128)(2,1)} %get-tuple-element.53.rest_0_.rest_3_), channel_id=1, source_target_pairs={{0,24},{4,28},{8,0},{12,4},{16,8},{20,12},{24,16},{28,20},{32,56},... | collective-permute-start | bytes 2850824 | tf_op jit(solution)/shard_map/ppermute | solution.py:473
  19.9 25.1 %collective-permute-start.4 = (bf16[128,3712]{1,0:T(8,128)(2,1)}, bf16[128,3712]{1,0:T(8,128)(2,1)S(1)}, u32[]{:S(2)}, u32[]{:S(2)}) collective-permute-start(bf16[128,3712]{1,0:T(8,128)(2,1)} %get-tuple-element.54.rest_4_.rest_9_.rest_12_), channel_id=1, source_target_pairs={{0,96},{4,100},{8,104},{12,108},{16,112},{20,116},{24,120},{28,124... | collective-permute-start | bytes 2850824 | tf_op jit(solution)/shard_map/ppermute | solution.py:473
  24.0 26.0 %collective-permute-start = (bf16[128,3712]{1,0:T(8,128)(2,1)}, bf16[128,3712]{1,0:T(8,128)(2,1)S(1)}, u32[]{:S(2)}, u32[]{:S(2)}) collective-permute-start(bf16[128,3712]{1,0:T(8,128)(2,1)} %get-tuple-element.53.rest_0_.rest_3_), channel_id=1, source_target_pairs={{0,8},{4,12},{8,16},{12,20},{16,24},{20,28},{24,0},{28,4},{32,40},... | collective-permute-start | bytes 2850824 | tf_op jit(solution)/shard_map/ppermute | solution.py:473
  24.0 26.9 %collective-permute-start.3 = (bf16[128,3712]{1,0:T(8,128)(2,1)}, bf16[128,3712]{1,0:T(8,128)(2,1)S(1)}, u32[]{:S(2)}, u32[]{:S(2)}) collective-permute-start(bf16[128,3712]{1,0:T(8,128)(2,1)} %get-tuple-element.54.rest_4_.rest_9_.rest_12_), channel_id=1, source_target_pairs={{0,32},{4,36},{8,40},{12,44},{16,48},{20,52},{24,56},{28,60},{32,6... | collective-permute-start | bytes 2850824 | tf_op jit(solution)/shard_map/ppermute | solution.py:473
  41.4 23.5 %collective-permute-start.2 = (bf16[128,1920]{1,0:T(8,128)(2,1)}, bf16[128,1920]{1,0:T(8,128)(2,1)S(1)}, u32[]{:S(2)}, u32[]{:S(2)}) collective-permute-start(bf16[128,1920]{1,0:T(8,128)(2,1)} %slice.16), channel_id=1, source_target_pairs={{0,24},{4,28},{8,0},{12,4},{16,8},{20,12},{24,16},{28,20},{32,56},... | collective-permute-start | bytes 1474568 | tf_op jit(solution)/shard_map/ppermute | solution.py:473
  75.6 23.3 %collective-permute-start.8 = (bf16[64,3584]{1,0:T(8,128)(2,1)}, bf16[64,3584]{1,0:T(8,128)(2,1)S(1)}, u32[]{:S(2)}, u32[]{:S(2)}) collective-permute-start(bf16[64,3584]{1,0:T(8,128)(2,1)} %get-tuple-element.56), channel_id=1, source_target_pairs={{0,32},{4,36},{8,40},{12,44},{16,48},{20,52},{24,56},{28,60},{32,6... | collective-permute-start | bytes 1376264 | tf_op jit(solution)/shard_map/ppermute | solution.py:473
  75.7 23.8 %collective-permute-start.9 = (bf16[64,3584]{1,0:T(8,128)(2,1)}, bf16[64,3584]{1,0:T(8,128)(2,1)S(1)}, u32[]{:S(2)}, u32[]{:S(2)}) collective-permute-start(bf16[64,3584]{1,0:T(8,128)(2,1)} %get-tuple-element.57), channel_id=1, source_target_pairs={{0,96},{4,100},{8,104},{12,108},{16,112},{20,116},{24,120},{28,124... | collective-permute-start | bytes 1376264 | tf_op jit(solution)/shard_map/ppermute | solution.py:473
  78.9 20.6 %collective-permute-start.10 = (bf16[64,3584]{1,0:T(8,128)(2,1)}, bf16[64,3584]{1,0:T(8,128)(2,1)S(1)}, u32[]{:S(2)}, u32[]{:S(2)}) collective-permute-start(bf16[64,3584]{1,0:T(8,128)(2,1)} %get-tuple-element.58), channel_id=1, source_target_pairs={{0,64},{4,68},{8,72},{12,76},{16,80},{20,84},{24,88},{28,92},{32,9... | collective-permute-start | bytes 1376264 | tf_op jit(solution)/shard_map/ppermute | solution.py:473
  79.0 24.6 %collective-permute-start.11 = (bf16[64,3584]{1,0:T(8,128)(2,1)}, bf16[64,3584]{1,0:T(8,128)(2,1)S(1)}, u32[]{:S(2)}, u32[]{:S(2)}) collective-permute-start(bf16[64,3584]{1,0:T(8,128)(2,1)} %get-tuple-element.60), channel_id=1, source_target_pairs={{0,8},{4,12},{8,16},{12,20},{16,24},{20,28},{24,0},{28,4},{32,40},... | collective-permute-start | bytes 1376264 | tf_op jit(solution)/shard_map/ppermute | solution.py:473
  79.0 25.4 %collective-permute-start.12 = (bf16[64,3584]{1,0:T(8,128)(2,1)}, bf16[64,3584]{1,0:T(8,128)(2,1)S(1)}, u32[]{:S(2)}, u32[]{:S(2)}) collective-permute-start(bf16[64,3584]{1,0:T(8,128)(2,1)} %get-tuple-element.61), channel_id=1, source_target_pairs={{0,24},{4,28},{8,0},{12,4},{16,8},{20,12},{24,16},{28,20},{32,56},... | collective-permute-start | bytes 1376264 | tf_op jit(solution)/shard_map/ppermute | solution.py:473
  100.4 45.7 %collective-permute-start.21 = (bf16[64,3584]{1,0:T(8,128)(2,1)}, bf16[64,3584]{1,0:T(8,128)(2,1)S(1)}, u32[]{:S(2)}, u32[]{:S(2)}) collective-permute-start(bf16[64,3584]{1,0:T(8,128)(2,1)} %get-tuple-element.73), channel_id=1, source_target_pairs={{0,96},{4,100},{8,104},{12,108},{16,112},{20,116},{24,120},{28,124... | collective-permute-start | bytes 1376264 | tf_op jit(solution)/shard_map/ppermute | solution.py:473
  104.3 41.9 %collective-permute-start.22 = (bf16[64,3584]{1,0:T(8,128)(2,1)}, bf16[64,3584]{1,0:T(8,128)(2,1)S(1)}, u32[]{:S(2)}, u32[]{:S(2)}) collective-permute-start(bf16[64,3584]{1,0:T(8,128)(2,1)} %get-tuple-element.74), channel_id=1, source_target_pairs={{0,64},{4,68},{8,72},{12,76},{16,80},{20,84},{24,88},{28,92},{32,9... | collective-permute-start | bytes 1376264 | tf_op jit(solution)/shard_map/ppermute | solution.py:473
  105.1 43.1 %collective-permute-start.23 = (bf16[64,3584]{1,0:T(8,128)(2,1)}, bf16[64,3584]{1,0:T(8,128)(2,1)S(1)}, u32[]{:S(2)}, u32[]{:S(2)}) collective-permute-start(bf16[64,3584]{1,0:T(8,128)(2,1)} %get-tuple-element.76), channel_id=1, source_target_pairs={{0,8},{4,12},{8,16},{12,20},{16,24},{20,28},{24,0},{28,4},{32,40},... | collective-permute-start | bytes 1376264 | tf_op jit(solution)/shard_map/ppermute | solution.py:473
  114.8 33.4 %collective-permute-start.24 = (bf16[64,3584]{1,0:T(8,128)(2,1)}, bf16[64,3584]{1,0:T(8,128)(2,1)S(1)}, u32[]{:S(2)}, u32[]{:S(2)}) collective-permute-start(bf16[64,3584]{1,0:T(8,128)(2,1)} %get-tuple-element.77), channel_id=1, source_target_pairs={{0,24},{4,28},{8,0},{12,4},{16,8},{20,12},{24,16},{28,20},{32,56},... | collective-permute-start | bytes 1376264 | tf_op jit(solution)/shard_map/ppermute | solution.py:473
  117.1 32.6 %collective-permute-start.25 = (bf16[64,3584]{1,0:T(8,128)(2,1)}, bf16[64,3584]{1,0:T(8,128)(2,1)}, u32[]{:S(2)}, u32[]{:S(2)}) collective-permute-start(bf16[64,3584]{1,0:T(8,128)(2,1)} %get-tuple-element.78), channel_id=1, source_target_pairs={{0,16},{4,20},{8,24},{12,28},{16,0},{20,4},{24,8},{28,12},{32,48},... | collective-permute-start | bytes 1376264 | tf_op jit(solution)/shard_map/ppermute | solution.py:473
  146.1 32.3 %collective-permute-start.14 = (bf16[64,3584]{1,0:T(8,128)(2,1)}, bf16[64,3584]{1,0:T(8,128)(2,1)S(1)}, u32[]{:S(2)}, u32[]{:S(2)}) collective-permute-start(bf16[64,3584]{1,0:T(8,128)(2,1)} %get-tuple-element.64), channel_id=1, source_target_pairs={{0,96},{4,100},{8,104},{12,108},{16,112},{20,116},{24,120},{28,124... | collective-permute-start | bytes 1376264 | tf_op jit(solution)/shard_map/ppermute | solution.py:473
  146.2 34.4 %collective-permute-start.15 = (bf16[64,3584]{1,0:T(8,128)(2,1)}, bf16[64,3584]{1,0:T(8,128)(2,1)S(1)}, u32[]{:S(2)}, u32[]{:S(2)}) collective-permute-start(bf16[64,3584]{1,0:T(8,128)(2,1)} %get-tuple-element.65), channel_id=1, source_target_pairs={{0,32},{4,36},{8,40},{12,44},{16,48},{20,52},{24,56},{28,60},{32,6... | collective-permute-start | bytes 1376264 | tf_op jit(solution)/shard_map/ppermute | solution.py:473
  148.2 35.1 %collective-permute-start.16 = (bf16[64,3584]{1,0:T(8,128)(2,1)}, bf16[64,3584]{1,0:T(8,128)(2,1)S(1)}, u32[]{:S(2)}, u32[]{:S(2)}) collective-permute-start(bf16[64,3584]{1,0:T(8,128)(2,1)} %get-tuple-element.66), channel_id=1, source_target_pairs={{0,64},{4,68},{8,72},{12,76},{16,80},{20,84},{24,88},{28,92},{32,9... | collective-permute-start | bytes 1376264 | tf_op jit(solution)/shard_map/ppermute | solution.py:473
  148.2 35.1 %collective-permute-start.17 = (bf16[64,3584]{1,0:T(8,128)(2,1)}, bf16[64,3584]{1,0:T(8,128)(2,1)S(1)}, u32[]{:S(2)}, u32[]{:S(2)}) collective-permute-start(bf16[64,3584]{1,0:T(8,128)(2,1)} %get-tuple-element.68), channel_id=1, source_target_pairs={{0,24},{4,28},{8,0},{12,4},{16,8},{20,12},{24,16},{28,20},{32,56},... | collective-permute-start | bytes 1376264 | tf_op jit(solution)/shard_map/ppermute | solution.py:473
  149.7 36.4 %collective-permute-start.18 = (bf16[64,3584]{1,0:T(8,128)(2,1)}, bf16[64,3584]{1,0:T(8,128)(2,1)S(1)}, u32[]{:S(2)}, u32[]{:S(2)}) collective-permute-start(bf16[64,3584]{1,0:T(8,128)(2,1)} %get-tuple-element.69), channel_id=1, source_target_pairs={{0,8},{4,12},{8,16},{12,20},{16,24},{20,28},{24,0},{28,4},{32,40},... | collective-permute-start | bytes 1376264 | tf_op jit(solution)/shard_map/ppermute | solution.py:473
  183.3 19.3 %collective-permute-start.27 = (bf16[64,3584]{1,0:T(8,128)(2,1)}, bf16[64,3584]{1,0:T(8,128)(2,1)S(1)}, u32[]{:S(2)}, u32[]{:S(2)}) collective-permute-start(bf16[64,3584]{1,0:T(8,128)(2,1)} %get-tuple-element.81), channel_id=1, source_target_pairs={{0,32},{4,36},{8,40},{12,44},{16,48},{20,52},{24,56},{28,60},{32,6... | collective-permute-start | bytes 1376264 | tf_op jit(solution)/shard_map/ppermute | solution.py:473
  (56 other events, 656.9 us)
Sparse Core Ops, SparseCore 0:
  9.0 32.1 all-gather.3
  42.9 31.0 all-gather.5
  75.7 31.0 all-gather.7

commit v4 on v2

--- a/solution.py
+++ b/solution.py
@@ -9,6 +9,8 @@
 TOP = 2
 BLOCK = 16
 LANES = 128
+CHUNKS = 2
+PIECES = 7
 VMEM_BYTES = 56 * 1024 * 1024
 
 
@@ -60,71 +62,92 @@
     return (payload * scale).astype(jnp.bfloat16)
 
 
-def send_kernel(experts, chunks, ids_ref, tokens_ref, *rest):
-    out_refs, (pick, gather, spread, spread3) = rest[:chunks], rest[chunks:]
-    count, width = tokens_ref.shape
-    rows = out_refs[0].shape[0]
+def pick_kernel(experts, chunk, ids_ref, tokens_ref, out_ref, tokens, rows_out, pick, got, put):
+    count, width = tokens.shape
+    rows = rows_out.shape[0]
     each = rows // experts
-    blocks = width // BLOCK
-
-    @pl.when(pl.program_id(0) == 0)
+    pieces = got.shape[0]
+    wide = width // pieces
+
+    def loaded(i):
+        part = (slice(None), pl.ds(i * wide, wide))
+        return pltpu.make_async_copy(tokens_ref.at[part], tokens.at[part], got.at[i])
+
+    def stored(i):
+        part = (slice(None), pl.ds(i * wide, wide))
+        return pltpu.make_async_copy(rows_out.at[part], out_ref.at[part], put.at[i])
+
+    for i in range(pieces):
+        loaded(i).start()
+    key = slot_keys(ids_ref, experts)
+    all_keys = times(ones_where(iota((rows, experts), 0) // each == iota((rows, experts), 1)), key)
+    place = (iota((rows, count), 0) % each + each * chunk).astype(jnp.float32)
+    pick[...] = ones_where(all_keys == place)
+    for i in range(pieces):
+        loaded(i).wait()
+        part = tokens[:, i * wide : (i + 1) * wide]
+        rows_out[:, i * wide : (i + 1) * wide] = times(pick[...], part).astype(jnp.bfloat16)
+        stored(i).start()
+    for i in range(pieces):
+        stored(i).wait()
+
+
+def slots_of_tokens(tokens, turned_ids, experts, slots, chunk):
+    count, width = tokens.shape
+    rows = experts * slots // CHUNKS
+    return pl.pallas_call(
+        functools.partial(pick_kernel, experts, chunk),
+        name="pick_slots",
+        out_shape=jax.ShapeDtypeStruct((rows, width), jnp.bfloat16),
+        in_specs=[pl.BlockSpec(memory_space=pltpu.VMEM), pl.BlockSpec(memory_space=pl.ANY)],
+        out_specs=pl.BlockSpec(memory_space=pl.ANY),
+        scratch_shapes=[
+            pltpu.VMEM((count, width), jnp.bfloat16),
+            pltpu.VMEM((rows, width), jnp.bfloat16),
+            pltpu.VMEM((rows, count), jnp.bfloat16),
+            pltpu.SemaphoreType.DMA((PIECES,)),
+            pltpu.SemaphoreType.DMA((PIECES,)),
+        ],
+        compiler_params=pltpu.CompilerParams(vmem_limit_bytes=VMEM_BYTES),
+    )(turned_ids, tokens)
+
+
+def expert_kernel(
+    steps,
+    x_ref,
+    g0,
+    g1,
+    u0,
+    u1,
+    d0,
+    d1,
+    out_ref,
+    gate0,
+    gate1,
+    up0,
+    up1,
+    hid0,
+    hid1,
+    gather,
+    spread,
+    spread3,
+):
+    step = pl.program_id(0)
+    pairs = ((gate0, g0), (gate1, g1), (up0, u0), (up1, u1))
+
+    @pl.when(step == 0)
     def _():
-        key = slot_keys(ids_ref, experts)
-        wide = times(ones_where(iota((rows, experts), 0) // each == iota((rows, experts), 1)), key)
-        place = (iota((rows, count), 0) % each).astype(jnp.float32)
-        for j in range(chunks):
-            pick[j * rows : (j + 1) * rows, :] = ones_where(wide == place + float(each * j))
+        for total, _w in pairs:
+            total[...] = jnp.zeros_like(total)
+        width, blocks = gather.shape
         gather[...] = ones_where(iota((width, blocks), 0) == BLOCK * iota((width, blocks), 1))
         spread[...] = ones_where(iota((blocks, width), 1) // BLOCK == iota((blocks, width), 0))
         for j in range(3):
             spread3[j * blocks : (j + 1) * blocks, :] = spread[...]
 
-    restored = restored_rows(tokens_ref[...], gather[...], spread[...], spread3[...])
-    for j in range(chunks):
-        out_refs[j][...] = times(pick[j * rows : (j + 1) * rows, :], restored).astype(jnp.bfloat16)
-
-
-def slots_of_tokens(tokens, turned_ids, experts, slots, chunks):
-    count, width = tokens.shape
-    rows = experts * slots // chunks
-    wide = 1024
-    blocks = wide // BLOCK
-    return pl.pallas_call(
-        functools.partial(send_kernel, experts, chunks),
-        name="send_slots",
-        out_shape=[jax.ShapeDtypeStruct((rows, width), jnp.bfloat16)] * chunks,
-        grid=(width // wide,),
-        in_specs=[
-            pl.BlockSpec((TOP, count), lambda d: (0, 0)),
-            pl.BlockSpec((count, wide), lambda d: (0, d)),
-        ],
-        out_specs=[pl.BlockSpec((rows, wide), lambda d: (0, d))] * chunks,
-        scratch_shapes=[
-            pltpu.VMEM((rows * chunks, count), jnp.bfloat16),
-            pltpu.VMEM((wide, blocks), jnp.bfloat16),
-            pltpu.VMEM((blocks, wide), jnp.bfloat16),
-            pltpu.VMEM((3 * blocks, wide), jnp.bfloat16),
-        ],
-        compiler_params=pltpu.CompilerParams(
-            dimension_semantics=("arbitrary",), vmem_limit_bytes=VMEM_BYTES
-        ),
-    )(turned_ids, tokens)
-
-
-def expert_kernel(
-    steps, x_ref, g0, g1, u0, u1, d0, d1, out_ref, gate0, gate1, up0, up1, hid0, hid1
-):
-    step = pl.program_id(0)
-    pairs = ((gate0, g0), (gate1, g1), (up0, u0), (up1, u1))
-
-    @pl.when(step == 0)
-    def _():
-        for total, _w in pairs:
-            total[...] = jnp.zeros_like(total)
-
     @pl.when(step < steps)
     def _():
-        x = x_ref[...]
+        x = restored_rows(x_ref[...], gather[...], spread[...], spread3[...])
         for total, w in pairs:
             total[...] += jnp.dot(x, w[...], preferred_element_type=jnp.float32)
 
@@ -159,7 +182,12 @@
         in_specs=[pl.BlockSpec((count, wide), lambda s: (0, first(s)))] + [into] * 4 + [out_of] * 2,
         out_specs=pl.BlockSpec((count, wide), lambda s: (0, second(s))),
         scratch_shapes=[pltpu.VMEM((count, half), jnp.float32)] * 4
-        + [pltpu.VMEM((count, half), jnp.bfloat16)] * 2,
+        + [pltpu.VMEM((count, half), jnp.bfloat16)] * 2
+        + [
+            pltpu.VMEM((wide, wide // BLOCK), jnp.bfloat16),
+            pltpu.VMEM((wide // BLOCK, wide), jnp.bfloat16),
+            pltpu.VMEM((3 * wide // BLOCK, wide), jnp.bfloat16),
+        ],
         compiler_params=pltpu.CompilerParams(
             dimension_semantics=("arbitrary",), vmem_limit_bytes=VMEM_BYTES
         ),
@@ -214,41 +242,69 @@
 
 def mix_kernel(chunks, table_ref, *rest):
     in_refs, out_ref = rest[:chunks], rest[chunks]
-    count = out_ref.shape[0]
-    total = times(table_ref[0], in_refs[0][...])
-    for j in range(1, chunks):
-        total = total + times(table_ref[j], in_refs[j][...])
-    out_ref[...] = (total[:count] + total[count:]).astype(jnp.bfloat16)
+    values, mixed, got, put = rest[chunks + 1 :]
+    count, width = mixed.shape
+    rows = values.shape[1]
+    pieces = put.shape[0]
+    wide = width // pieces
+
+    def loaded(j, i):
+        part = (slice(None), pl.ds(i * wide, wide))
+        return pltpu.make_async_copy(in_refs[j].at[part], values.at[j].at[part], got.at[j, i])
+
+    def stored(i):
+        part = (slice(None), pl.ds(i * wide, wide))
+        return pltpu.make_async_copy(mixed.at[part], out_ref.at[part], put.at[i])
+
+    for i in range(pieces):
+        for j in range(chunks):
+            loaded(j, i).start()
+    for i in range(pieces):
+        total = None
+        for j in range(chunks):
+            loaded(j, i).wait()
+            part = times(table_ref[j], values[j, :, i * wide : (i + 1) * wide])
+            total = part if total is None else total + part
+        total = total[:count] + total[count:]
+        mixed[:, i * wide : (i + 1) * wide] = total.astype(jnp.bfloat16)
+        stored(i).start()
+    for i in range(pieces):
+        stored(i).wait()
 
 
 def mix(table, parts):
     chunks, count, rows = table.shape
     count //= 2
     width = parts[0].shape[1]
-    wide = 1024
+    anywhere = pl.BlockSpec(memory_space=pl.ANY)
     return pl.pallas_call(
         functools.partial(mix_kernel, chunks),
         name="mix_slots",
         out_shape=jax.ShapeDtypeStruct((count, width), jnp.bfloat16),
-        grid=(width // wide,),
-        in_specs=[pl.BlockSpec(table.shape, lambda d: (0, 0, 0))]
-        + [pl.BlockSpec((rows, wide), lambda d: (0, d))] * chunks,
-        out_specs=pl.BlockSpec((count, wide), lambda d: (0, d)),
-        compiler_params=pltpu.CompilerParams(
-            dimension_semantics=("arbitrary",), vmem_limit_bytes=VMEM_BYTES
-        ),
+        in_specs=[pl.BlockSpec(memory_space=pltpu.VMEM)] + [anywhere] * chunks,
+        out_specs=anywhere,
+        scratch_shapes=[
+            pltpu.VMEM((chunks, rows, width), jnp.bfloat16),
+            pltpu.VMEM((count, width), jnp.bfloat16),
+            pltpu.SemaphoreType.DMA((chunks, PIECES)),
+            pltpu.SemaphoreType.DMA((PIECES,)),
+        ],
+        compiler_params=pltpu.CompilerParams(vmem_limit_bytes=VMEM_BYTES),
     )(table, *parts)
 
 
 def exchange(rows, devices):
     count, width = rows.shape
-    split = rows.reshape(devices, count // devices, width)
-    return lax.all_to_all(split, "ep", split_axis=0, concat_axis=0, tiled=True).reshape(
-        count, width
-    )
-
-
-CHUNKS = 2
+    chips = devices // 2
+    groups = [list(range(core, devices, 2)) for core in range(2)]
+    return lax.all_to_all(
+        rows.reshape(chips, count // chips, width),
+        "ep",
+        split_axis=0,
+        concat_axis=0,
+        axis_index_groups=groups,
+        tiled=True,
+    ).reshape(count, width)
 
 
 def on_device(tokens, expert_ids, affinity, w_gate, w_up, w_down):
@@ -259,11 +315,10 @@
     gates, ups, downs = [(w, lax.ppermute(w, "ep", pairs)) for w in (w_gate, w_up, w_down)]
     turned_ids = expert_ids.T
     table = weights_of_slots(turned_ids, affinity.T, experts, slots, CHUNKS)
-    sent = slots_of_tokens(tokens, turned_ids, experts, slots, CHUNKS)
     parts = []
-    for rows in sent:
-        computed = expert(exchange(rows, devices), gates, ups, downs)
-        parts.append(exchange(computed, devices))
+    for chunk in range(CHUNKS):
+        rows = exchange(slots_of_tokens(tokens, turned_ids, experts, slots, chunk), devices)
+        parts.append(exchange(expert(rows, gates, ups, downs), devices))
     return mix(table, parts)
 
 

time: 232 us -> 245 us (1.056)
  waiting for transfers between devices: 90.7 us -> 145 us
  blocking collectives: 54.1 us -> 0 us
  starting transfers between devices: 15 us -> 22.5 us
  Pallas kernels: 70.9 us -> 76.7 us
    all_to_all x1 -> x0, blocking collectives: 54.1 us -> none  [exchange(): lax.all_to_all(split, 'ep', split_axis=0, concat_axis=0, tiled=True)]
    all_to_all x3 -> x4, waiting for transfers between devices: 90.7 us -> 145 us  [exchange(): lax.all_to_all(rows.reshape(chips, count // chips, width), 'ep', split_ax...]
    pallas_call x2, Pallas kernels: 50.4 us -> 59.3 us  [expert(): pl.pallas_call(functools.partial(expert_kernel, steps), name='expert_rows...]
    all_to_all x3 -> x4, starting transfers between devices: 14.5 us -> 22 us  [exchange(): lax.all_to_all(rows.reshape(chips, count // chips, width), 'ep', split_ax...]
    pallas_call x1 -> x2, Pallas kernels: 10.8 us -> 9.12 us  [slots_of_tokens(): pl.pallas_call(functools.partial(pick_kernel, experts, chunk), name='pick...]
  transfers between devices with their start and end apart: 6 -> 7, of which waited for: 3 -> 4; matrix products, arithmetic and copies ran while one was open for 0% -> 0% of each run, Pallas kernels for 27% -> 29%
where the time goes in v4:
time: 245 us; the launch traced here: 244 us
  waiting for transfers between devices  145 us (59%)
  Pallas kernels  76.7 us (31%)
  starting transfers between devices  22.5 us (9%)
    all_to_all x4, waiting for transfers between devices, exchange(): lax.all_to_all(rows.reshape(chips, count // chips, width), 'ep', split_ax...  145 us
    pallas_call x2, Pallas kernels, expert(): pl.pallas_call(functools.partial(expert_kernel, steps), name='expert_rows...  59.3 us
    all_to_all x4, starting transfers between devices, exchange(): lax.all_to_all(rows.reshape(chips, count // chips, width), 'ep', split_ax...  22 us
    pallas_call x2, Pallas kernels, slots_of_tokens(): pl.pallas_call(functools.partial(pick_kernel, experts, chunk), name='pick...  9.12 us
    pallas_call x1, Pallas kernels, mix(): pl.pallas_call(functools.partial(mix_kernel, chunks), name='mix_slots', o...  6.37 us
  transfers between devices with their start and end apart: 7, of which 4 were waited for; matrix products, arithmetic and copies ran while one was open for 0% of the time, Pallas kernels for 29%

profile of v4, /device:TPU:0, one launch (start us, length us, event | category | flops | bytes accessed | tf_op | source)
XLA Modules:
  0.0 243.9 jit_solution(8343732561869172708)
XLA Ops:
  0.0 0.0 collective-permute-start
  0.0 0.5 collective-permute-start.1
  0.5 0.0 collective-permute-start.2
  0.5 4.6 %pick_slots.2 = bf16[256,7168]{1,0:T(8,128)(2,1)} custom-call(s32[2,128]{1,0:T(2,128)} %bitcast.14, bf16[128,7168]{1,0:T(8,128)(2,1)} %tokens_ref.3), custom_call_target="tpu_custom_call" | custom-call | tf_op jit(solution)/shard_map/pick_slots/pallas_call | solution.py:98
  5.1 8.2 %all-to-all-start = ((bf16[16,16,7168]{2,1,0:T(8,128)(2,1)}), bf16[16,16,7168]{2,1,0:T(8,128)(2,1)}, u32[]{:S(2)}, u32[]{:S(2)}) async-start(bf16[16,16,7168]{2,1,0:T(8,128)(2,1)} %bitcast.13), calls=%async_computation | async-start | bytes 7340032 | tf_op jit(solution)/shard_map/all_to_all | solution.py:300
  13.3 4.6 %pick_slots.3 = bf16[256,7168]{1,0:T(8,128)(2,1)} custom-call(s32[2,128]{1,0:T(2,128)} %bitcast.15, bf16[128,7168]{1,0:T(8,128)(2,1)} %tokens_ref.3), custom_call_target="tpu_custom_call" | custom-call | tf_op jit(solution)/shard_map/pick_slots/pallas_call | solution.py:98
  17.8 52.4 %all-to-all-done = bf16[16,16,7168]{2,1,0:T(8,128)(2,1)} async-done(((bf16[16,16,7168]{2,1,0:T(8,128)(2,1)}), bf16[16,16,7168]{2,1,0:T(8,128)(2,1)}, u32[]{:S(2)}, u32[]{:S(2)}) %all-to-all-start) | async-done | bytes 3670048 | tf_op jit(solution)/shard_map/all_to_all | solution.py:300
  70.2 4.6 %all-to-all-start.2 = ((bf16[16,16,7168]{2,1,0:T(8,128)(2,1)}), bf16[16,16,7168]{2,1,0:T(8,128)(2,1)}, u32[]{:S(2)}, u32[]{:S(2)}) async-start(bf16[16,16,7168]{2,1,0:T(8,128)(2,1)} %bitcast.12), calls=%async_computation.2 | async-start | bytes 7340032 | tf_op jit(solution)/shard_map/all_to_all | solution.py:300
  74.9 0.0 collective-permute-done.g1
  74.9 0.0 collective-permute-done.1.u1
  74.9 0.0 collective-permute-done.2.d1
  74.9 29.6 %expert_rows.2 = bf16[256,7168]{1,0:T(8,128)(2,1)} custom-call(bf16[256,7168]{1,0:T(8,128)(2,1)} %bitcast.3.x_ref, bf16[1,7168,512]{2,1,0:T(8,128)(2,1)} %g0.3, bf16[1,7168,512]{2,1,0:T(8,128)(2,1)} %collective-permute-done.g1, bf16[1,7168,512]{2,1,0:T(8,128)(2,1)} %u0.3, bf16[1,7168,512]{2,1,0:T(8,128)(2,1)} %collective-permute-done.1.u1, ...), custom_call_target="tpu_custom_call" | custom-call | flops 11274289152 | bytes 51380224 | tf_op jit(solution)/shard_map/expert_rows/pallas_call | solution.py:177
  104.6 24.7 %all-to-all-done.2 = bf16[16,16,7168]{2,1,0:T(8,128)(2,1)} async-done(((bf16[16,16,7168]{2,1,0:T(8,128)(2,1)}), bf16[16,16,7168]{2,1,0:T(8,128)(2,1)}, u32[]{:S(2)}, u32[]{:S(2)}) %all-to-all-start.2) | async-done | bytes 3670048 | tf_op jit(solution)/shard_map/all_to_all | solution.py:300
  129.3 4.7 %all-to-all-start.1 = ((bf16[16,16,7168]{2,1,0:T(8,128)(2,1)}), bf16[16,16,7168]{2,1,0:T(8,128)(2,1)}, u32[]{:S(2)}, u32[]{:S(2)}) async-start(bf16[16,16,7168]{2,1,0:T(8,128)(2,1)} %bitcast.10), calls=%async_computation.1 | async-start | bytes 7340032 | tf_op jit(solution)/shard_map/all_to_all | solution.py:300
  134.0 29.6 %expert_rows.3 = bf16[256,7168]{1,0:T(8,128)(2,1)} custom-call(bf16[256,7168]{1,0:T(8,128)(2,1)} %bitcast.7.x_ref, bf16[1,7168,512]{2,1,0:T(8,128)(2,1)} %g0.3, bf16[1,7168,512]{2,1,0:T(8,128)(2,1)} %collective-permute-done.g1, bf16[1,7168,512]{2,1,0:T(8,128)(2,1)} %u0.3, bf16[1,7168,512]{2,1,0:T(8,128)(2,1)} %collective-permute-done.1.u1, ...), custom_call_target="tpu_custom_call" | custom-call | flops 11274289152 | bytes 51380224 | tf_op jit(solution)/shard_map/expert_rows/pallas_call | solution.py:177
  163.6 21.9 %all-to-all-done.1 = bf16[16,16,7168]{2,1,0:T(8,128)(2,1)} async-done(((bf16[16,16,7168]{2,1,0:T(8,128)(2,1)}), bf16[16,16,7168]{2,1,0:T(8,128)(2,1)}, u32[]{:S(2)}, u32[]{:S(2)}) %all-to-all-start.1) | async-done | bytes 3670048 | tf_op jit(solution)/shard_map/all_to_all | solution.py:300
  185.4 4.5 %all-to-all-start.3 = ((bf16[16,16,7168]{2,1,0:T(8,128)(2,1)}), bf16[16,16,7168]{2,1,0:T(8,128)(2,1)}, u32[]{:S(2)}, u32[]{:S(2)}) async-start(bf16[16,16,7168]{2,1,0:T(8,128)(2,1)} %bitcast.11), calls=%async_computation.3 | async-start | bytes 7340032 | tf_op jit(solution)/shard_map/all_to_all | solution.py:300
  190.0 2.0 slot_weights.1.table_ref
  191.9 45.6 %all-to-all-done.3 = bf16[16,16,7168]{2,1,0:T(8,128)(2,1)} async-done(((bf16[16,16,7168]{2,1,0:T(8,128)(2,1)}), bf16[16,16,7168]{2,1,0:T(8,128)(2,1)}, u32[]{:S(2)}, u32[]{:S(2)}) %all-to-all-start.3) | async-done | bytes 3670048 | tf_op jit(solution)/shard_map/all_to_all | solution.py:300
  237.6 6.4 %mix_slots.1 = bf16[128,7168]{1,0:T(8,128)(2,1)} custom-call(bf16[2,256,256]{2,1,0:T(8,128)(2,1)} %slot_weights.1.table_ref, bf16[256,7168]{1,0:T(8,128)(2,1)} %bitcast.5.rest_0_, bf16[256,7168]{1,0:T(8,128)(2,1)} %bitcast.9.rest_1_), custom_call_target="tpu_custom_call" | custom-call | tf_op jit(solution)/shard_map/mix_slots/pallas_call | solution.py:280
Async XLA Ops:
  0.0 74.9 %collective-permute-start = (bf16[1,7168,512]{2,1,0:T(8,128)(2,1)}, bf16[1,7168,512]{2,1,0:T(8,128)(2,1)}, u32[]{:S(2)}, u32[]{:S(2)}) collective-permute-start(bf16[1,7168,512]{2,1,0:T(8,128)(2,1)} %g0.3), channel_id=1, source_target_pairs={{0,4},{4,0},{8,12},{12,8},{16,20},{20,16},{24,28},{28,24},{32,36},... | collective-permute-start | bytes 22020104 | tf_op jit(solution)/shard_map/ppermute | solution.py:315
  0.0 74.9 %collective-permute-start.1 = (bf16[1,7168,512]{2,1,0:T(8,128)(2,1)}, bf16[1,7168,512]{2,1,0:T(8,128)(2,1)}, u32[]{:S(2)}, u32[]{:S(2)}) collective-permute-start(bf16[1,7168,512]{2,1,0:T(8,128)(2,1)} %u0.3), channel_id=1, source_target_pairs={{0,4},{4,0},{8,12},{12,8},{16,20},{20,16},{24,28},{28,24},{32,36},... | collective-permute-start | bytes 22020104 | tf_op jit(solution)/shard_map/ppermute | solution.py:315
  0.5 74.4 %collective-permute-start.2 = (bf16[1,512,7168]{2,1,0:T(8,128)(2,1)}, bf16[1,512,7168]{2,1,0:T(8,128)(2,1)}, u32[]{:S(2)}, u32[]{:S(2)}) collective-permute-start(bf16[1,512,7168]{2,1,0:T(8,128)(2,1)} %d0.3), channel_id=1, source_target_pairs={{0,4},{4,0},{8,12},{12,8},{16,20},{20,16},{24,28},{28,24},{32,36},... | collective-permute-start | bytes 22020104 | tf_op jit(solution)/shard_map/ppermute | solution.py:315
  5.1 65.1 %all-to-all-start = ((bf16[16,16,7168]{2,1,0:T(8,128)(2,1)}), bf16[16,16,7168]{2,1,0:T(8,128)(2,1)}, u32[]{:S(2)}, u32[]{:S(2)}) async-start(bf16[16,16,7168]{2,1,0:T(8,128)(2,1)} %bitcast.13), calls=%async_computation | async-start | bytes 7340032 | tf_op jit(solution)/shard_map/all_to_all | solution.py:300
  70.2 59.1 %all-to-all-start.2 = ((bf16[16,16,7168]{2,1,0:T(8,128)(2,1)}), bf16[16,16,7168]{2,1,0:T(8,128)(2,1)}, u32[]{:S(2)}, u32[]{:S(2)}) async-start(bf16[16,16,7168]{2,1,0:T(8,128)(2,1)} %bitcast.12), calls=%async_computation.2 | async-start | bytes 7340032 | tf_op jit(solution)/shard_map/all_to_all | solution.py:300
  129.3 56.1 %all-to-all-start.1 = ((bf16[16,16,7168]{2,1,0:T(8,128)(2,1)}), bf16[16,16,7168]{2,1,0:T(8,128)(2,1)}, u32[]{:S(2)}, u32[]{:S(2)}) async-start(bf16[16,16,7168]{2,1,0:T(8,128)(2,1)} %bitcast.10), calls=%async_computation.1 | async-start | bytes 7340032 | tf_op jit(solution)/shard_map/all_to_all | solution.py:300
  185.4 52.1 %all-to-all-start.3 = ((bf16[16,16,7168]{2,1,0:T(8,128)(2,1)}), bf16[16,16,7168]{2,1,0:T(8,128)(2,1)}, u32[]{:S(2)}, u32[]{:S(2)}) async-start(bf16[16,16,7168]{2,1,0:T(8,128)(2,1)} %bitcast.11), calls=%async_computation.3 | async-start | bytes 7340032 | tf_op jit(solution)/shard_map/all_to_all | solution.py:300

commit v5 on v4

--- a/solution.py
+++ b/solution.py
@@ -167,19 +167,19 @@
 
 def expert(rows, gates, ups, downs):
     count, width = rows.shape
-    half = gates[0].shape[-1]
+    half = gates.shape[-1]
     wide = 1024
     steps = width // wide
     first = lambda s: jnp.minimum(s, steps - 1)
     second = lambda s: jnp.maximum(s - steps, 0)
-    into = pl.BlockSpec((None, wide, half), lambda s: (0, first(s), 0))
-    out_of = pl.BlockSpec((None, half, wide), lambda s: (0, 0, second(s)))
+    into = [pl.BlockSpec((None, wide, half), lambda s, c=c: (c, first(s), 0)) for c in range(2)]
+    out_of = [pl.BlockSpec((None, half, wide), lambda s, c=c: (c, 0, second(s))) for c in range(2)]
     return pl.pallas_call(
         functools.partial(expert_kernel, steps),
         name="expert_rows",
         out_shape=jax.ShapeDtypeStruct((count, width), jnp.bfloat16),
         grid=(2 * steps,),
-        in_specs=[pl.BlockSpec((count, wide), lambda s: (0, first(s)))] + [into] * 4 + [out_of] * 2,
+        in_specs=[pl.BlockSpec((count, wide), lambda s: (0, first(s)))] + into * 2 + out_of,
         out_specs=pl.BlockSpec((count, wide), lambda s: (0, second(s))),
         scratch_shapes=[pltpu.VMEM((count, half), jnp.float32)] * 4
         + [pltpu.VMEM((count, half), jnp.bfloat16)] * 2
@@ -196,7 +196,7 @@
             transcendentals=count * half * 2,
             bytes_accessed=width * half * 12 + count * width * 4,
         ),
-    )(rows, *gates, *ups, *downs)
+    )(rows, gates, gates, ups, ups, downs, downs)
 
 
 def table_kernel(experts, chunks, ids_ref, affinity_ref, out_ref):
@@ -295,24 +295,21 @@
 
 def exchange(rows, devices):
     count, width = rows.shape
-    chips = devices // 2
-    groups = [list(range(core, devices, 2)) for core in range(2)]
-    return lax.all_to_all(
-        rows.reshape(chips, count // chips, width),
-        "ep",
-        split_axis=0,
-        concat_axis=0,
-        axis_index_groups=groups,
-        tiled=True,
-    ).reshape(count, width)
+    split = rows.reshape(devices, count // devices, width)
+    return lax.all_to_all(split, "ep", split_axis=0, concat_axis=0, tiled=True).reshape(
+        count, width
+    )
 
 
 def on_device(tokens, expert_ids, affinity, w_gate, w_up, w_down):
     devices = lax.axis_size("ep")
     experts = devices // 2
     slots = 2 * tokens.shape[0] * TOP // experts
-    pairs = [(s, s ^ 1) for s in range(devices)]
-    gates, ups, downs = [(w, lax.ppermute(w, "ep", pairs)) for w in (w_gate, w_up, w_down)]
+    mates = [[s, s + 1] for s in range(0, devices, 2)]
+    gates, ups, downs = [
+        lax.all_gather(w, "ep", axis_index_groups=mates, axis=0, tiled=True)
+        for w in (w_gate, w_up, w_down)
+    ]
     turned_ids = expert_ids.T
     table = weights_of_slots(turned_ids, affinity.T, experts, slots, CHUNKS)
     parts = []

time: 245 us -> 258 us (1.053)
  between operations: 0.08 us -> 13.2 us
  waiting for transfers between devices: 145 us -> 141 us
  starting transfers between devices: 22.5 us -> 25.8 us
    all_to_all x4, waiting for transfers between devices: 145 us -> 107 us  [exchange(): lax.all_to_all(split, 'ep', split_axis=0, concat_axis=0, tiled=True)]
    all_gather x0 -> x3, waiting for transfers between devices: none -> 32.3 us  [on_device(): lax.all_gather(w, 'ep', axis_index_groups=mates, axis=0, tiled=True)]
    all_to_all x4, starting transfers between devices: 22 us -> 25.7 us  [exchange(): lax.all_to_all(split, 'ep', split_axis=0, concat_axis=0, tiled=True)]
  transfers between devices with their start and end apart: 7 -> 7, of which waited for: 4 -> 4; matrix products, arithmetic and copies ran while one was open for 0% -> 0% of each run, Pallas kernels for 29% -> 27%
where the time goes in v5:
time: 258 us; the launch traced here: 257 us
  waiting for transfers between devices  141 us (55%)
  Pallas kernels  76.9 us (30%)
  starting transfers between devices  25.8 us (10%)
  between operations  13.2 us (5%)
    all_to_all x4, waiting for transfers between devices, exchange(): lax.all_to_all(split, 'ep', split_axis=0, concat_axis=0, tiled=True)  107 us
    pallas_call x2, Pallas kernels, expert(): pl.pallas_call(functools.partial(expert_kernel, steps), name='expert_rows...  59.3 us
    all_gather x3, waiting for transfers between devices, on_device(): lax.all_gather(w, 'ep', axis_index_groups=mates, axis=0, tiled=True)  32.3 us
    all_to_all x4, starting transfers between devices, exchange(): lax.all_to_all(split, 'ep', split_axis=0, concat_axis=0, tiled=True)  25.7 us
    pallas_call x2, Pallas kernels, slots_of_tokens(): pl.pallas_call(functools.partial(pick_kernel, experts, chunk), name='pick...  9.31 us
    pallas_call x1, Pallas kernels, mix(): pl.pallas_call(functools.partial(mix_kernel, chunks), name='mix_slots', o...  6.37 us
  transfers between devices with their start and end apart: 7, of which 4 were waited for; matrix products, arithmetic and copies ran while one was open for 0% of the time, Pallas kernels for 27%

profile of v5, /device:TPU:0, one launch (start us, length us, event | category | flops | bytes accessed | tf_op | source)
XLA Modules:
  0.0 257.0 jit_solution(3659070275805531948)
XLA Ops:
  6.5 0.0 all-gather.4.cloned.1.call-start
  6.5 0.7 all-gather.4.cloned.1.call-update
  7.3 0.0 all-gather.6.cloned.1.call-start
  7.3 0.7 all-gather.6.cloned.1.call-update
  8.0 0.0 all-gather.8.cloned.1.call-start
  8.1 0.7 all-gather.8.cloned.1.call-update
  8.7 4.6 %pick_slots.2 = bf16[256,7168]{1,0:T(8,128)(2,1)} custom-call(s32[2,128]{1,0:T(2,128)} %bitcast.14, bf16[128,7168]{1,0:T(8,128)(2,1)} %tokens_ref.3), custom_call_target="tpu_custom_call" | custom-call | tf_op jit(solution)/shard_map/pick_slots/pallas_call | solution.py:98
  13.4 8.5 %all-to-all-start = ((bf16[32,8,7168]{2,1,0:T(8,128)(2,1)}), bf16[32,8,7168]{2,1,0:T(8,128)(2,1)}, u32[]{:S(2)}, u32[]{:S(2)}) async-start(bf16[32,8,7168]{2,1,0:T(8,128)(2,1)} %bitcast.11), calls=%async_computation | async-start | bytes 7340032 | tf_op jit(solution)/shard_map/all_to_all | solution.py:299
  21.9 4.7 %pick_slots.3 = bf16[256,7168]{1,0:T(8,128)(2,1)} custom-call(s32[2,128]{1,0:T(2,128)} %bitcast.15, bf16[128,7168]{1,0:T(8,128)(2,1)} %tokens_ref.3), custom_call_target="tpu_custom_call" | custom-call | tf_op jit(solution)/shard_map/pick_slots/pallas_call | solution.py:98
  26.6 43.0 %all-to-all-done = bf16[32,8,7168]{2,1,0:T(8,128)(2,1)} async-done(((bf16[32,8,7168]{2,1,0:T(8,128)(2,1)}), bf16[32,8,7168]{2,1,0:T(8,128)(2,1)}, u32[]{:S(2)}, u32[]{:S(2)}) %all-to-all-start) | async-done | bytes 3670048 | tf_op jit(solution)/shard_map/all_to_all | solution.py:299
  69.6 4.8 %all-to-all-start.2 = ((bf16[32,8,7168]{2,1,0:T(8,128)(2,1)}), bf16[32,8,7168]{2,1,0:T(8,128)(2,1)}, u32[]{:S(2)}, u32[]{:S(2)}) async-start(bf16[32,8,7168]{2,1,0:T(8,128)(2,1)} %bitcast.10), calls=%async_computation.2 | async-start | bytes 7340032 | tf_op jit(solution)/shard_map/all_to_all | solution.py:299
  74.5 0.0 all-gather.4.cloned.1.call-done.g0.g1
  74.5 0.0 all-gather.6.cloned.1.call-done.u0.u1
  74.5 32.3 %all-gather.8.cloned.1.call-done.d0.d1 = bf16[2,512,7168]{2,1,0:T(8,128)(2,1)} async-done(((bf16[1,512,7168]{2,1,0:T(8,128)(2,1)}), bf16[2,512,7168]{2,1,0:T(8,128)(2,1)}) %all-gather.8.cloned.1.call-update) | async-done | bytes 14680080 | tf_op jit(solution)/shard_map/all_gather | solution.py:310
  106.8 29.6 %expert_rows.2 = bf16[256,7168]{1,0:T(8,128)(2,1)} custom-call(bf16[256,7168]{1,0:T(8,128)(2,1)} %bitcast.3.x_ref, bf16[2,7168,512]{2,1,0:T(8,128)(2,1)} %all-gather.4.cloned.1.call-done.g0.g1, bf16[2,7168,512]{2,1,0:T(8,128)(2,1)} %all-gather.4.cloned.1.call-done.g0.g1, bf16[2,7168,512]{2,1,0:T(8,128)(2,1)} %all-gather.6.cloned.1.call-done.u0.u1, ...), custom_call_target="tpu_custom_call" | custom-call | flops 11274289152 | bytes 51380224 | tf_op jit(solution)/shard_map/expert_rows/pallas_call | solution.py:177
  136.4 0.0 all-to-all-done.2
  136.4 7.5 %all-to-all-start.1 = ((bf16[32,8,7168]{2,1,0:T(8,128)(2,1)}), bf16[32,8,7168]{2,1,0:T(8,128)(2,1)}, u32[]{:S(2)}, u32[]{:S(2)}) async-start(bf16[32,8,7168]{2,1,0:T(8,128)(2,1)} %bitcast.12), calls=%async_computation.1 | async-start | bytes 7340032 | tf_op jit(solution)/shard_map/all_to_all | solution.py:299
  143.9 29.7 %expert_rows.3 = bf16[256,7168]{1,0:T(8,128)(2,1)} custom-call(bf16[256,7168]{1,0:T(8,128)(2,1)} %bitcast.7.x_ref, bf16[2,7168,512]{2,1,0:T(8,128)(2,1)} %all-gather.4.cloned.1.call-done.g0.g1, bf16[2,7168,512]{2,1,0:T(8,128)(2,1)} %all-gather.4.cloned.1.call-done.g0.g1, bf16[2,7168,512]{2,1,0:T(8,128)(2,1)} %all-gather.6.cloned.1.call-done.u0.u1, ...), custom_call_target="tpu_custom_call" | custom-call | flops 11274289152 | bytes 51380224 | tf_op jit(solution)/shard_map/expert_rows/pallas_call | solution.py:177
  173.6 18.0 %all-to-all-done.1 = bf16[32,8,7168]{2,1,0:T(8,128)(2,1)} async-done(((bf16[32,8,7168]{2,1,0:T(8,128)(2,1)}), bf16[32,8,7168]{2,1,0:T(8,128)(2,1)}, u32[]{:S(2)}, u32[]{:S(2)}) %all-to-all-start.1) | async-done | bytes 3670048 | tf_op jit(solution)/shard_map/all_to_all | solution.py:299
  191.6 4.8 %all-to-all-start.3 = ((bf16[32,8,7168]{2,1,0:T(8,128)(2,1)}), bf16[32,8,7168]{2,1,0:T(8,128)(2,1)}, u32[]{:S(2)}, u32[]{:S(2)}) async-start(bf16[32,8,7168]{2,1,0:T(8,128)(2,1)} %bitcast.13), calls=%async_computation.3 | async-start | bytes 7340032 | tf_op jit(solution)/shard_map/all_to_all | solution.py:299
  196.4 2.0 slot_weights.1.table_ref
  198.4 45.7 %all-to-all-done.3 = bf16[32,8,7168]{2,1,0:T(8,128)(2,1)} async-done(((bf16[32,8,7168]{2,1,0:T(8,128)(2,1)}), bf16[32,8,7168]{2,1,0:T(8,128)(2,1)}, u32[]{:S(2)}, u32[]{:S(2)}) %all-to-all-start.3) | async-done | bytes 3670048 | tf_op jit(solution)/shard_map/all_to_all | solution.py:299
  244.1 6.4 %mix_slots.1 = bf16[128,7168]{1,0:T(8,128)(2,1)} custom-call(bf16[2,256,256]{2,1,0:T(8,128)(2,1)} %slot_weights.1.table_ref, bf16[256,7168]{1,0:T(8,128)(2,1)} %bitcast.5.rest_0_, bf16[256,7168]{1,0:T(8,128)(2,1)} %bitcast.9.rest_1_), custom_call_target="tpu_custom_call" | custom-call | tf_op jit(solution)/shard_map/mix_slots/pallas_call | solution.py:280
Async XLA Ops:
  6.5 67.9 %all-gather.4.cloned.1.call-start = ((), (), s32[]{:S(2)}) async-start(), calls=%async_computation.4 | async-start | bytes 22020096 | tf_op jit(solution)/shard_map/all_gather | solution.py:310
  7.3 67.2 %all-gather.6.cloned.1.call-start = ((), (), s32[]{:S(2)}) async-start(), calls=%async_computation.5 | async-start | bytes 22020096 | tf_op jit(solution)/shard_map/all_gather | solution.py:310
  8.0 98.8 %all-gather.8.cloned.1.call-start = ((), (), s32[]{:S(2)}) async-start(), calls=%async_computation.6 | async-start | bytes 22020096 | tf_op jit(solution)/shard_map/all_gather | solution.py:310
  13.4 56.2 %all-to-all-start = ((bf16[32,8,7168]{2,1,0:T(8,128)(2,1)}), bf16[32,8,7168]{2,1,0:T(8,128)(2,1)}, u32[]{:S(2)}, u32[]{:S(2)}) async-start(bf16[32,8,7168]{2,1,0:T(8,128)(2,1)} %bitcast.11), calls=%async_computation | async-start | bytes 7340032 | tf_op jit(solution)/shard_map/all_to_all | solution.py:299
  69.6 66.8 %all-to-all-start.2 = ((bf16[32,8,7168]{2,1,0:T(8,128)(2,1)}), bf16[32,8,7168]{2,1,0:T(8,128)(2,1)}, u32[]{:S(2)}, u32[]{:S(2)}) async-start(bf16[32,8,7168]{2,1,0:T(8,128)(2,1)} %bitcast.10), calls=%async_computation.2 | async-start | bytes 7340032 | tf_op jit(solution)/shard_map/all_to_all | solution.py:299
  136.4 55.2 %all-to-all-start.1 = ((bf16[32,8,7168]{2,1,0:T(8,128)(2,1)}), bf16[32,8,7168]{2,1,0:T(8,128)(2,1)}, u32[]{:S(2)}, u32[]{:S(2)}) async-start(bf16[32,8,7168]{2,1,0:T(8,128)(2,1)} %bitcast.12), calls=%async_computation.1 | async-start | bytes 7340032 | tf_op jit(solution)/shard_map/all_to_all | solution.py:299
  191.6 52.5 %all-to-all-start.3 = ((bf16[32,8,7168]{2,1,0:T(8,128)(2,1)}), bf16[32,8,7168]{2,1,0:T(8,128)(2,1)}, u32[]{:S(2)}, u32[]{:S(2)}) async-start(bf16[32,8,7168]{2,1,0:T(8,128)(2,1)} %bitcast.13), calls=%async_computation.3 | async-start | bytes 7340032 | tf_op jit(solution)/shard_map/all_to_all | solution.py:299
Sparse Core Ops, SparseCore 0:
  9.0 32.1 all-gather.3
  42.9 31.0 all-gather.5
  75.7 31.0 all-gather.7

commit v6 on v5

--- a/solution.py
+++ b/solution.py
@@ -112,28 +112,10 @@
     )(turned_ids, tokens)
 
 
-def expert_kernel(
-    steps,
-    x_ref,
-    g0,
-    g1,
-    u0,
-    u1,
-    d0,
-    d1,
-    out_ref,
-    gate0,
-    gate1,
-    up0,
-    up1,
-    hid0,
-    hid1,
-    gather,
-    spread,
-    spread3,
-):
+def hidden_kernel(x_ref, g0, g1, u0, u1, out_ref, gate0, gate1, up0, up1, gather, spread, spread3):
     step = pl.program_id(0)
     pairs = ((gate0, g0), (gate1, g1), (up0, u0), (up1, u1))
+    half = gate0.shape[1]
 
     @pl.when(step == 0)
     def _():
@@ -145,63 +127,81 @@
         for j in range(3):
             spread3[j * blocks : (j + 1) * blocks, :] = spread[...]
 
-    @pl.when(step < steps)
+    x = restored_rows(x_ref[...], gather[...], spread[...], spread3[...])
+    for total, w in pairs:
+        total[...] += times(x, w[...])
+
+    @pl.when(step == pl.num_programs(0) - 1)
     def _():
-        x = restored_rows(x_ref[...], gather[...], spread[...], spread3[...])
-        for total, w in pairs:
-            total[...] += jnp.dot(x, w[...], preferred_element_type=jnp.float32)
-
-    @pl.when(step == steps - 1)
-    def _():
-        for hid, gate, up in ((hid0, gate0, up0), (hid1, gate1, up1)):
+        for at, gate, up in ((0, gate0, up0), (half, gate1, up1)):
             v = gate[...]
-            hid[...] = (v / (1.0 + jnp.exp(-v)) * up[...]).astype(jnp.bfloat16)
-
-    @pl.when(step >= steps)
-    def _():
-        out_ref[...] = (
-            jnp.dot(hid0[...], d0[...], preferred_element_type=jnp.float32)
-            + jnp.dot(hid1[...], d1[...], preferred_element_type=jnp.float32)
-        ).astype(jnp.bfloat16)
-
-
-def expert(rows, gates, ups, downs):
+            out_ref[:, at : at + half] = (v / (1.0 + jnp.exp(-v)) * up[...]).astype(jnp.bfloat16)
+
+
+def hidden_units(rows, gates, ups):
     count, width = rows.shape
     half = gates.shape[-1]
     wide = 1024
-    steps = width // wide
-    first = lambda s: jnp.minimum(s, steps - 1)
-    second = lambda s: jnp.maximum(s - steps, 0)
-    into = [pl.BlockSpec((None, wide, half), lambda s, c=c: (c, first(s), 0)) for c in range(2)]
-    out_of = [pl.BlockSpec((None, half, wide), lambda s, c=c: (c, 0, second(s))) for c in range(2)]
-    return pl.pallas_call(
-        functools.partial(expert_kernel, steps),
-        name="expert_rows",
-        out_shape=jax.ShapeDtypeStruct((count, width), jnp.bfloat16),
-        grid=(2 * steps,),
-        in_specs=[pl.BlockSpec((count, wide), lambda s: (0, first(s)))] + into * 2 + out_of,
-        out_specs=pl.BlockSpec((count, wide), lambda s: (0, second(s))),
+    blocks = wide // BLOCK
+    into = [pl.BlockSpec((None, wide, half), lambda s, c=c: (c, s, 0)) for c in range(2)]
+    return pl.pallas_call(
+        hidden_kernel,
+        name="hidden_units",
+        out_shape=jax.ShapeDtypeStruct((count, 2 * half), jnp.bfloat16),
+        grid=(width // wide,),
+        in_specs=[pl.BlockSpec((count, wide), lambda s: (0, s))] + into * 2,
+        out_specs=pl.BlockSpec((count, 2 * half), lambda s: (0, 0)),
         scratch_shapes=[pltpu.VMEM((count, half), jnp.float32)] * 4
-        + [pltpu.VMEM((count, half), jnp.bfloat16)] * 2
         + [
-            pltpu.VMEM((wide, wide // BLOCK), jnp.bfloat16),
-            pltpu.VMEM((wide // BLOCK, wide), jnp.bfloat16),
-            pltpu.VMEM((3 * wide // BLOCK, wide), jnp.bfloat16),
+            pltpu.VMEM((wide, blocks), jnp.bfloat16),
+            pltpu.VMEM((blocks, wide), jnp.bfloat16),
+            pltpu.VMEM((3 * blocks, wide), jnp.bfloat16),
         ],
         compiler_params=pltpu.CompilerParams(
             dimension_semantics=("arbitrary",), vmem_limit_bytes=VMEM_BYTES
         ),
         cost_estimate=pl.CostEstimate(
-            flops=count * width * half * 12,
+            flops=count * width * half * 8,
             transcendentals=count * half * 2,
-            bytes_accessed=width * half * 12 + count * width * 4,
-        ),
-    )(rows, gates, gates, ups, ups, downs, downs)
-
-
-def table_kernel(experts, chunks, ids_ref, affinity_ref, out_ref):
+            bytes_accessed=width * half * 8 + count * width * 2,
+        ),
+    )(rows, gates, gates, ups, ups)
+
+
+def down_kernel(hidden_ref, d0, d1, out_ref):
+    half = d0.shape[0]
+    hidden = hidden_ref[...]
+    out_ref[...] = (times(hidden[:, :half], d0[...]) + times(hidden[:, half:], d1[...])).astype(
+        jnp.bfloat16
+    )
+
+
+def down_rows(hidden, downs):
+    count = hidden.shape[0]
+    _, half, width = downs.shape
+    wide = 1024
+    out_of = [pl.BlockSpec((None, half, wide), lambda s, c=c: (c, 0, s)) for c in range(2)]
+    return pl.pallas_call(
+        down_kernel,
+        name="down_rows",
+        out_shape=jax.ShapeDtypeStruct((count, width), jnp.bfloat16),
+        grid=(width // wide,),
+        in_specs=[pl.BlockSpec(hidden.shape, lambda s: (0, 0))] + out_of,
+        out_specs=pl.BlockSpec((count, wide), lambda s: (0, s)),
+        compiler_params=pltpu.CompilerParams(
+            dimension_semantics=("arbitrary",), vmem_limit_bytes=VMEM_BYTES
+        ),
+        cost_estimate=pl.CostEstimate(
+            flops=count * width * half * 4,
+            transcendentals=0,
+            bytes_accessed=width * half * 4 + count * width * 2,
+        ),
+    )(hidden, downs, downs)
+
+
+def table_kernel(experts, chunks, ids_ref, affinity_ref, *out_refs):
     count = ids_ref.shape[1]
-    rows = out_ref.shape[2]
+    rows = out_refs[0].shape[1]
     each = rows // experts
     key = slot_keys(ids_ref, experts)
     total = affinity_ref[0:1, :]
@@ -226,8 +226,8 @@
     place = (iota((count, rows), 1) % each).astype(jnp.float32)
     for j in range(chunks):
         hit = wide == place + float(each * j)
-        out_ref[j, 0:count, :] = jnp.where(hit, upper, 0.0).astype(jnp.bfloat16)
-        out_ref[j, count : 2 * count, :] = jnp.where(hit, lower, 0.0).astype(jnp.bfloat16)
+        out_refs[j][0:count, :] = jnp.where(hit, upper, 0.0).astype(jnp.bfloat16)
+        out_refs[j][count : 2 * count, :] = jnp.where(hit, lower, 0.0).astype(jnp.bfloat16)
 
 
 def weights_of_slots(turned_ids, turned_affinity, experts, slots, chunks):
@@ -236,61 +236,62 @@
     return pl.pallas_call(
         functools.partial(table_kernel, experts, chunks),
         name="slot_weights",
-        out_shape=jax.ShapeDtypeStruct((chunks, 2 * count, rows), jnp.bfloat16),
+        out_shape=[jax.ShapeDtypeStruct((2 * count, rows), jnp.bfloat16)] * chunks,
     )(turned_ids, turned_affinity)
 
 
-def mix_kernel(chunks, table_ref, *rest):
-    in_refs, out_ref = rest[:chunks], rest[chunks]
-    values, mixed, got, put = rest[chunks + 1 :]
+def mix_kernel(table_ref, in_ref, *rest):
+    known_refs, out_ref = rest[:-5], rest[-5]
+    values, mixed, got, put = rest[-4:]
     count, width = mixed.shape
-    rows = values.shape[1]
     pieces = put.shape[0]
     wide = width // pieces
 
-    def loaded(j, i):
-        part = (slice(None), pl.ds(i * wide, wide))
-        return pltpu.make_async_copy(in_refs[j].at[part], values.at[j].at[part], got.at[j, i])
+    def part(i):
+        return (slice(None), pl.ds(i * wide, wide))
+
+    def loaded(i):
+        return pltpu.make_async_copy(in_ref.at[part(i)], values.at[part(i)], got.at[i])
 
     def stored(i):
-        part = (slice(None), pl.ds(i * wide, wide))
-        return pltpu.make_async_copy(mixed.at[part], out_ref.at[part], put.at[i])
-
-    for i in range(pieces):
-        for j in range(chunks):
-            loaded(j, i).start()
-    for i in range(pieces):
-        total = None
-        for j in range(chunks):
-            loaded(j, i).wait()
-            part = times(table_ref[j], values[j, :, i * wide : (i + 1) * wide])
-            total = part if total is None else total + part
-        total = total[:count] + total[count:]
-        mixed[:, i * wide : (i + 1) * wide] = total.astype(jnp.bfloat16)
+        return pltpu.make_async_copy(mixed.at[part(i)], out_ref.at[part(i)], put.at[i])
+
+    for i in range(pieces):
+        loaded(i).start()
+    for i in range(pieces):
+        loaded(i).wait()
+        both = times(table_ref[...], values[:, i * wide : (i + 1) * wide])
+        total = both[:count] + both[count:]
+        for known in known_refs:
+            total = total + known[:, i * wide : (i + 1) * wide]
+        mixed[:, i * wide : (i + 1) * wide] = total.astype(mixed.dtype)
         stored(i).start()
     for i in range(pieces):
         stored(i).wait()
 
 
-def mix(table, parts):
-    chunks, count, rows = table.shape
-    count //= 2
-    width = parts[0].shape[1]
+def mix(table, rows, known, dtype):
+    count = table.shape[0] // 2
+    slots, width = rows.shape
     anywhere = pl.BlockSpec(memory_space=pl.ANY)
-    return pl.pallas_call(
-        functools.partial(mix_kernel, chunks),
+    vmem = pl.BlockSpec(memory_space=pltpu.VMEM)
+    return pl.pallas_call(
+        mix_kernel,
         name="mix_slots",
-        out_shape=jax.ShapeDtypeStruct((count, width), jnp.bfloat16),
-        in_specs=[pl.BlockSpec(memory_space=pltpu.VMEM)] + [anywhere] * chunks,
+        out_shape=jax.ShapeDtypeStruct((count, width), dtype),
+        in_specs=[vmem, anywhere] + [vmem] * len(known),
         out_specs=anywhere,
         scratch_shapes=[
-            pltpu.VMEM((chunks, rows, width), jnp.bfloat16),
-            pltpu.VMEM((count, width), jnp.bfloat16),
-            pltpu.SemaphoreType.DMA((chunks, PIECES)),
+            pltpu.VMEM((slots, width), jnp.bfloat16),
+            pltpu.VMEM((count, width), dtype),
+            pltpu.SemaphoreType.DMA((PIECES,)),
             pltpu.SemaphoreType.DMA((PIECES,)),
         ],
         compiler_params=pltpu.CompilerParams(vmem_limit_bytes=VMEM_BYTES),
-    )(table, *parts)
+        cost_estimate=pl.CostEstimate(
+            flops=4 * count * slots * width, transcendentals=0, bytes_accessed=2 * slots * width
+        ),
+    )(table, rows, *known)
 
 
 def exchange(rows, devices):
@@ -315,8 +316,12 @@
     parts = []
     for chunk in range(CHUNKS):
         rows = exchange(slots_of_tokens(tokens, turned_ids, experts, slots, chunk), devices)
-        parts.append(exchange(expert(rows, gates, ups, downs), devices))
-    return mix(table, parts)
+        computed = down_rows(hidden_units(rows, gates, ups), downs)
+        parts.append(exchange(computed, devices))
+    known = []
+    for chunk in range(CHUNKS - 1):
+        known = [mix(table[chunk], parts[chunk], known, jnp.float32)]
+    return mix(table[CHUNKS - 1], parts[CHUNKS - 1], known, jnp.bfloat16)
 
 
 def solution(mesh):

time: 258 us -> 241 us (0.934)
  waiting for transfers between devices: 141 us -> 116 us
  Pallas kernels: 76.9 us -> 87.4 us
  starting transfers between devices: 25.8 us -> 23.1 us
    all_gather x3, waiting for transfers between devices: 32.3 us -> 10.4 us  [on_device(): lax.all_gather(w, 'ep', axis_index_groups=mates, axis=0, tiled=True)]
    pallas_call x3 -> x6, Pallas kernels: 65.6 us -> 76.2 us  [the longest x2 42 us: hidden_units(): pl.pallas_call(hidden_kernel, name='hidden_units', out_shape=jax.ShapeDty...]
    all_to_all x4, waiting for transfers between devices: 107 us -> 104 us  [exchange(): lax.all_to_all(split, 'ep', split_axis=0, concat_axis=0, tiled=True)]
    all_to_all x4, starting transfers between devices: 25.7 us -> 23.1 us  [exchange(): lax.all_to_all(split, 'ep', split_axis=0, concat_axis=0, tiled=True)]
  transfers between devices with their start and end apart: 7 -> 7, of which waited for: 4 -> 5; matrix products, arithmetic and copies ran while one was open for 0% -> 0% of each run, Pallas kernels for 27% -> 34%
where the time goes in v6:
time: 241 us; the launch traced here: 240 us
  waiting for transfers between devices  116 us (48%)
  Pallas kernels  87.4 us (36%)
  starting transfers between devices  23.1 us (10%)
  between operations  13.2 us (5%)
    all_to_all x4, waiting for transfers between devices, exchange(): lax.all_to_all(split, 'ep', split_axis=0, concat_axis=0, tiled=True)  104 us
    pallas_call x2, Pallas kernels, hidden_units(): pl.pallas_call(hidden_kernel, name='hidden_units', out_shape=jax.ShapeDty...  42 us
    all_to_all x4, starting transfers between devices, exchange(): lax.all_to_all(split, 'ep', split_axis=0, concat_axis=0, tiled=True)  23.1 us
    pallas_call x2, Pallas kernels, down_rows(): pl.pallas_call(down_kernel, name='down_rows', out_shape=jax.ShapeDtypeStr...  23.1 us
    pallas_call x2, Pallas kernels, mix(): pl.pallas_call(mix_kernel, name='mix_slots', out_shape=jax.ShapeDtypeStru...  11.1 us
    all_gather x3, waiting for transfers between devices, on_device(): lax.all_gather(w, 'ep', axis_index_groups=mates, axis=0, tiled=True)  10.4 us
    pallas_call x2, Pallas kernels, slots_of_tokens(): pl.pallas_call(functools.partial(pick_kernel, experts, chunk), name='pick...  9.3 us
  transfers between devices with their start and end apart: 7, of which 5 were waited for; matrix products, arithmetic and copies ran while one was open for 0% of the time, Pallas kernels for 34%

profile of v6, /device:TPU:0, one launch (start us, length us, event | category | flops | bytes accessed | tf_op | source)
XLA Modules:
  0.0 239.8 jit_solution(3755961878089253700)
XLA Ops:
  6.5 0.7 all-gather.4.cloned.1.call-update
  7.3 0.0 all-gather.6.cloned.1.call-start
  7.3 0.7 all-gather.6.cloned.1.call-update
  8.0 0.0 all-gather.8.cloned.1.call-start
  8.1 0.7 all-gather.8.cloned.1.call-update
  8.7 4.6 %pick_slots.3 = bf16[256,7168]{1,0:T(8,128)(2,1)} custom-call(s32[2,128]{1,0:T(2,128)} %bitcast.14, bf16[128,7168]{1,0:T(8,128)(2,1)} %tokens_ref.3), custom_call_target="tpu_custom_call" | custom-call | tf_op jit(solution)/shard_map/pick_slots/pallas_call | solution.py:98
  13.4 8.5 %all-to-all-start.2 = ((bf16[32,8,7168]{2,1,0:T(8,128)(2,1)}), bf16[32,8,7168]{2,1,0:T(8,128)(2,1)}, u32[]{:S(2)}, u32[]{:S(2)}) async-start(bf16[32,8,7168]{2,1,0:T(8,128)(2,1)} %bitcast.11), calls=%async_computation.2 | async-start | bytes 7340032 | tf_op jit(solution)/shard_map/all_to_all | solution.py:300
  21.9 4.7 %pick_slots.2 = bf16[256,7168]{1,0:T(8,128)(2,1)} custom-call(s32[2,128]{1,0:T(2,128)} %bitcast.15, bf16[128,7168]{1,0:T(8,128)(2,1)} %tokens_ref.3), custom_call_target="tpu_custom_call" | custom-call | tf_op jit(solution)/shard_map/pick_slots/pallas_call | solution.py:98
  26.6 43.0 %all-to-all-done.2 = bf16[32,8,7168]{2,1,0:T(8,128)(2,1)} async-done(((bf16[32,8,7168]{2,1,0:T(8,128)(2,1)}), bf16[32,8,7168]{2,1,0:T(8,128)(2,1)}, u32[]{:S(2)}, u32[]{:S(2)}) %all-to-all-start.2) | async-done | bytes 3670048 | tf_op jit(solution)/shard_map/all_to_all | solution.py:300
  69.6 4.8 %all-to-all-start = ((bf16[32,8,7168]{2,1,0:T(8,128)(2,1)}), bf16[32,8,7168]{2,1,0:T(8,128)(2,1)}, u32[]{:S(2)}, u32[]{:S(2)}) async-start(bf16[32,8,7168]{2,1,0:T(8,128)(2,1)} %bitcast.10), calls=%async_computation | async-start | bytes 7340032 | tf_op jit(solution)/shard_map/all_to_all | solution.py:300
  74.4 0.0 all-gather.4.cloned.1.call-done.g0.g1
  74.5 22.0 %hidden_units.3.hidden_ref = bf16[256,1024]{1,0:T(8,128)(2,1)} custom-call(bf16[256,7168]{1,0:T(8,128)(2,1)} %bitcast.7.x_ref, bf16[2,7168,512]{2,1,0:T(8,128)(2,1)} %all-gather.4.cloned.1.call-done.g0.g1, bf16[2,7168,512]{2,1,0:T(8,128)(2,1)} %all-gather.4.cloned.1.call-done.g0.g1, bf16[2,7168,512]{2,1,0:T(8,128)(2,1)} %all-gather.6.cloned.1.call-done.u0.u1, ...), custom_call_target="tpu_custom_call" | custom-call | flops 7516192768 | bytes 33030144 | tf_op jit(solution)/shard_map/hidden_units/pallas_call | solution.py:147
  96.4 10.3 %all-gather.8.cloned.1.call-done.d0.d1 = bf16[2,512,7168]{2,1,0:T(8,128)(2,1)} async-done(((bf16[1,512,7168]{2,1,0:T(8,128)(2,1)}), bf16[2,512,7168]{2,1,0:T(8,128)(2,1)}) %all-gather.8.cloned.1.call-update) | async-done | bytes 14680080 | tf_op jit(solution)/shard_map/all_gather | solution.py:311
  106.8 11.5 %down_rows.3 = bf16[256,7168]{1,0:T(8,128)(2,1)} custom-call(bf16[256,1024]{1,0:T(8,128)(2,1)} %hidden_units.3.hidden_ref, bf16[2,512,7168]{2,1,0:T(8,128)(2,1)} %all-gather.8.cloned.1.call-done.d0.d1, bf16[2,512,7168]{2,1,0:T(8,128)(2,1)} %all-gather.8.cloned.1.call-done.d0.d1), custom_call_target="tpu_custom_call" | custom-call | flops 3758096384 | bytes 18350080 | tf_op jit(solution)/shard_map/down_rows/pallas_call | solution.py:184
  118.3 3.8 %all-to-all-done = bf16[32,8,7168]{2,1,0:T(8,128)(2,1)} async-done(((bf16[32,8,7168]{2,1,0:T(8,128)(2,1)}), bf16[32,8,7168]{2,1,0:T(8,128)(2,1)}, u32[]{:S(2)}, u32[]{:S(2)}) %all-to-all-start) | async-done | bytes 3670048 | tf_op jit(solution)/shard_map/all_to_all | solution.py:300
  122.1 4.8 %all-to-all-start.3 = ((bf16[32,8,7168]{2,1,0:T(8,128)(2,1)}), bf16[32,8,7168]{2,1,0:T(8,128)(2,1)}, u32[]{:S(2)}, u32[]{:S(2)}) async-start(bf16[32,8,7168]{2,1,0:T(8,128)(2,1)} %bitcast.12), calls=%async_computation.3 | async-start | bytes 7340032 | tf_op jit(solution)/shard_map/all_to_all | solution.py:300
  127.0 20.0 %hidden_units.2.hidden_ref = bf16[256,1024]{1,0:T(8,128)(2,1)} custom-call(bf16[256,7168]{1,0:T(8,128)(2,1)} %bitcast.3.x_ref, bf16[2,7168,512]{2,1,0:T(8,128)(2,1)} %all-gather.4.cloned.1.call-done.g0.g1, bf16[2,7168,512]{2,1,0:T(8,128)(2,1)} %all-gather.4.cloned.1.call-done.g0.g1, bf16[2,7168,512]{2,1,0:T(8,128)(2,1)} %all-gather.6.cloned.1.call-done.u0.u1, ...), custom_call_target="tpu_custom_call" | custom-call | flops 7516192768 | bytes 33030144 | tf_op jit(solution)/shard_map/hidden_units/pallas_call | solution.py:147
  147.0 11.5 %down_rows.2 = bf16[256,7168]{1,0:T(8,128)(2,1)} custom-call(bf16[256,1024]{1,0:T(8,128)(2,1)} %hidden_units.2.hidden_ref, bf16[2,512,7168]{2,1,0:T(8,128)(2,1)} %all-gather.8.cloned.1.call-done.d0.d1, bf16[2,512,7168]{2,1,0:T(8,128)(2,1)} %all-gather.8.cloned.1.call-done.d0.d1), custom_call_target="tpu_custom_call" | custom-call | flops 3758096384 | bytes 18350080 | tf_op jit(solution)/shard_map/down_rows/pallas_call | solution.py:184
  158.5 16.1 %all-to-all-done.3 = bf16[32,8,7168]{2,1,0:T(8,128)(2,1)} async-done(((bf16[32,8,7168]{2,1,0:T(8,128)(2,1)}), bf16[32,8,7168]{2,1,0:T(8,128)(2,1)}, u32[]{:S(2)}, u32[]{:S(2)}) %all-to-all-start.3) | async-done | bytes 3670048 | tf_op jit(solution)/shard_map/all_to_all | solution.py:300
  174.6 4.8 %all-to-all-start.1 = ((bf16[32,8,7168]{2,1,0:T(8,128)(2,1)}), bf16[32,8,7168]{2,1,0:T(8,128)(2,1)}, u32[]{:S(2)}, u32[]{:S(2)}) async-start(bf16[32,8,7168]{2,1,0:T(8,128)(2,1)} %bitcast.13), calls=%async_computation.1 | async-start | bytes 7340032 | tf_op jit(solution)/shard_map/all_to_all | solution.py:300
  179.5 2.0 slot_weights.1
  181.4 5.0 %mix_slots.2.rest_0_ = f32[128,7168]{1,0:T(8,128)} custom-call(bf16[256,256]{1,0:T(8,128)(2,1)} %get-tuple-element.8.table_ref, bf16[256,7168]{1,0:T(8,128)(2,1)} %bitcast.9.in_ref), custom_call_target="tpu_custom_call" | custom-call | flops 939524096 | bytes 3670016 | tf_op jit(solution)/shard_map/mix_slots/pallas_call | solution.py:278
  186.4 40.7 %all-to-all-done.1 = bf16[32,8,7168]{2,1,0:T(8,128)(2,1)} async-done(((bf16[32,8,7168]{2,1,0:T(8,128)(2,1)}), bf16[32,8,7168]{2,1,0:T(8,128)(2,1)}, u32[]{:S(2)}, u32[]{:S(2)}) %all-to-all-start.1) | async-done | bytes 3670048 | tf_op jit(solution)/shard_map/all_to_all | solution.py:300
  227.1 6.1 %mix_slots.3 = bf16[128,7168]{1,0:T(8,128)(2,1)} custom-call(bf16[256,256]{1,0:T(8,128)(2,1)} %get-tuple-element.7.table_ref, bf16[256,7168]{1,0:T(8,128)(2,1)} %bitcast.5.in_ref, f32[128,7168]{1,0:T(8,128)} %mix_slots.2.rest_0_), custom_call_target="tpu_custom_call" | custom-call | flops 939524096 | bytes 3670016 | tf_op jit(solution)/shard_map/mix_slots/pallas_call | solution.py:278
  (2 shorter events, 0.0 us)
Async XLA Ops:
  6.5 67.9 %all-gather.4.cloned.1.call-start = ((), (), s32[]{:S(2)}) async-start(), calls=%async_computation.4 | async-start | bytes 22020096 | tf_op jit(solution)/shard_map/all_gather | solution.py:311
  7.3 67.2 %all-gather.6.cloned.1.call-start = ((), (), s32[]{:S(2)}) async-start(), calls=%async_computation.5 | async-start | bytes 22020096 | tf_op jit(solution)/shard_map/all_gather | solution.py:311
  8.0 98.8 %all-gather.8.cloned.1.call-start = ((), (), s32[]{:S(2)}) async-start(), calls=%async_computation.6 | async-start | bytes 22020096 | tf_op jit(solution)/shard_map/all_gather | solution.py:311
  13.4 56.2 %all-to-all-start.2 = ((bf16[32,8,7168]{2,1,0:T(8,128)(2,1)}), bf16[32,8,7168]{2,1,0:T(8,128)(2,1)}, u32[]{:S(2)}, u32[]{:S(2)}) async-start(bf16[32,8,7168]{2,1,0:T(8,128)(2,1)} %bitcast.11), calls=%async_computation.2 | async-start | bytes 7340032 | tf_op jit(solution)/shard_map/all_to_all | solution.py:300
  69.6 52.5 %all-to-all-start = ((bf16[32,8,7168]{2,1,0:T(8,128)(2,1)}), bf16[32,8,7168]{2,1,0:T(8,128)(2,1)}, u32[]{:S(2)}, u32[]{:S(2)}) async-start(bf16[32,8,7168]{2,1,0:T(8,128)(2,1)} %bitcast.10), calls=%async_computation | async-start | bytes 7340032 | tf_op jit(solution)/shard_map/all_to_all | solution.py:300
  122.1 52.5 %all-to-all-start.3 = ((bf16[32,8,7168]{2,1,0:T(8,128)(2,1)}), bf16[32,8,7168]{2,1,0:T(8,128)(2,1)}, u32[]{:S(2)}, u32[]{:S(2)}) async-start(bf16[32,8,7168]{2,1,0:T(8,128)(2,1)} %bitcast.12), calls=%async_computation.3 | async-start | bytes 7340032 | tf_op jit(solution)/shard_map/all_to_all | solution.py:300
  174.6 52.5 %all-to-all-start.1 = ((bf16[32,8,7168]{2,1,0:T(8,128)(2,1)}), bf16[32,8,7168]{2,1,0:T(8,128)(2,1)}, u32[]{:S(2)}, u32[]{:S(2)}) async-start(bf16[32,8,7168]{2,1,0:T(8,128)(2,1)} %bitcast.13), calls=%async_computation.1 | async-start | bytes 7340032 | tf_op jit(solution)/shard_map/all_to_all | solution.py:300
Sparse Core Ops, SparseCore 0:
  9.0 32.1 all-gather.3
  42.9 31.0 all-gather.5
  75.7 31.0 all-gather.7

commit v7 on v4

--- a/solution.py
+++ b/solution.py
@@ -199,9 +199,9 @@
     )(rows, *gates, *ups, *downs)
 
 
-def table_kernel(experts, chunks, ids_ref, affinity_ref, out_ref):
+def table_kernel(experts, chunks, ids_ref, affinity_ref, *out_refs):
     count = ids_ref.shape[1]
-    rows = out_ref.shape[2]
+    rows = out_refs[0].shape[1]
     each = rows // experts
     key = slot_keys(ids_ref, experts)
     total = affinity_ref[0:1, :]
@@ -226,8 +226,8 @@
     place = (iota((count, rows), 1) % each).astype(jnp.float32)
     for j in range(chunks):
         hit = wide == place + float(each * j)
-        out_ref[j, 0:count, :] = jnp.where(hit, upper, 0.0).astype(jnp.bfloat16)
-        out_ref[j, count : 2 * count, :] = jnp.where(hit, lower, 0.0).astype(jnp.bfloat16)
+        out_refs[j][0:count, :] = jnp.where(hit, upper, 0.0).astype(jnp.bfloat16)
+        out_refs[j][count : 2 * count, :] = jnp.where(hit, lower, 0.0).astype(jnp.bfloat16)
 
 
 def weights_of_slots(turned_ids, turned_affinity, experts, slots, chunks):
@@ -236,75 +236,70 @@
     return pl.pallas_call(
         functools.partial(table_kernel, experts, chunks),
         name="slot_weights",
-        out_shape=jax.ShapeDtypeStruct((chunks, 2 * count, rows), jnp.bfloat16),
+        out_shape=[jax.ShapeDtypeStruct((2 * count, rows), jnp.bfloat16)] * chunks,
     )(turned_ids, turned_affinity)
 
 
-def mix_kernel(chunks, table_ref, *rest):
-    in_refs, out_ref = rest[:chunks], rest[chunks]
-    values, mixed, got, put = rest[chunks + 1 :]
+def mix_kernel(table_ref, in_ref, *rest):
+    known_refs, out_ref = rest[:-5], rest[-5]
+    values, mixed, got, put = rest[-4:]
     count, width = mixed.shape
-    rows = values.shape[1]
     pieces = put.shape[0]
     wide = width // pieces
 
-    def loaded(j, i):
-        part = (slice(None), pl.ds(i * wide, wide))
-        return pltpu.make_async_copy(in_refs[j].at[part], values.at[j].at[part], got.at[j, i])
+    def part(i):
+        return (slice(None), pl.ds(i * wide, wide))
+
+    def loaded(i):
+        return pltpu.make_async_copy(in_ref.at[part(i)], values.at[part(i)], got.at[i])
 
     def stored(i):
-        part = (slice(None), pl.ds(i * wide, wide))
-        return pltpu.make_async_copy(mixed.at[part], out_ref.at[part], put.at[i])
-
-    for i in range(pieces):
-        for j in range(chunks):
-            loaded(j, i).start()
-    for i in range(pieces):
-        total = None
-        for j in range(chunks):
-            loaded(j, i).wait()
-            part = times(table_ref[j], values[j, :, i * wide : (i + 1) * wide])
-            total = part if total is None else total + part
-        total = total[:count] + total[count:]
-        mixed[:, i * wide : (i + 1) * wide] = total.astype(jnp.bfloat16)
+        return pltpu.make_async_copy(mixed.at[part(i)], out_ref.at[part(i)], put.at[i])
+
+    for i in range(pieces):
+        loaded(i).start()
+    for i in range(pieces):
+        loaded(i).wait()
+        both = times(table_ref[...], values[:, i * wide : (i + 1) * wide])
+        total = both[:count] + both[count:]
+        for known in known_refs:
+            total = total + known[:, i * wide : (i + 1) * wide]
+        mixed[:, i * wide : (i + 1) * wide] = total.astype(mixed.dtype)
         stored(i).start()
     for i in range(pieces):
         stored(i).wait()
 
 
-def mix(table, parts):
-    chunks, count, rows = table.shape
-    count //= 2
-    width = parts[0].shape[1]
+def mix(table, rows, known, dtype):
+    count = table.shape[0] // 2
+    slots, width = rows.shape
     anywhere = pl.BlockSpec(memory_space=pl.ANY)
+    vmem = pl.BlockSpec(memory_space=pltpu.VMEM)
     return pl.pallas_call(
-        functools.partial(mix_kernel, chunks),
+        mix_kernel,
         name="mix_slots",
-        out_shape=jax.ShapeDtypeStruct((count, width), jnp.bfloat16),
-        in_specs=[pl.BlockSpec(memory_space=pltpu.VMEM)] + [anywhere] * chunks,
+        out_shape=jax.ShapeDtypeStruct((count, width), dtype),
+        in_specs=[vmem, anywhere] + [vmem] * len(known),
         out_specs=anywhere,
         scratch_shapes=[
-            pltpu.VMEM((chunks, rows, width), jnp.bfloat16),
-            pltpu.VMEM((count, width), jnp.bfloat16),
-            pltpu.SemaphoreType.DMA((chunks, PIECES)),
+            pltpu.VMEM((slots, width), jnp.bfloat16),
+            pltpu.VMEM((count, width), dtype),
+            pltpu.SemaphoreType.DMA((PIECES,)),
             pltpu.SemaphoreType.DMA((PIECES,)),
         ],
         compiler_params=pltpu.CompilerParams(vmem_limit_bytes=VMEM_BYTES),
-    )(table, *parts)
+        cost_estimate=pl.CostEstimate(
+            flops=4 * count * slots * width, transcendentals=0, bytes_accessed=2 * slots * width
+        ),
+    )(table, rows, *known)
 
 
 def exchange(rows, devices):
     count, width = rows.shape
-    chips = devices // 2
-    groups = [list(range(core, devices, 2)) for core in range(2)]
-    return lax.all_to_all(
-        rows.reshape(chips, count // chips, width),
-        "ep",
-        split_axis=0,
-        concat_axis=0,
-        axis_index_groups=groups,
-        tiled=True,
-    ).reshape(count, width)
+    split = rows.reshape(devices, count // devices, width)
+    return lax.all_to_all(split, "ep", split_axis=0, concat_axis=0, tiled=True).reshape(
+        count, width
+    )
 
 
 def on_device(tokens, expert_ids, affinity, w_gate, w_up, w_down):
@@ -319,7 +314,10 @@
     for chunk in range(CHUNKS):
         rows = exchange(slots_of_tokens(tokens, turned_ids, experts, slots, chunk), devices)
         parts.append(exchange(expert(rows, gates, ups, downs), devices))
-    return mix(table, parts)
+    known = []
+    for chunk in range(CHUNKS - 1):
+        known = [mix(table[chunk], parts[chunk], known, jnp.float32)]
+    return mix(table[CHUNKS - 1], parts[CHUNKS - 1], known, jnp.bfloat16)
 
 
 def solution(mesh):

time: 245 us -> 226 us (0.922)
  waiting for transfers between devices: 145 us -> 120 us
  Pallas kernels: 76.7 us -> 81.5 us
    all_to_all x4, waiting for transfers between devices: 145 us -> 120 us  [exchange(): lax.all_to_all(split, 'ep', split_axis=0, concat_axis=0, tiled=True)]
    pallas_call x1 -> x2, Pallas kernels: 6.37 us -> 11.1 us  [mix(): pl.pallas_call(mix_kernel, name='mix_slots', out_shape=jax.ShapeDtypeStru...]
  transfers between devices with their start and end apart: 7 -> 7, of which waited for: 4 -> 4; matrix products, arithmetic and copies ran while one was open for 0% -> 0% of each run, Pallas kernels for 29% -> 33%
where the time goes in v7:
time: 226 us; the launch traced here: 225 us
  waiting for transfers between devices  120 us (53%)
  Pallas kernels  81.5 us (36%)
  starting transfers between devices  23.7 us (10%)
    all_to_all x4, waiting for transfers between devices, exchange(): lax.all_to_all(split, 'ep', split_axis=0, concat_axis=0, tiled=True)  120 us
    pallas_call x2, Pallas kernels, expert(): pl.pallas_call(functools.partial(expert_kernel, steps), name='expert_rows...  59.3 us
    all_to_all x4, starting transfers between devices, exchange(): lax.all_to_all(split, 'ep', split_axis=0, concat_axis=0, tiled=True)  23.2 us
    pallas_call x2, Pallas kernels, mix(): pl.pallas_call(mix_kernel, name='mix_slots', out_shape=jax.ShapeDtypeStru...  11.1 us
    pallas_call x2, Pallas kernels, slots_of_tokens(): pl.pallas_call(functools.partial(pick_kernel, experts, chunk), name='pick...  9.16 us
  transfers between devices with their start and end apart: 7, of which 4 were waited for; matrix products, arithmetic and copies ran while one was open for 0% of the time, Pallas kernels for 33%

profile of v7, /device:TPU:0, one launch (start us, length us, event | category | flops | bytes accessed | tf_op | source)
XLA Modules:
  0.0 225.1 jit_solution(395953712703254800)
XLA Ops:
  0.0 0.0 collective-permute-start
  0.0 0.5 collective-permute-start.1
  0.5 0.0 collective-permute-start.2
  0.5 4.6 %pick_slots.3 = bf16[256,7168]{1,0:T(8,128)(2,1)} custom-call(s32[2,128]{1,0:T(2,128)} %bitcast.14, bf16[128,7168]{1,0:T(8,128)(2,1)} %tokens_ref.3), custom_call_target="tpu_custom_call" | custom-call | tf_op jit(solution)/shard_map/pick_slots/pallas_call | solution.py:98
  5.1 8.7 %all-to-all-start.2 = ((bf16[32,8,7168]{2,1,0:T(8,128)(2,1)}), bf16[32,8,7168]{2,1,0:T(8,128)(2,1)}, u32[]{:S(2)}, u32[]{:S(2)}) async-start(bf16[32,8,7168]{2,1,0:T(8,128)(2,1)} %bitcast.13), calls=%async_computation.2 | async-start | bytes 7340032 | tf_op jit(solution)/shard_map/all_to_all | solution.py:300
  13.8 4.6 %pick_slots.2 = bf16[256,7168]{1,0:T(8,128)(2,1)} custom-call(s32[2,128]{1,0:T(2,128)} %bitcast.15, bf16[128,7168]{1,0:T(8,128)(2,1)} %tokens_ref.3), custom_call_target="tpu_custom_call" | custom-call | tf_op jit(solution)/shard_map/pick_slots/pallas_call | solution.py:98
  18.4 43.1 %all-to-all-done.2 = bf16[32,8,7168]{2,1,0:T(8,128)(2,1)} async-done(((bf16[32,8,7168]{2,1,0:T(8,128)(2,1)}), bf16[32,8,7168]{2,1,0:T(8,128)(2,1)}, u32[]{:S(2)}, u32[]{:S(2)}) %all-to-all-start.2) | async-done | bytes 3670048 | tf_op jit(solution)/shard_map/all_to_all | solution.py:300
  61.5 4.8 %all-to-all-start = ((bf16[32,8,7168]{2,1,0:T(8,128)(2,1)}), bf16[32,8,7168]{2,1,0:T(8,128)(2,1)}, u32[]{:S(2)}, u32[]{:S(2)}) async-start(bf16[32,8,7168]{2,1,0:T(8,128)(2,1)} %bitcast.12), calls=%async_computation | async-start | bytes 7340032 | tf_op jit(solution)/shard_map/all_to_all | solution.py:300
  66.3 0.0 collective-permute-done.g1
  66.3 0.0 collective-permute-done.1.u1
  66.3 0.0 collective-permute-done.2.d1
  66.3 29.6 %expert_rows.3 = bf16[256,7168]{1,0:T(8,128)(2,1)} custom-call(bf16[256,7168]{1,0:T(8,128)(2,1)} %bitcast.7.x_ref, bf16[1,7168,512]{2,1,0:T(8,128)(2,1)} %g0.3, bf16[1,7168,512]{2,1,0:T(8,128)(2,1)} %collective-permute-done.g1, bf16[1,7168,512]{2,1,0:T(8,128)(2,1)} %u0.3, bf16[1,7168,512]{2,1,0:T(8,128)(2,1)} %collective-permute-done.1.u1, ...), custom_call_target="tpu_custom_call" | custom-call | flops 11274289152 | bytes 51380224 | tf_op jit(solution)/shard_map/expert_rows/pallas_call | solution.py:177
  96.0 18.0 %all-to-all-done = bf16[32,8,7168]{2,1,0:T(8,128)(2,1)} async-done(((bf16[32,8,7168]{2,1,0:T(8,128)(2,1)}), bf16[32,8,7168]{2,1,0:T(8,128)(2,1)}, u32[]{:S(2)}, u32[]{:S(2)}) %all-to-all-start) | async-done | bytes 3670048 | tf_op jit(solution)/shard_map/all_to_all | solution.py:300
  114.0 4.8 %all-to-all-start.3 = ((bf16[32,8,7168]{2,1,0:T(8,128)(2,1)}), bf16[32,8,7168]{2,1,0:T(8,128)(2,1)}, u32[]{:S(2)}, u32[]{:S(2)}) async-start(bf16[32,8,7168]{2,1,0:T(8,128)(2,1)} %bitcast.11), calls=%async_computation.3 | async-start | bytes 7340032 | tf_op jit(solution)/shard_map/all_to_all | solution.py:300
  118.8 29.6 %expert_rows.2 = bf16[256,7168]{1,0:T(8,128)(2,1)} custom-call(bf16[256,7168]{1,0:T(8,128)(2,1)} %bitcast.3.x_ref, bf16[1,7168,512]{2,1,0:T(8,128)(2,1)} %g0.3, bf16[1,7168,512]{2,1,0:T(8,128)(2,1)} %collective-permute-done.g1, bf16[1,7168,512]{2,1,0:T(8,128)(2,1)} %u0.3, bf16[1,7168,512]{2,1,0:T(8,128)(2,1)} %collective-permute-done.1.u1, ...), custom_call_target="tpu_custom_call" | custom-call | flops 11274289152 | bytes 51380224 | tf_op jit(solution)/shard_map/expert_rows/pallas_call | solution.py:177
  148.5 18.0 %all-to-all-done.3 = bf16[32,8,7168]{2,1,0:T(8,128)(2,1)} async-done(((bf16[32,8,7168]{2,1,0:T(8,128)(2,1)}), bf16[32,8,7168]{2,1,0:T(8,128)(2,1)}, u32[]{:S(2)}, u32[]{:S(2)}) %all-to-all-start.3) | async-done | bytes 3670048 | tf_op jit(solution)/shard_map/all_to_all | solution.py:300
  166.5 4.8 %all-to-all-start.1 = ((bf16[32,8,7168]{2,1,0:T(8,128)(2,1)}), bf16[32,8,7168]{2,1,0:T(8,128)(2,1)}, u32[]{:S(2)}, u32[]{:S(2)}) async-start(bf16[32,8,7168]{2,1,0:T(8,128)(2,1)} %bitcast.10), calls=%async_computation.1 | async-start | bytes 7340032 | tf_op jit(solution)/shard_map/all_to_all | solution.py:300
  171.3 1.9 slot_weights.1
  173.3 5.0 %mix_slots.2.rest_0_ = f32[128,7168]{1,0:T(8,128)} custom-call(bf16[256,256]{1,0:T(8,128)(2,1)} %get-tuple-element.8.table_ref, bf16[256,7168]{1,0:T(8,128)(2,1)} %bitcast.9.in_ref), custom_call_target="tpu_custom_call" | custom-call | flops 939524096 | bytes 3670016 | tf_op jit(solution)/shard_map/mix_slots/pallas_call | solution.py:278
  178.2 40.7 %all-to-all-done.1 = bf16[32,8,7168]{2,1,0:T(8,128)(2,1)} async-done(((bf16[32,8,7168]{2,1,0:T(8,128)(2,1)}), bf16[32,8,7168]{2,1,0:T(8,128)(2,1)}, u32[]{:S(2)}, u32[]{:S(2)}) %all-to-all-start.1) | async-done | bytes 3670048 | tf_op jit(solution)/shard_map/all_to_all | solution.py:300
  219.0 6.1 %mix_slots.3 = bf16[128,7168]{1,0:T(8,128)(2,1)} custom-call(bf16[256,256]{1,0:T(8,128)(2,1)} %get-tuple-element.7.table_ref, bf16[256,7168]{1,0:T(8,128)(2,1)} %bitcast.5.in_ref, f32[128,7168]{1,0:T(8,128)} %mix_slots.2.rest_0_), custom_call_target="tpu_custom_call" | custom-call | flops 939524096 | bytes 3670016 | tf_op jit(solution)/shard_map/mix_slots/pallas_call | solution.py:278
Async XLA Ops:
  0.0 66.3 %collective-permute-start = (bf16[1,7168,512]{2,1,0:T(8,128)(2,1)}, bf16[1,7168,512]{2,1,0:T(8,128)(2,1)}, u32[]{:S(2)}, u32[]{:S(2)}) collective-permute-start(bf16[1,7168,512]{2,1,0:T(8,128)(2,1)} %g0.3), channel_id=1, source_target_pairs={{0,4},{4,0},{8,12},{12,8},{16,20},{20,16},{24,28},{28,24},{32,36},... | collective-permute-start | bytes 22020104 | tf_op jit(solution)/shard_map/ppermute | solution.py:310
  0.0 66.3 %collective-permute-start.1 = (bf16[1,7168,512]{2,1,0:T(8,128)(2,1)}, bf16[1,7168,512]{2,1,0:T(8,128)(2,1)}, u32[]{:S(2)}, u32[]{:S(2)}) collective-permute-start(bf16[1,7168,512]{2,1,0:T(8,128)(2,1)} %u0.3), channel_id=1, source_target_pairs={{0,4},{4,0},{8,12},{12,8},{16,20},{20,16},{24,28},{28,24},{32,36},... | collective-permute-start | bytes 22020104 | tf_op jit(solution)/shard_map/ppermute | solution.py:310
  0.5 65.8 %collective-permute-start.2 = (bf16[1,512,7168]{2,1,0:T(8,128)(2,1)}, bf16[1,512,7168]{2,1,0:T(8,128)(2,1)}, u32[]{:S(2)}, u32[]{:S(2)}) collective-permute-start(bf16[1,512,7168]{2,1,0:T(8,128)(2,1)} %d0.3), channel_id=1, source_target_pairs={{0,4},{4,0},{8,12},{12,8},{16,20},{20,16},{24,28},{28,24},{32,36},... | collective-permute-start | bytes 22020104 | tf_op jit(solution)/shard_map/ppermute | solution.py:310
  5.1 56.3 %all-to-all-start.2 = ((bf16[32,8,7168]{2,1,0:T(8,128)(2,1)}), bf16[32,8,7168]{2,1,0:T(8,128)(2,1)}, u32[]{:S(2)}, u32[]{:S(2)}) async-start(bf16[32,8,7168]{2,1,0:T(8,128)(2,1)} %bitcast.13), calls=%async_computation.2 | async-start | bytes 7340032 | tf_op jit(solution)/shard_map/all_to_all | solution.py:300
  61.5 52.5 %all-to-all-start = ((bf16[32,8,7168]{2,1,0:T(8,128)(2,1)}), bf16[32,8,7168]{2,1,0:T(8,128)(2,1)}, u32[]{:S(2)}, u32[]{:S(2)}) async-start(bf16[32,8,7168]{2,1,0:T(8,128)(2,1)} %bitcast.12), calls=%async_computation | async-start | bytes 7340032 | tf_op jit(solution)/shard_map/all_to_all | solution.py:300
  114.0 52.5 %all-to-all-start.3 = ((bf16[32,8,7168]{2,1,0:T(8,128)(2,1)}), bf16[32,8,7168]{2,1,0:T(8,128)(2,1)}, u32[]{:S(2)}, u32[]{:S(2)}) async-start(bf16[32,8,7168]{2,1,0:T(8,128)(2,1)} %bitcast.11), calls=%async_computation.3 | async-start | bytes 7340032 | tf_op jit(solution)/shard_map/all_to_all | solution.py:300
  166.5 52.5 %all-to-all-start.1 = ((bf16[32,8,7168]{2,1,0:T(8,128)(2,1)}), bf16[32,8,7168]{2,1,0:T(8,128)(2,1)}, u32[]{:S(2)}, u32[]{:S(2)}) async-start(bf16[32,8,7168]{2,1,0:T(8,128)(2,1)} %bitcast.10), calls=%async_computation.1 | async-start | bytes 7340032 | tf_op jit(solution)/shard_map/all_to_all | solution.py:300

commit v8 on v7

--- a/solution.py
+++ b/solution.py
@@ -241,8 +241,8 @@
 
 
 def mix_kernel(table_ref, in_ref, *rest):
-    known_refs, out_ref = rest[:-5], rest[-5]
-    values, mixed, got, put = rest[-4:]
+    known_refs, out_ref = rest[:-7], rest[-7]
+    values, mixed, known, got, put, held = rest[-6:]
     count, width = mixed.shape
     pieces = put.shape[0]
     wide = width // pieces
@@ -256,21 +256,27 @@
     def stored(i):
         return pltpu.make_async_copy(mixed.at[part(i)], out_ref.at[part(i)], put.at[i])
 
+    def kept(i):
+        return pltpu.make_async_copy(known_refs[0].at[part(i)], known.at[part(i)], held.at[i])
+
     for i in range(pieces):
         loaded(i).start()
+        if known_refs:
+            kept(i).start()
     for i in range(pieces):
         loaded(i).wait()
         both = times(table_ref[...], values[:, i * wide : (i + 1) * wide])
         total = both[:count] + both[count:]
-        for known in known_refs:
-            total = total + known[:, i * wide : (i + 1) * wide]
+        if known_refs:
+            kept(i).wait()
+            total = total + known[:, i * wide : (i + 1) * wide].astype(jnp.float32)
         mixed[:, i * wide : (i + 1) * wide] = total.astype(mixed.dtype)
         stored(i).start()
     for i in range(pieces):
         stored(i).wait()
 
 
-def mix(table, rows, known, dtype):
+def mix(table, rows, known):
     count = table.shape[0] // 2
     slots, width = rows.shape
     anywhere = pl.BlockSpec(memory_space=pl.ANY)
@@ -278,12 +284,14 @@
     return pl.pallas_call(
         mix_kernel,
         name="mix_slots",
-        out_shape=jax.ShapeDtypeStruct((count, width), dtype),
-        in_specs=[vmem, anywhere] + [vmem] * len(known),
+        out_shape=jax.ShapeDtypeStruct((count, width), jnp.bfloat16),
+        in_specs=[vmem, anywhere] + [anywhere] * len(known),
         out_specs=anywhere,
         scratch_shapes=[
             pltpu.VMEM((slots, width), jnp.bfloat16),
-            pltpu.VMEM((count, width), dtype),
+            pltpu.VMEM((count, width), jnp.bfloat16),
+            pltpu.VMEM((count, width), jnp.bfloat16),
+            pltpu.SemaphoreType.DMA((PIECES,)),
             pltpu.SemaphoreType.DMA((PIECES,)),
             pltpu.SemaphoreType.DMA((PIECES,)),
         ],
@@ -316,8 +324,8 @@
         parts.append(exchange(expert(rows, gates, ups, downs), devices))
     known = []
     for chunk in range(CHUNKS - 1):
-        known = [mix(table[chunk], parts[chunk], known, jnp.float32)]
-    return mix(table[CHUNKS - 1], parts[CHUNKS - 1], known, jnp.bfloat16)
+        known = [mix(table[chunk], parts[chunk], known)]
+    return mix(table[CHUNKS - 1], parts[CHUNKS - 1], known)
 
 
 def solution(mesh):

time: 226 us -> 225 us (level)
  transfers between devices with their start and end apart: 7 -> 7, of which waited for: 4 -> 4; matrix products, arithmetic and copies ran while one was open for 0% -> 0% of each run, Pallas kernels for 33% -> 34%
where the time goes in v8:
time: 225 us; the launch traced here: 224 us
  waiting for transfers between devices  120 us (53%)
  Pallas kernels  80.6 us (36%)
  starting transfers between devices  23.8 us (11%)
    all_to_all x4, waiting for transfers between devices, exchange(): lax.all_to_all(split, 'ep', split_axis=0, concat_axis=0, tiled=True)  120 us
    pallas_call x2, Pallas kernels, expert(): pl.pallas_call(functools.partial(expert_kernel, steps), name='expert_rows...  59.3 us
    all_to_all x4, starting transfers between devices, exchange(): lax.all_to_all(split, 'ep', split_axis=0, concat_axis=0, tiled=True)  23.3 us
    pallas_call x2, Pallas kernels, mix(): pl.pallas_call(mix_kernel, name='mix_slots', out_shape=jax.ShapeDtypeStru...  10.2 us
    pallas_call x2, Pallas kernels, slots_of_tokens(): pl.pallas_call(functools.partial(pick_kernel, experts, chunk), name='pick...  9.16 us
  transfers between devices with their start and end apart: 7, of which 4 were waited for; matrix products, arithmetic and copies ran while one was open for 0% of the time, Pallas kernels for 34%

profile of v8, /device:TPU:0, one launch (start us, length us, event | category | flops | bytes accessed | tf_op | source)
XLA Modules:
  0.0 224.4 jit_solution(3665760979705536007)
XLA Ops:
  0.0 0.0 collective-permute-start
  0.0 0.5 collective-permute-start.1
  0.5 0.0 collective-permute-start.2
  0.5 4.6 %pick_slots.3 = bf16[256,7168]{1,0:T(8,128)(2,1)} custom-call(s32[2,128]{1,0:T(2,128)} %bitcast.14, bf16[128,7168]{1,0:T(8,128)(2,1)} %tokens_ref.3), custom_call_target="tpu_custom_call" | custom-call | tf_op jit(solution)/shard_map/pick_slots/pallas_call | solution.py:98
  5.1 8.7 %all-to-all-start.2 = ((bf16[32,8,7168]{2,1,0:T(8,128)(2,1)}), bf16[32,8,7168]{2,1,0:T(8,128)(2,1)}, u32[]{:S(2)}, u32[]{:S(2)}) async-start(bf16[32,8,7168]{2,1,0:T(8,128)(2,1)} %bitcast.13), calls=%async_computation.2 | async-start | bytes 7340032 | tf_op jit(solution)/shard_map/all_to_all | solution.py:308
  13.8 4.6 %pick_slots.2 = bf16[256,7168]{1,0:T(8,128)(2,1)} custom-call(s32[2,128]{1,0:T(2,128)} %bitcast.15, bf16[128,7168]{1,0:T(8,128)(2,1)} %tokens_ref.3), custom_call_target="tpu_custom_call" | custom-call | tf_op jit(solution)/shard_map/pick_slots/pallas_call | solution.py:98
  18.4 43.1 %all-to-all-done.2 = bf16[32,8,7168]{2,1,0:T(8,128)(2,1)} async-done(((bf16[32,8,7168]{2,1,0:T(8,128)(2,1)}), bf16[32,8,7168]{2,1,0:T(8,128)(2,1)}, u32[]{:S(2)}, u32[]{:S(2)}) %all-to-all-start.2) | async-done | bytes 3670048 | tf_op jit(solution)/shard_map/all_to_all | solution.py:308
  61.4 4.8 %all-to-all-start = ((bf16[32,8,7168]{2,1,0:T(8,128)(2,1)}), bf16[32,8,7168]{2,1,0:T(8,128)(2,1)}, u32[]{:S(2)}, u32[]{:S(2)}) async-start(bf16[32,8,7168]{2,1,0:T(8,128)(2,1)} %bitcast.12), calls=%async_computation | async-start | bytes 7340032 | tf_op jit(solution)/shard_map/all_to_all | solution.py:308
  66.3 0.0 collective-permute-done.g1
  66.3 0.0 collective-permute-done.1.u1
  66.3 0.0 collective-permute-done.2.d1
  66.3 29.6 %expert_rows.3 = bf16[256,7168]{1,0:T(8,128)(2,1)} custom-call(bf16[256,7168]{1,0:T(8,128)(2,1)} %bitcast.7.x_ref, bf16[1,7168,512]{2,1,0:T(8,128)(2,1)} %g0.3, bf16[1,7168,512]{2,1,0:T(8,128)(2,1)} %collective-permute-done.g1, bf16[1,7168,512]{2,1,0:T(8,128)(2,1)} %u0.3, bf16[1,7168,512]{2,1,0:T(8,128)(2,1)} %collective-permute-done.1.u1, ...), custom_call_target="tpu_custom_call" | custom-call | flops 11274289152 | bytes 51380224 | tf_op jit(solution)/shard_map/expert_rows/pallas_call | solution.py:177
  96.0 18.0 %all-to-all-done = bf16[32,8,7168]{2,1,0:T(8,128)(2,1)} async-done(((bf16[32,8,7168]{2,1,0:T(8,128)(2,1)}), bf16[32,8,7168]{2,1,0:T(8,128)(2,1)}, u32[]{:S(2)}, u32[]{:S(2)}) %all-to-all-start) | async-done | bytes 3670048 | tf_op jit(solution)/shard_map/all_to_all | solution.py:308
  114.0 4.8 %all-to-all-start.3 = ((bf16[32,8,7168]{2,1,0:T(8,128)(2,1)}), bf16[32,8,7168]{2,1,0:T(8,128)(2,1)}, u32[]{:S(2)}, u32[]{:S(2)}) async-start(bf16[32,8,7168]{2,1,0:T(8,128)(2,1)} %bitcast.11), calls=%async_computation.3 | async-start | bytes 7340032 | tf_op jit(solution)/shard_map/all_to_all | solution.py:308
  118.8 29.6 %expert_rows.2 = bf16[256,7168]{1,0:T(8,128)(2,1)} custom-call(bf16[256,7168]{1,0:T(8,128)(2,1)} %bitcast.3.x_ref, bf16[1,7168,512]{2,1,0:T(8,128)(2,1)} %g0.3, bf16[1,7168,512]{2,1,0:T(8,128)(2,1)} %collective-permute-done.g1, bf16[1,7168,512]{2,1,0:T(8,128)(2,1)} %u0.3, bf16[1,7168,512]{2,1,0:T(8,128)(2,1)} %collective-permute-done.1.u1, ...), custom_call_target="tpu_custom_call" | custom-call | flops 11274289152 | bytes 51380224 | tf_op jit(solution)/shard_map/expert_rows/pallas_call | solution.py:177
  148.4 18.0 %all-to-all-done.3 = bf16[32,8,7168]{2,1,0:T(8,128)(2,1)} async-done(((bf16[32,8,7168]{2,1,0:T(8,128)(2,1)}), bf16[32,8,7168]{2,1,0:T(8,128)(2,1)}, u32[]{:S(2)}, u32[]{:S(2)}) %all-to-all-start.3) | async-done | bytes 3670048 | tf_op jit(solution)/shard_map/all_to_all | solution.py:308
  166.5 5.0 %all-to-all-start.1 = ((bf16[32,8,7168]{2,1,0:T(8,128)(2,1)}), bf16[32,8,7168]{2,1,0:T(8,128)(2,1)}, u32[]{:S(2)}, u32[]{:S(2)}) async-start(bf16[32,8,7168]{2,1,0:T(8,128)(2,1)} %bitcast.10), calls=%async_computation.1 | async-start | bytes 7340032 | tf_op jit(solution)/shard_map/all_to_all | solution.py:308
  171.5 2.0 slot_weights.1
  173.4 5.0 %mix_slots.2.rest_0_ = bf16[128,7168]{1,0:T(8,128)(2,1)} custom-call(bf16[256,256]{1,0:T(8,128)(2,1)} %get-tuple-element.8.table_ref, bf16[256,7168]{1,0:T(8,128)(2,1)} %bitcast.9.in_ref), custom_call_target="tpu_custom_call" | custom-call | flops 939524096 | bytes 3670016 | tf_op jit(solution)/shard_map/mix_slots/pallas_call | solution.py:284
  178.4 40.6 %all-to-all-done.1 = bf16[32,8,7168]{2,1,0:T(8,128)(2,1)} async-done(((bf16[32,8,7168]{2,1,0:T(8,128)(2,1)}), bf16[32,8,7168]{2,1,0:T(8,128)(2,1)}, u32[]{:S(2)}, u32[]{:S(2)}) %all-to-all-start.1) | async-done | bytes 3670048 | tf_op jit(solution)/shard_map/all_to_all | solution.py:308
  219.0 5.3 %mix_slots.3 = bf16[128,7168]{1,0:T(8,128)(2,1)} custom-call(bf16[256,256]{1,0:T(8,128)(2,1)} %get-tuple-element.7.table_ref, bf16[256,7168]{1,0:T(8,128)(2,1)} %bitcast.5.in_ref, bf16[128,7168]{1,0:T(8,128)(2,1)} %mix_slots.2.rest_0_), custom_call_target="tpu_custom_call" | custom-call | flops 939524096 | bytes 3670016 | tf_op jit(solution)/shard_map/mix_slots/pallas_call | solution.py:284
Async XLA Ops:
  0.0 66.3 %collective-permute-start = (bf16[1,7168,512]{2,1,0:T(8,128)(2,1)}, bf16[1,7168,512]{2,1,0:T(8,128)(2,1)}, u32[]{:S(2)}, u32[]{:S(2)}) collective-permute-start(bf16[1,7168,512]{2,1,0:T(8,128)(2,1)} %g0.3), channel_id=1, source_target_pairs={{0,4},{4,0},{8,12},{12,8},{16,20},{20,16},{24,28},{28,24},{32,36},... | collective-permute-start | bytes 22020104 | tf_op jit(solution)/shard_map/ppermute | solution.py:318
  0.0 66.3 %collective-permute-start.1 = (bf16[1,7168,512]{2,1,0:T(8,128)(2,1)}, bf16[1,7168,512]{2,1,0:T(8,128)(2,1)}, u32[]{:S(2)}, u32[]{:S(2)}) collective-permute-start(bf16[1,7168,512]{2,1,0:T(8,128)(2,1)} %u0.3), channel_id=1, source_target_pairs={{0,4},{4,0},{8,12},{12,8},{16,20},{20,16},{24,28},{28,24},{32,36},... | collective-permute-start | bytes 22020104 | tf_op jit(solution)/shard_map/ppermute | solution.py:318
  0.5 65.8 %collective-permute-start.2 = (bf16[1,512,7168]{2,1,0:T(8,128)(2,1)}, bf16[1,512,7168]{2,1,0:T(8,128)(2,1)}, u32[]{:S(2)}, u32[]{:S(2)}) collective-permute-start(bf16[1,512,7168]{2,1,0:T(8,128)(2,1)} %d0.3), channel_id=1, source_target_pairs={{0,4},{4,0},{8,12},{12,8},{16,20},{20,16},{24,28},{28,24},{32,36},... | collective-permute-start | bytes 22020104 | tf_op jit(solution)/shard_map/ppermute | solution.py:318
  5.1 56.3 %all-to-all-start.2 = ((bf16[32,8,7168]{2,1,0:T(8,128)(2,1)}), bf16[32,8,7168]{2,1,0:T(8,128)(2,1)}, u32[]{:S(2)}, u32[]{:S(2)}) async-start(bf16[32,8,7168]{2,1,0:T(8,128)(2,1)} %bitcast.13), calls=%async_computation.2 | async-start | bytes 7340032 | tf_op jit(solution)/shard_map/all_to_all | solution.py:308
  61.4 52.5 %all-to-all-start = ((bf16[32,8,7168]{2,1,0:T(8,128)(2,1)}), bf16[32,8,7168]{2,1,0:T(8,128)(2,1)}, u32[]{:S(2)}, u32[]{:S(2)}) async-start(bf16[32,8,7168]{2,1,0:T(8,128)(2,1)} %bitcast.12), calls=%async_computation | async-start | bytes 7340032 | tf_op jit(solution)/shard_map/all_to_all | solution.py:308
  114.0 52.5 %all-to-all-start.3 = ((bf16[32,8,7168]{2,1,0:T(8,128)(2,1)}), bf16[32,8,7168]{2,1,0:T(8,128)(2,1)}, u32[]{:S(2)}, u32[]{:S(2)}) async-start(bf16[32,8,7168]{2,1,0:T(8,128)(2,1)} %bitcast.11), calls=%async_computation.3 | async-start | bytes 7340032 | tf_op jit(solution)/shard_map/all_to_all | solution.py:308
  166.5 52.5 %all-to-all-start.1 = ((bf16[32,8,7168]{2,1,0:T(8,128)(2,1)}), bf16[32,8,7168]{2,1,0:T(8,128)(2,1)}, u32[]{:S(2)}, u32[]{:S(2)}) async-start(bf16[32,8,7168]{2,1,0:T(8,128)(2,1)} %bitcast.10), calls=%async_computation.1 | async-start | bytes 7340032 | tf_op jit(solution)/shard_map/all_to_all | solution.py:308

commit v9 on v8

--- a/solution.py
+++ b/solution.py
@@ -62,7 +62,9 @@
     return (payload * scale).astype(jnp.bfloat16)
 
 
-def pick_kernel(experts, chunk, ids_ref, tokens_ref, out_ref, tokens, rows_out, pick, got, put):
+def pick_kernel(
+    experts, chunk, ids_in, tokens_ref, out_ref, ids_ref, tokens, rows_out, pick, got, put, first
+):
     count, width = tokens.shape
     rows = rows_out.shape[0]
     each = rows // experts
@@ -77,8 +79,11 @@
         part = (slice(None), pl.ds(i * wide, wide))
         return pltpu.make_async_copy(rows_out.at[part], out_ref.at[part], put.at[i])
 
+    ids_copy = pltpu.make_async_copy(ids_in, ids_ref, first)
+    ids_copy.start()
     for i in range(pieces):
         loaded(i).start()
+    ids_copy.wait()
     key = slot_keys(ids_ref, experts)
     all_keys = times(ones_where(iota((rows, experts), 0) // each == iota((rows, experts), 1)), key)
     place = (iota((rows, count), 0) % each + each * chunk).astype(jnp.float32)
@@ -99,14 +104,16 @@
         functools.partial(pick_kernel, experts, chunk),
         name="pick_slots",
         out_shape=jax.ShapeDtypeStruct((rows, width), jnp.bfloat16),
-        in_specs=[pl.BlockSpec(memory_space=pltpu.VMEM), pl.BlockSpec(memory_space=pl.ANY)],
+        in_specs=[pl.BlockSpec(memory_space=pl.ANY)] * 2,
         out_specs=pl.BlockSpec(memory_space=pl.ANY),
         scratch_shapes=[
+            pltpu.VMEM((TOP, count), jnp.int32),
             pltpu.VMEM((count, width), jnp.bfloat16),
             pltpu.VMEM((rows, width), jnp.bfloat16),
             pltpu.VMEM((rows, count), jnp.bfloat16),
             pltpu.SemaphoreType.DMA((PIECES,)),
             pltpu.SemaphoreType.DMA((PIECES,)),
+            pltpu.SemaphoreType.DMA,
         ],
         compiler_params=pltpu.CompilerParams(vmem_limit_bytes=VMEM_BYTES),
     )(turned_ids, tokens)
@@ -240,9 +247,9 @@
     )(turned_ids, turned_affinity)
 
 
-def mix_kernel(table_ref, in_ref, *rest):
-    known_refs, out_ref = rest[:-7], rest[-7]
-    values, mixed, known, got, put, held = rest[-6:]
+def mix_kernel(table_in, in_ref, *rest):
+    known_refs, out_ref = rest[:-9], rest[-9]
+    table_ref, values, mixed, known, got, put, held, first = rest[-8:]
     count, width = mixed.shape
     pieces = put.shape[0]
     wide = width // pieces
@@ -259,10 +266,13 @@
     def kept(i):
         return pltpu.make_async_copy(known_refs[0].at[part(i)], known.at[part(i)], held.at[i])
 
+    table_copy = pltpu.make_async_copy(table_in, table_ref, first)
+    table_copy.start()
     for i in range(pieces):
         loaded(i).start()
         if known_refs:
             kept(i).start()
+    table_copy.wait()
     for i in range(pieces):
         loaded(i).wait()
         both = times(table_ref[...], values[:, i * wide : (i + 1) * wide])
@@ -280,20 +290,21 @@
     count = table.shape[0] // 2
     slots, width = rows.shape
     anywhere = pl.BlockSpec(memory_space=pl.ANY)
-    vmem = pl.BlockSpec(memory_space=pltpu.VMEM)
     return pl.pallas_call(
         mix_kernel,
         name="mix_slots",
         out_shape=jax.ShapeDtypeStruct((count, width), jnp.bfloat16),
-        in_specs=[vmem, anywhere] + [anywhere] * len(known),
+        in_specs=[anywhere] * (2 + len(known)),
         out_specs=anywhere,
         scratch_shapes=[
+            pltpu.VMEM(table.shape, jnp.bfloat16),
             pltpu.VMEM((slots, width), jnp.bfloat16),
             pltpu.VMEM((count, width), jnp.bfloat16),
             pltpu.VMEM((count, width), jnp.bfloat16),
             pltpu.SemaphoreType.DMA((PIECES,)),
             pltpu.SemaphoreType.DMA((PIECES,)),
             pltpu.SemaphoreType.DMA((PIECES,)),
+            pltpu.SemaphoreType.DMA,
         ],
         compiler_params=pltpu.CompilerParams(vmem_limit_bytes=VMEM_BYTES),
         cost_estimate=pl.CostEstimate(

time: 225 us -> 225 us (level)
  transfers between devices with their start and end apart: 7 -> 7, of which waited for: 4 -> 4; matrix products, arithmetic and copies ran while one was open for 0% -> 0% of each run, Pallas kernels for 34% -> 33%
where the time goes in v9:
time: 225 us
  waiting for transfers between devices  120 us (53%)
  Pallas kernels  80.6 us (36%)
  starting transfers between devices  23.8 us (11%)
    all_to_all x4, waiting for transfers between devices, exchange(): lax.all_to_all(split, 'ep', split_axis=0, concat_axis=0, tiled=True)  120 us
    pallas_call x2, Pallas kernels, expert(): pl.pallas_call(functools.partial(expert_kernel, steps), name='expert_rows...  59.3 us
    all_to_all x4, starting transfers between devices, exchange(): lax.all_to_all(split, 'ep', split_axis=0, concat_axis=0, tiled=True)  23.3 us
    pallas_call x2, Pallas kernels, mix(): pl.pallas_call(mix_kernel, name='mix_slots', out_shape=jax.ShapeDtypeStru...  10.6 us
    pallas_call x2, Pallas kernels, slots_of_tokens(): pl.pallas_call(functools.partial(pick_kernel, experts, chunk), name='pick...  8.81 us
  transfers between devices with their start and end apart: 7, of which 4 were waited for; matrix products, arithmetic and copies ran while one was open for 0% of the time, Pallas kernels for 33%

profile of v9, /device:TPU:0, one launch (start us, length us, event | category | flops | bytes accessed | tf_op | source)
XLA Modules:
  0.0 224.6 jit_solution(983512936140990373)
XLA Ops:
  0.0 0.0 collective-permute-start
  0.0 0.5 collective-permute-start.1
  0.5 0.0 collective-permute-start.2
  0.5 4.4 %pick_slots.3 = bf16[256,7168]{1,0:T(8,128)(2,1)} custom-call(s32[2,128]{1,0:T(2,128)} %bitcast.14, bf16[128,7168]{1,0:T(8,128)(2,1)} %tokens_ref.3), custom_call_target="tpu_custom_call" | custom-call | tf_op jit(solution)/shard_map/pick_slots/pallas_call | solution.py:103
  4.9 8.7 %all-to-all-start.2 = ((bf16[32,8,7168]{2,1,0:T(8,128)(2,1)}), bf16[32,8,7168]{2,1,0:T(8,128)(2,1)}, u32[]{:S(2)}, u32[]{:S(2)}) async-start(bf16[32,8,7168]{2,1,0:T(8,128)(2,1)} %bitcast.13), calls=%async_computation.2 | async-start | bytes 7340032 | tf_op jit(solution)/shard_map/all_to_all | solution.py:319
  13.6 4.4 %pick_slots.2 = bf16[256,7168]{1,0:T(8,128)(2,1)} custom-call(s32[2,128]{1,0:T(2,128)} %bitcast.15, bf16[128,7168]{1,0:T(8,128)(2,1)} %tokens_ref.3), custom_call_target="tpu_custom_call" | custom-call | tf_op jit(solution)/shard_map/pick_slots/pallas_call | solution.py:103
  18.0 43.3 %all-to-all-done.2 = bf16[32,8,7168]{2,1,0:T(8,128)(2,1)} async-done(((bf16[32,8,7168]{2,1,0:T(8,128)(2,1)}), bf16[32,8,7168]{2,1,0:T(8,128)(2,1)}, u32[]{:S(2)}, u32[]{:S(2)}) %all-to-all-start.2) | async-done | bytes 3670048 | tf_op jit(solution)/shard_map/all_to_all | solution.py:319
  61.3 4.8 %all-to-all-start = ((bf16[32,8,7168]{2,1,0:T(8,128)(2,1)}), bf16[32,8,7168]{2,1,0:T(8,128)(2,1)}, u32[]{:S(2)}, u32[]{:S(2)}) async-start(bf16[32,8,7168]{2,1,0:T(8,128)(2,1)} %bitcast.12), calls=%async_computation | async-start | bytes 7340032 | tf_op jit(solution)/shard_map/all_to_all | solution.py:319
  66.1 0.0 collective-permute-done.g1
  66.1 0.0 collective-permute-done.1.u1
  66.1 0.0 collective-permute-done.2.d1
  66.1 29.6 %expert_rows.3 = bf16[256,7168]{1,0:T(8,128)(2,1)} custom-call(bf16[256,7168]{1,0:T(8,128)(2,1)} %bitcast.7.x_ref, bf16[1,7168,512]{2,1,0:T(8,128)(2,1)} %g0.3, bf16[1,7168,512]{2,1,0:T(8,128)(2,1)} %collective-permute-done.g1, bf16[1,7168,512]{2,1,0:T(8,128)(2,1)} %u0.3, bf16[1,7168,512]{2,1,0:T(8,128)(2,1)} %collective-permute-done.1.u1, ...), custom_call_target="tpu_custom_call" | custom-call | flops 11274289152 | bytes 51380224 | tf_op jit(solution)/shard_map/expert_rows/pallas_call | solution.py:184
  95.8 18.0 %all-to-all-done = bf16[32,8,7168]{2,1,0:T(8,128)(2,1)} async-done(((bf16[32,8,7168]{2,1,0:T(8,128)(2,1)}), bf16[32,8,7168]{2,1,0:T(8,128)(2,1)}, u32[]{:S(2)}, u32[]{:S(2)}) %all-to-all-start) | async-done | bytes 3670048 | tf_op jit(solution)/shard_map/all_to_all | solution.py:319
  113.8 4.8 %all-to-all-start.3 = ((bf16[32,8,7168]{2,1,0:T(8,128)(2,1)}), bf16[32,8,7168]{2,1,0:T(8,128)(2,1)}, u32[]{:S(2)}, u32[]{:S(2)}) async-start(bf16[32,8,7168]{2,1,0:T(8,128)(2,1)} %bitcast.11), calls=%async_computation.3 | async-start | bytes 7340032 | tf_op jit(solution)/shard_map/all_to_all | solution.py:319
  118.6 29.6 %expert_rows.2 = bf16[256,7168]{1,0:T(8,128)(2,1)} custom-call(bf16[256,7168]{1,0:T(8,128)(2,1)} %bitcast.3.x_ref, bf16[1,7168,512]{2,1,0:T(8,128)(2,1)} %g0.3, bf16[1,7168,512]{2,1,0:T(8,128)(2,1)} %collective-permute-done.g1, bf16[1,7168,512]{2,1,0:T(8,128)(2,1)} %u0.3, bf16[1,7168,512]{2,1,0:T(8,128)(2,1)} %collective-permute-done.1.u1, ...), custom_call_target="tpu_custom_call" | custom-call | flops 11274289152 | bytes 51380224 | tf_op jit(solution)/shard_map/expert_rows/pallas_call | solution.py:184
  148.3 18.0 %all-to-all-done.3 = bf16[32,8,7168]{2,1,0:T(8,128)(2,1)} async-done(((bf16[32,8,7168]{2,1,0:T(8,128)(2,1)}), bf16[32,8,7168]{2,1,0:T(8,128)(2,1)}, u32[]{:S(2)}, u32[]{:S(2)}) %all-to-all-start.3) | async-done | bytes 3670048 | tf_op jit(solution)/shard_map/all_to_all | solution.py:319
  166.3 5.0 %all-to-all-start.1 = ((bf16[32,8,7168]{2,1,0:T(8,128)(2,1)}), bf16[32,8,7168]{2,1,0:T(8,128)(2,1)}, u32[]{:S(2)}, u32[]{:S(2)}) async-start(bf16[32,8,7168]{2,1,0:T(8,128)(2,1)} %bitcast.10), calls=%async_computation.1 | async-start | bytes 7340032 | tf_op jit(solution)/shard_map/all_to_all | solution.py:319
  171.3 2.0 slot_weights.1
  173.3 4.9 %mix_slots.2.rest_0_ = bf16[128,7168]{1,0:T(8,128)(2,1)} custom-call(bf16[256,256]{1,0:T(8,128)(2,1)} %get-tuple-element.8.table_in, bf16[256,7168]{1,0:T(8,128)(2,1)} %bitcast.9.in_ref), custom_call_target="tpu_custom_call" | custom-call | flops 939524096 | bytes 3670016 | tf_op jit(solution)/shard_map/mix_slots/pallas_call | solution.py:293
  178.2 40.6 %all-to-all-done.1 = bf16[32,8,7168]{2,1,0:T(8,128)(2,1)} async-done(((bf16[32,8,7168]{2,1,0:T(8,128)(2,1)}), bf16[32,8,7168]{2,1,0:T(8,128)(2,1)}, u32[]{:S(2)}, u32[]{:S(2)}) %all-to-all-start.1) | async-done | bytes 3670048 | tf_op jit(solution)/shard_map/all_to_all | solution.py:319
  218.8 5.7 %mix_slots.3 = bf16[128,7168]{1,0:T(8,128)(2,1)} custom-call(bf16[256,256]{1,0:T(8,128)(2,1)} %get-tuple-element.7.table_in, bf16[256,7168]{1,0:T(8,128)(2,1)} %bitcast.5.in_ref, bf16[128,7168]{1,0:T(8,128)(2,1)} %mix_slots.2.rest_0_), custom_call_target="tpu_custom_call" | custom-call | flops 939524096 | bytes 3670016 | tf_op jit(solution)/shard_map/mix_slots/pallas_call | solution.py:293
Async XLA Ops:
  0.0 66.1 %collective-permute-start = (bf16[1,7168,512]{2,1,0:T(8,128)(2,1)}, bf16[1,7168,512]{2,1,0:T(8,128)(2,1)}, u32[]{:S(2)}, u32[]{:S(2)}) collective-permute-start(bf16[1,7168,512]{2,1,0:T(8,128)(2,1)} %g0.3), channel_id=1, source_target_pairs={{0,4},{4,0},{8,12},{12,8},{16,20},{20,16},{24,28},{28,24},{32,36},... | collective-permute-start | bytes 22020104 | tf_op jit(solution)/shard_map/ppermute | solution.py:329
  0.0 66.1 %collective-permute-start.1 = (bf16[1,7168,512]{2,1,0:T(8,128)(2,1)}, bf16[1,7168,512]{2,1,0:T(8,128)(2,1)}, u32[]{:S(2)}, u32[]{:S(2)}) collective-permute-start(bf16[1,7168,512]{2,1,0:T(8,128)(2,1)} %u0.3), channel_id=1, source_target_pairs={{0,4},{4,0},{8,12},{12,8},{16,20},{20,16},{24,28},{28,24},{32,36},... | collective-permute-start | bytes 22020104 | tf_op jit(solution)/shard_map/ppermute | solution.py:329
  0.5 65.6 %collective-permute-start.2 = (bf16[1,512,7168]{2,1,0:T(8,128)(2,1)}, bf16[1,512,7168]{2,1,0:T(8,128)(2,1)}, u32[]{:S(2)}, u32[]{:S(2)}) collective-permute-start(bf16[1,512,7168]{2,1,0:T(8,128)(2,1)} %d0.3), channel_id=1, source_target_pairs={{0,4},{4,0},{8,12},{12,8},{16,20},{20,16},{24,28},{28,24},{32,36},... | collective-permute-start | bytes 22020104 | tf_op jit(solution)/shard_map/ppermute | solution.py:329
  4.9 56.3 %all-to-all-start.2 = ((bf16[32,8,7168]{2,1,0:T(8,128)(2,1)}), bf16[32,8,7168]{2,1,0:T(8,128)(2,1)}, u32[]{:S(2)}, u32[]{:S(2)}) async-start(bf16[32,8,7168]{2,1,0:T(8,128)(2,1)} %bitcast.13), calls=%async_computation.2 | async-start | bytes 7340032 | tf_op jit(solution)/shard_map/all_to_all | solution.py:319
  61.3 52.5 %all-to-all-start = ((bf16[32,8,7168]{2,1,0:T(8,128)(2,1)}), bf16[32,8,7168]{2,1,0:T(8,128)(2,1)}, u32[]{:S(2)}, u32[]{:S(2)}) async-start(bf16[32,8,7168]{2,1,0:T(8,128)(2,1)} %bitcast.12), calls=%async_computation | async-start | bytes 7340032 | tf_op jit(solution)/shard_map/all_to_all | solution.py:319
  113.8 52.5 %all-to-all-start.3 = ((bf16[32,8,7168]{2,1,0:T(8,128)(2,1)}), bf16[32,8,7168]{2,1,0:T(8,128)(2,1)}, u32[]{:S(2)}, u32[]{:S(2)}) async-start(bf16[32,8,7168]{2,1,0:T(8,128)(2,1)} %bitcast.11), calls=%async_computation.3 | async-start | bytes 7340032 | tf_op jit(solution)/shard_map/all_to_all | solution.py:319
  166.3 52.5 %all-to-all-start.1 = ((bf16[32,8,7168]{2,1,0:T(8,128)(2,1)}), bf16[32,8,7168]{2,1,0:T(8,128)(2,1)}, u32[]{:S(2)}, u32[]{:S(2)}) async-start(bf16[32,8,7168]{2,1,0:T(8,128)(2,1)} %bitcast.10), calls=%async_computation.1 | async-start | bytes 7340032 | tf_op jit(solution)/shard_map/all_to_all | solution.py:319

commit v10 on v8

--- a/solution.py
+++ b/solution.py
@@ -62,7 +62,9 @@
     return (payload * scale).astype(jnp.bfloat16)
 
 
-def pick_kernel(experts, chunk, ids_ref, tokens_ref, out_ref, tokens, rows_out, pick, got, put):
+def pick_kernel(
+    experts, chunk, ids_in, tokens_ref, out_ref, ids_ref, tokens, rows_out, pick, got, put, first
+):
     count, width = tokens.shape
     rows = rows_out.shape[0]
     each = rows // experts
@@ -77,8 +79,11 @@
         part = (slice(None), pl.ds(i * wide, wide))
         return pltpu.make_async_copy(rows_out.at[part], out_ref.at[part], put.at[i])
 
+    ids_copy = pltpu.make_async_copy(ids_in, ids_ref, first)
+    ids_copy.start()
     for i in range(pieces):
         loaded(i).start()
+    ids_copy.wait()
     key = slot_keys(ids_ref, experts)
     all_keys = times(ones_where(iota((rows, experts), 0) // each == iota((rows, experts), 1)), key)
     place = (iota((rows, count), 0) % each + each * chunk).astype(jnp.float32)
@@ -99,14 +104,16 @@
         functools.partial(pick_kernel, experts, chunk),
         name="pick_slots",
         out_shape=jax.ShapeDtypeStruct((rows, width), jnp.bfloat16),
-        in_specs=[pl.BlockSpec(memory_space=pltpu.VMEM), pl.BlockSpec(memory_space=pl.ANY)],
+        in_specs=[pl.BlockSpec(memory_space=pl.ANY)] * 2,
         out_specs=pl.BlockSpec(memory_space=pl.ANY),
         scratch_shapes=[
+            pltpu.VMEM((TOP, count), jnp.int32),
             pltpu.VMEM((count, width), jnp.bfloat16),
             pltpu.VMEM((rows, width), jnp.bfloat16),
             pltpu.VMEM((rows, count), jnp.bfloat16),
             pltpu.SemaphoreType.DMA((PIECES,)),
             pltpu.SemaphoreType.DMA((PIECES,)),
+            pltpu.SemaphoreType.DMA,
         ],
         compiler_params=pltpu.CompilerParams(vmem_limit_bytes=VMEM_BYTES),
     )(turned_ids, tokens)

time: 225 us -> 225 us (level)
  transfers between devices with their start and end apart: 7 -> 7, of which waited for: 4 -> 4; matrix products, arithmetic and copies ran while one was open for 0% -> 0% of each run, Pallas kernels for 34% -> 33%
where the time goes in v10:
time: 225 us; the launch traced here: 224 us
  waiting for transfers between devices  120 us (53%)
  Pallas kernels  80.3 us (36%)
  starting transfers between devices  23.8 us (11%)
    all_to_all x4, waiting for transfers between devices, exchange(): lax.all_to_all(split, 'ep', split_axis=0, concat_axis=0, tiled=True)  120 us
    pallas_call x2, Pallas kernels, expert(): pl.pallas_call(functools.partial(expert_kernel, steps), name='expert_rows...  59.3 us
    all_to_all x4, starting transfers between devices, exchange(): lax.all_to_all(split, 'ep', split_axis=0, concat_axis=0, tiled=True)  23.3 us
    pallas_call x2, Pallas kernels, mix(): pl.pallas_call(mix_kernel, name='mix_slots', out_shape=jax.ShapeDtypeStru...  10.2 us
    pallas_call x2, Pallas kernels, slots_of_tokens(): pl.pallas_call(functools.partial(pick_kernel, experts, chunk), name='pick...  8.81 us
  transfers between devices with their start and end apart: 7, of which 4 were waited for; matrix products, arithmetic and copies ran while one was open for 0% of the time, Pallas kernels for 33%

profile of v10, /device:TPU:0, one launch (start us, length us, event | category | flops | bytes accessed | tf_op | source)
XLA Modules:
  0.0 224.2 jit_solution(635317159121359411)
XLA Ops:
  0.0 0.0 collective-permute-start
  0.0 0.5 collective-permute-start.1
  0.5 0.0 collective-permute-start.2
  0.5 4.4 %pick_slots.3 = bf16[256,7168]{1,0:T(8,128)(2,1)} custom-call(s32[2,128]{1,0:T(2,128)} %bitcast.14, bf16[128,7168]{1,0:T(8,128)(2,1)} %tokens_ref.3), custom_call_target="tpu_custom_call" | custom-call | tf_op jit(solution)/shard_map/pick_slots/pallas_call | solution.py:103
  4.9 8.7 %all-to-all-start.2 = ((bf16[32,8,7168]{2,1,0:T(8,128)(2,1)}), bf16[32,8,7168]{2,1,0:T(8,128)(2,1)}, u32[]{:S(2)}, u32[]{:S(2)}) async-start(bf16[32,8,7168]{2,1,0:T(8,128)(2,1)} %bitcast.13), calls=%async_computation.2 | async-start | bytes 7340032 | tf_op jit(solution)/shard_map/all_to_all | solution.py:315
  13.6 4.4 %pick_slots.2 = bf16[256,7168]{1,0:T(8,128)(2,1)} custom-call(s32[2,128]{1,0:T(2,128)} %bitcast.15, bf16[128,7168]{1,0:T(8,128)(2,1)} %tokens_ref.3), custom_call_target="tpu_custom_call" | custom-call | tf_op jit(solution)/shard_map/pick_slots/pallas_call | solution.py:103
  18.0 43.3 %all-to-all-done.2 = bf16[32,8,7168]{2,1,0:T(8,128)(2,1)} async-done(((bf16[32,8,7168]{2,1,0:T(8,128)(2,1)}), bf16[32,8,7168]{2,1,0:T(8,128)(2,1)}, u32[]{:S(2)}, u32[]{:S(2)}) %all-to-all-start.2) | async-done | bytes 3670048 | tf_op jit(solution)/shard_map/all_to_all | solution.py:315
  61.3 4.8 %all-to-all-start = ((bf16[32,8,7168]{2,1,0:T(8,128)(2,1)}), bf16[32,8,7168]{2,1,0:T(8,128)(2,1)}, u32[]{:S(2)}, u32[]{:S(2)}) async-start(bf16[32,8,7168]{2,1,0:T(8,128)(2,1)} %bitcast.12), calls=%async_computation | async-start | bytes 7340032 | tf_op jit(solution)/shard_map/all_to_all | solution.py:315
  66.1 0.0 collective-permute-done.g1
  66.1 0.0 collective-permute-done.1.u1
  66.1 0.0 collective-permute-done.2.d1
  66.1 29.6 %expert_rows.3 = bf16[256,7168]{1,0:T(8,128)(2,1)} custom-call(bf16[256,7168]{1,0:T(8,128)(2,1)} %bitcast.7.x_ref, bf16[1,7168,512]{2,1,0:T(8,128)(2,1)} %g0.3, bf16[1,7168,512]{2,1,0:T(8,128)(2,1)} %collective-permute-done.g1, bf16[1,7168,512]{2,1,0:T(8,128)(2,1)} %u0.3, bf16[1,7168,512]{2,1,0:T(8,128)(2,1)} %collective-permute-done.1.u1, ...), custom_call_target="tpu_custom_call" | custom-call | flops 11274289152 | bytes 51380224 | tf_op jit(solution)/shard_map/expert_rows/pallas_call | solution.py:184
  95.8 18.0 %all-to-all-done = bf16[32,8,7168]{2,1,0:T(8,128)(2,1)} async-done(((bf16[32,8,7168]{2,1,0:T(8,128)(2,1)}), bf16[32,8,7168]{2,1,0:T(8,128)(2,1)}, u32[]{:S(2)}, u32[]{:S(2)}) %all-to-all-start) | async-done | bytes 3670048 | tf_op jit(solution)/shard_map/all_to_all | solution.py:315
  113.8 4.8 %all-to-all-start.3 = ((bf16[32,8,7168]{2,1,0:T(8,128)(2,1)}), bf16[32,8,7168]{2,1,0:T(8,128)(2,1)}, u32[]{:S(2)}, u32[]{:S(2)}) async-start(bf16[32,8,7168]{2,1,0:T(8,128)(2,1)} %bitcast.11), calls=%async_computation.3 | async-start | bytes 7340032 | tf_op jit(solution)/shard_map/all_to_all | solution.py:315
  118.6 29.6 %expert_rows.2 = bf16[256,7168]{1,0:T(8,128)(2,1)} custom-call(bf16[256,7168]{1,0:T(8,128)(2,1)} %bitcast.3.x_ref, bf16[1,7168,512]{2,1,0:T(8,128)(2,1)} %g0.3, bf16[1,7168,512]{2,1,0:T(8,128)(2,1)} %collective-permute-done.g1, bf16[1,7168,512]{2,1,0:T(8,128)(2,1)} %u0.3, bf16[1,7168,512]{2,1,0:T(8,128)(2,1)} %collective-permute-done.1.u1, ...), custom_call_target="tpu_custom_call" | custom-call | flops 11274289152 | bytes 51380224 | tf_op jit(solution)/shard_map/expert_rows/pallas_call | solution.py:184
  148.3 18.0 %all-to-all-done.3 = bf16[32,8,7168]{2,1,0:T(8,128)(2,1)} async-done(((bf16[32,8,7168]{2,1,0:T(8,128)(2,1)}), bf16[32,8,7168]{2,1,0:T(8,128)(2,1)}, u32[]{:S(2)}, u32[]{:S(2)}) %all-to-all-start.3) | async-done | bytes 3670048 | tf_op jit(solution)/shard_map/all_to_all | solution.py:315
  166.3 5.0 %all-to-all-start.1 = ((bf16[32,8,7168]{2,1,0:T(8,128)(2,1)}), bf16[32,8,7168]{2,1,0:T(8,128)(2,1)}, u32[]{:S(2)}, u32[]{:S(2)}) async-start(bf16[32,8,7168]{2,1,0:T(8,128)(2,1)} %bitcast.10), calls=%async_computation.1 | async-start | bytes 7340032 | tf_op jit(solution)/shard_map/all_to_all | solution.py:315
  171.3 2.0 slot_weights.1
  173.3 5.0 %mix_slots.2.rest_0_ = bf16[128,7168]{1,0:T(8,128)(2,1)} custom-call(bf16[256,256]{1,0:T(8,128)(2,1)} %get-tuple-element.8.table_ref, bf16[256,7168]{1,0:T(8,128)(2,1)} %bitcast.9.in_ref), custom_call_target="tpu_custom_call" | custom-call | flops 939524096 | bytes 3670016 | tf_op jit(solution)/shard_map/mix_slots/pallas_call | solution.py:291
  178.2 40.6 %all-to-all-done.1 = bf16[32,8,7168]{2,1,0:T(8,128)(2,1)} async-done(((bf16[32,8,7168]{2,1,0:T(8,128)(2,1)}), bf16[32,8,7168]{2,1,0:T(8,128)(2,1)}, u32[]{:S(2)}, u32[]{:S(2)}) %all-to-all-start.1) | async-done | bytes 3670048 | tf_op jit(solution)/shard_map/all_to_all | solution.py:315
  218.8 5.3 %mix_slots.3 = bf16[128,7168]{1,0:T(8,128)(2,1)} custom-call(bf16[256,256]{1,0:T(8,128)(2,1)} %get-tuple-element.7.table_ref, bf16[256,7168]{1,0:T(8,128)(2,1)} %bitcast.5.in_ref, bf16[128,7168]{1,0:T(8,128)(2,1)} %mix_slots.2.rest_0_), custom_call_target="tpu_custom_call" | custom-call | flops 939524096 | bytes 3670016 | tf_op jit(solution)/shard_map/mix_slots/pallas_call | solution.py:291
Async XLA Ops:
  0.0 66.1 %collective-permute-start = (bf16[1,7168,512]{2,1,0:T(8,128)(2,1)}, bf16[1,7168,512]{2,1,0:T(8,128)(2,1)}, u32[]{:S(2)}, u32[]{:S(2)}) collective-permute-start(bf16[1,7168,512]{2,1,0:T(8,128)(2,1)} %g0.3), channel_id=1, source_target_pairs={{0,4},{4,0},{8,12},{12,8},{16,20},{20,16},{24,28},{28,24},{32,36},... | collective-permute-start | bytes 22020104 | tf_op jit(solution)/shard_map/ppermute | solution.py:325
  0.0 66.1 %collective-permute-start.1 = (bf16[1,7168,512]{2,1,0:T(8,128)(2,1)}, bf16[1,7168,512]{2,1,0:T(8,128)(2,1)}, u32[]{:S(2)}, u32[]{:S(2)}) collective-permute-start(bf16[1,7168,512]{2,1,0:T(8,128)(2,1)} %u0.3), channel_id=1, source_target_pairs={{0,4},{4,0},{8,12},{12,8},{16,20},{20,16},{24,28},{28,24},{32,36},... | collective-permute-start | bytes 22020104 | tf_op jit(solution)/shard_map/ppermute | solution.py:325
  0.5 65.6 %collective-permute-start.2 = (bf16[1,512,7168]{2,1,0:T(8,128)(2,1)}, bf16[1,512,7168]{2,1,0:T(8,128)(2,1)}, u32[]{:S(2)}, u32[]{:S(2)}) collective-permute-start(bf16[1,512,7168]{2,1,0:T(8,128)(2,1)} %d0.3), channel_id=1, source_target_pairs={{0,4},{4,0},{8,12},{12,8},{16,20},{20,16},{24,28},{28,24},{32,36},... | collective-permute-start | bytes 22020104 | tf_op jit(solution)/shard_map/ppermute | solution.py:325
  4.9 56.3 %all-to-all-start.2 = ((bf16[32,8,7168]{2,1,0:T(8,128)(2,1)}), bf16[32,8,7168]{2,1,0:T(8,128)(2,1)}, u32[]{:S(2)}, u32[]{:S(2)}) async-start(bf16[32,8,7168]{2,1,0:T(8,128)(2,1)} %bitcast.13), calls=%async_computation.2 | async-start | bytes 7340032 | tf_op jit(solution)/shard_map/all_to_all | solution.py:315
  61.3 52.5 %all-to-all-start = ((bf16[32,8,7168]{2,1,0:T(8,128)(2,1)}), bf16[32,8,7168]{2,1,0:T(8,128)(2,1)}, u32[]{:S(2)}, u32[]{:S(2)}) async-start(bf16[32,8,7168]{2,1,0:T(8,128)(2,1)} %bitcast.12), calls=%async_computation | async-start | bytes 7340032 | tf_op jit(solution)/shard_map/all_to_all | solution.py:315
  113.8 52.5 %all-to-all-start.3 = ((bf16[32,8,7168]{2,1,0:T(8,128)(2,1)}), bf16[32,8,7168]{2,1,0:T(8,128)(2,1)}, u32[]{:S(2)}, u32[]{:S(2)}) async-start(bf16[32,8,7168]{2,1,0:T(8,128)(2,1)} %bitcast.11), calls=%async_computation.3 | async-start | bytes 7340032 | tf_op jit(solution)/shard_map/all_to_all | solution.py:315
  166.3 52.5 %all-to-all-start.1 = ((bf16[32,8,7168]{2,1,0:T(8,128)(2,1)}), bf16[32,8,7168]{2,1,0:T(8,128)(2,1)}, u32[]{:S(2)}, u32[]{:S(2)}) async-start(bf16[32,8,7168]{2,1,0:T(8,128)(2,1)} %bitcast.10), calls=%async_computation.1 | async-start | bytes 7340032 | tf_op jit(solution)/shard_map/all_to_all | solution.py:315

commit v11 on v10

--- a/solution.py
+++ b/solution.py
@@ -322,12 +322,17 @@
     experts = devices // 2
     slots = 2 * tokens.shape[0] * TOP // experts
     pairs = [(s, s ^ 1) for s in range(devices)]
-    gates, ups, downs = [(w, lax.ppermute(w, "ep", pairs)) for w in (w_gate, w_up, w_down)]
+    gates, ups = [(w, lax.ppermute(w, "ep", pairs)) for w in (w_gate, w_up)]
     turned_ids = expert_ids.T
     table = weights_of_slots(turned_ids, affinity.T, experts, slots, CHUNKS)
     parts = []
-    for chunk in range(CHUNKS):
-        rows = exchange(slots_of_tokens(tokens, turned_ids, experts, slots, chunk), devices)
+    sent = [
+        slots_of_tokens(tokens, turned_ids, experts, slots, chunk) for chunk in range(CHUNKS)
+    ]
+    first, second, late = lax.optimization_barrier((exchange(sent[0], devices), sent[1], w_down))
+    downs = (w_down, lax.ppermute(late, "ep", pairs))
+    arrived = [first, exchange(second, devices)]
+    for rows in arrived:
         parts.append(exchange(expert(rows, gates, ups, downs), devices))
     known = []
     for chunk in range(CHUNKS - 1):

time: 225 us -> 224 us (level)
    all_to_all x4, waiting for transfers between devices: 120 us -> 112 us  [exchange(): lax.all_to_all(split, 'ep', split_axis=0, concat_axis=0, tiled=True)]
    ppermute x3, waiting for transfers between devices: 0.01 us -> 7.13 us  [the longest x1 7.12 us: on_device(): downs = (w_down, lax.ppermute(late, 'ep', pairs))]
  transfers between devices with their start and end apart: 7 -> 7, of which waited for: 4 -> 5; matrix products, arithmetic and copies ran while one was open for 0% -> 0% of each run, Pallas kernels for 33% -> 32%
where the time goes in v11:
time: 224 us
  waiting for transfers between devices  119 us (53%)
  Pallas kernels  80.2 us (36%)
  starting transfers between devices  23.8 us (11%)
    all_to_all x4, waiting for transfers between devices, exchange(): lax.all_to_all(split, 'ep', split_axis=0, concat_axis=0, tiled=True)  112 us
    pallas_call x2, Pallas kernels, expert(): pl.pallas_call(functools.partial(expert_kernel, steps), name='expert_rows...  59.3 us
    all_to_all x4, starting transfers between devices, exchange(): lax.all_to_all(split, 'ep', split_axis=0, concat_axis=0, tiled=True)  23.2 us
    pallas_call x2, Pallas kernels, mix(): pl.pallas_call(mix_kernel, name='mix_slots', out_shape=jax.ShapeDtypeStru...  10.2 us
    pallas_call x2, Pallas kernels, slots_of_tokens(): pl.pallas_call(functools.partial(pick_kernel, experts, chunk), name='pick...  8.8 us
    ppermute x1, waiting for transfers between devices, on_device(): downs = (w_down, lax.ppermute(late, 'ep', pairs))  7.12 us
  transfers between devices with their start and end apart: 7, of which 5 were waited for; matrix products, arithmetic and copies ran while one was open for 0% of the time, Pallas kernels for 32%

profile of v11, /device:TPU:0, one launch (start us, length us, event | category | flops | bytes accessed | tf_op | source)
XLA Modules:
  0.0 223.6 jit_solution(9028202846286612247)
XLA Ops:
  0.0 4.4 %pick_slots.2 = bf16[256,7168]{1,0:T(8,128)(2,1)} custom-call(s32[2,128]{1,0:T(2,128)} %bitcast.14, bf16[128,7168]{1,0:T(8,128)(2,1)} %tokens_ref.3), custom_call_target="tpu_custom_call" | custom-call | tf_op jit(solution)/shard_map/pick_slots/pallas_call | solution.py:103
  4.4 8.5 %all-to-all-start = ((bf16[32,8,7168]{2,1,0:T(8,128)(2,1)}), bf16[32,8,7168]{2,1,0:T(8,128)(2,1)}, u32[]{:S(2)}, u32[]{:S(2)}) async-start(bf16[32,8,7168]{2,1,0:T(8,128)(2,1)} %bitcast.13), calls=%async_computation | async-start | bytes 7340032 | tf_op jit(solution)/shard_map/all_to_all | solution.py:315
  13.0 0.3 collective-permute-start
  13.3 0.3 collective-permute-start.1
  13.6 4.4 %pick_slots.3 = bf16[256,7168]{1,0:T(8,128)(2,1)} custom-call(s32[2,128]{1,0:T(2,128)} %bitcast.15, bf16[128,7168]{1,0:T(8,128)(2,1)} %tokens_ref.3), custom_call_target="tpu_custom_call" | custom-call | tf_op jit(solution)/shard_map/pick_slots/pallas_call | solution.py:103
  18.0 42.7 %all-to-all-done = bf16[32,8,7168]{2,1,0:T(8,128)(2,1)} async-done(((bf16[32,8,7168]{2,1,0:T(8,128)(2,1)}), bf16[32,8,7168]{2,1,0:T(8,128)(2,1)}, u32[]{:S(2)}, u32[]{:S(2)}) %all-to-all-start) | async-done | bytes 3670048 | tf_op jit(solution)/shard_map/all_to_all | solution.py:315
  60.6 0.0 collective-permute-start.2
  60.6 4.8 %all-to-all-start.1 = ((bf16[32,8,7168]{2,1,0:T(8,128)(2,1)}), bf16[32,8,7168]{2,1,0:T(8,128)(2,1)}, u32[]{:S(2)}, u32[]{:S(2)}) async-start(bf16[32,8,7168]{2,1,0:T(8,128)(2,1)} %bitcast.12), calls=%async_computation.1 | async-start | bytes 7340032 | tf_op jit(solution)/shard_map/all_to_all | solution.py:315
  65.5 0.0 collective-permute-done.g1
  65.5 0.0 collective-permute-done.1.u1
  65.5 7.1 %collective-permute-done.2.d1 = bf16[1,512,7168]{2,1,0:T(8,128)(2,1)} collective-permute-done((bf16[1,512,7168]{2,1,0:T(8,128)(2,1)}, bf16[1,512,7168]{2,1,0:T(8,128)(2,1)}, u32[]{:S(2)}, u32[]{:S(2)}) %collective-permute-start.2) | collective-permute-done | bytes 7340064 | tf_op jit(solution)/shard_map/ppermute | solution.py:333
  72.6 29.6 %expert_rows.3 = bf16[256,7168]{1,0:T(8,128)(2,1)} custom-call(bf16[256,7168]{1,0:T(8,128)(2,1)} %bitcast.3.x_ref, bf16[1,7168,512]{2,1,0:T(8,128)(2,1)} %g0.3, bf16[1,7168,512]{2,1,0:T(8,128)(2,1)} %collective-permute-done.g1, bf16[1,7168,512]{2,1,0:T(8,128)(2,1)} %u0.3, bf16[1,7168,512]{2,1,0:T(8,128)(2,1)} %collective-permute-done.1.u1, ...), custom_call_target="tpu_custom_call" | custom-call | flops 11274289152 | bytes 51380224 | tf_op jit(solution)/shard_map/expert_rows/pallas_call | solution.py:184
  102.2 10.9 %all-to-all-done.1 = bf16[32,8,7168]{2,1,0:T(8,128)(2,1)} async-done(((bf16[32,8,7168]{2,1,0:T(8,128)(2,1)}), bf16[32,8,7168]{2,1,0:T(8,128)(2,1)}, u32[]{:S(2)}, u32[]{:S(2)}) %all-to-all-start.1) | async-done | bytes 3670048 | tf_op jit(solution)/shard_map/all_to_all | solution.py:315
  113.2 4.8 %all-to-all-start.3 = ((bf16[32,8,7168]{2,1,0:T(8,128)(2,1)}), bf16[32,8,7168]{2,1,0:T(8,128)(2,1)}, u32[]{:S(2)}, u32[]{:S(2)}) async-start(bf16[32,8,7168]{2,1,0:T(8,128)(2,1)} %bitcast.11), calls=%async_computation.3 | async-start | bytes 7340032 | tf_op jit(solution)/shard_map/all_to_all | solution.py:315
  118.0 29.6 %expert_rows.2 = bf16[256,7168]{1,0:T(8,128)(2,1)} custom-call(bf16[256,7168]{1,0:T(8,128)(2,1)} %bitcast.5.x_ref, bf16[1,7168,512]{2,1,0:T(8,128)(2,1)} %g0.3, bf16[1,7168,512]{2,1,0:T(8,128)(2,1)} %collective-permute-done.g1, bf16[1,7168,512]{2,1,0:T(8,128)(2,1)} %u0.3, bf16[1,7168,512]{2,1,0:T(8,128)(2,1)} %collective-permute-done.1.u1, ...), custom_call_target="tpu_custom_call" | custom-call | flops 11274289152 | bytes 51380224 | tf_op jit(solution)/shard_map/expert_rows/pallas_call | solution.py:184
  147.7 18.0 %all-to-all-done.3 = bf16[32,8,7168]{2,1,0:T(8,128)(2,1)} async-done(((bf16[32,8,7168]{2,1,0:T(8,128)(2,1)}), bf16[32,8,7168]{2,1,0:T(8,128)(2,1)}, u32[]{:S(2)}, u32[]{:S(2)}) %all-to-all-start.3) | async-done | bytes 3670048 | tf_op jit(solution)/shard_map/all_to_all | solution.py:315
  165.7 5.0 %all-to-all-start.2 = ((bf16[32,8,7168]{2,1,0:T(8,128)(2,1)}), bf16[32,8,7168]{2,1,0:T(8,128)(2,1)}, u32[]{:S(2)}, u32[]{:S(2)}) async-start(bf16[32,8,7168]{2,1,0:T(8,128)(2,1)} %bitcast.10), calls=%async_computation.2 | async-start | bytes 7340032 | tf_op jit(solution)/shard_map/all_to_all | solution.py:315
  170.7 2.0 slot_weights.1
  172.6 5.0 %mix_slots.2.rest_0_ = bf16[128,7168]{1,0:T(8,128)(2,1)} custom-call(bf16[256,256]{1,0:T(8,128)(2,1)} %get-tuple-element.13.table_ref, bf16[256,7168]{1,0:T(8,128)(2,1)} %bitcast.9.in_ref), custom_call_target="tpu_custom_call" | custom-call | flops 939524096 | bytes 3670016 | tf_op jit(solution)/shard_map/mix_slots/pallas_call | solution.py:291
  177.6 40.6 %all-to-all-done.2 = bf16[32,8,7168]{2,1,0:T(8,128)(2,1)} async-done(((bf16[32,8,7168]{2,1,0:T(8,128)(2,1)}), bf16[32,8,7168]{2,1,0:T(8,128)(2,1)}, u32[]{:S(2)}, u32[]{:S(2)}) %all-to-all-start.2) | async-done | bytes 3670048 | tf_op jit(solution)/shard_map/all_to_all | solution.py:315
  218.2 5.3 %mix_slots.3 = bf16[128,7168]{1,0:T(8,128)(2,1)} custom-call(bf16[256,256]{1,0:T(8,128)(2,1)} %get-tuple-element.10.table_ref, bf16[256,7168]{1,0:T(8,128)(2,1)} %bitcast.7.in_ref, bf16[128,7168]{1,0:T(8,128)(2,1)} %mix_slots.2.rest_0_), custom_call_target="tpu_custom_call" | custom-call | flops 939524096 | bytes 3670016 | tf_op jit(solution)/shard_map/mix_slots/pallas_call | solution.py:291
Async XLA Ops:
  4.4 56.2 %all-to-all-start = ((bf16[32,8,7168]{2,1,0:T(8,128)(2,1)}), bf16[32,8,7168]{2,1,0:T(8,128)(2,1)}, u32[]{:S(2)}, u32[]{:S(2)}) async-start(bf16[32,8,7168]{2,1,0:T(8,128)(2,1)} %bitcast.13), calls=%async_computation | async-start | bytes 7340032 | tf_op jit(solution)/shard_map/all_to_all | solution.py:315
  13.0 52.5 %collective-permute-start = (bf16[1,7168,512]{2,1,0:T(8,128)(2,1)}, bf16[1,7168,512]{2,1,0:T(8,128)(2,1)}, u32[]{:S(2)}, u32[]{:S(2)}) collective-permute-start(bf16[1,7168,512]{2,1,0:T(8,128)(2,1)} %g0.3), channel_id=1, source_target_pairs={{0,4},{4,0},{8,12},{12,8},{16,20},{20,16},{24,28},{28,24},{32,36},... | collective-permute-start | bytes 22020104 | tf_op jit(solution)/shard_map/ppermute | solution.py:325
  13.3 52.3 %collective-permute-start.1 = (bf16[1,7168,512]{2,1,0:T(8,128)(2,1)}, bf16[1,7168,512]{2,1,0:T(8,128)(2,1)}, u32[]{:S(2)}, u32[]{:S(2)}) collective-permute-start(bf16[1,7168,512]{2,1,0:T(8,128)(2,1)} %u0.3), channel_id=1, source_target_pairs={{0,4},{4,0},{8,12},{12,8},{16,20},{20,16},{24,28},{28,24},{32,36},... | collective-permute-start | bytes 22020104 | tf_op jit(solution)/shard_map/ppermute | solution.py:325
  60.6 12.0 %collective-permute-start.2 = (bf16[1,512,7168]{2,1,0:T(8,128)(2,1)}, bf16[1,512,7168]{2,1,0:T(8,128)(2,1)}, u32[]{:S(2)}, u32[]{:S(2)}) collective-permute-start(bf16[1,512,7168]{2,1,0:T(8,128)(2,1)} %d0.3), channel_id=1, source_target_pairs={{0,4},{4,0},{8,12},{12,8},{16,20},{20,16},{24,28},{28,24},{32,36},... | collective-permute-start | bytes 22020104 | tf_op jit(solution)/shard_map/ppermute | solution.py:333
  60.6 52.5 %all-to-all-start.1 = ((bf16[32,8,7168]{2,1,0:T(8,128)(2,1)}), bf16[32,8,7168]{2,1,0:T(8,128)(2,1)}, u32[]{:S(2)}, u32[]{:S(2)}) async-start(bf16[32,8,7168]{2,1,0:T(8,128)(2,1)} %bitcast.12), calls=%async_computation.1 | async-start | bytes 7340032 | tf_op jit(solution)/shard_map/all_to_all | solution.py:315
  113.2 52.5 %all-to-all-start.3 = ((bf16[32,8,7168]{2,1,0:T(8,128)(2,1)}), bf16[32,8,7168]{2,1,0:T(8,128)(2,1)}, u32[]{:S(2)}, u32[]{:S(2)}) async-start(bf16[32,8,7168]{2,1,0:T(8,128)(2,1)} %bitcast.11), calls=%async_computation.3 | async-start | bytes 7340032 | tf_op jit(solution)/shard_map/all_to_all | solution.py:315
  165.7 52.5 %all-to-all-start.2 = ((bf16[32,8,7168]{2,1,0:T(8,128)(2,1)}), bf16[32,8,7168]{2,1,0:T(8,128)(2,1)}, u32[]{:S(2)}, u32[]{:S(2)}) async-start(bf16[32,8,7168]{2,1,0:T(8,128)(2,1)} %bitcast.10), calls=%async_computation.2 | async-start | bytes 7340032 | tf_op jit(solution)/shard_map/all_to_all | solution.py:315

commit v12 on v11

--- a/solution.py
+++ b/solution.py
@@ -10,7 +10,7 @@
 BLOCK = 16
 LANES = 128
 CHUNKS = 2
-PIECES = 7
+PIECES = 14
 VMEM_BYTES = 56 * 1024 * 1024
 
 

time: 224 us -> 227 us (1.013)
  Pallas kernels: 80.2 us -> 85 us
    all_to_all x4, waiting for transfers between devices: 112 us -> 110 us  [exchange(): lax.all_to_all(split, 'ep', split_axis=0, concat_axis=0, tiled=True)]
    pallas_call x2, Pallas kernels: 10.2 us -> 12.6 us  [mix(): pl.pallas_call(mix_kernel, name='mix_slots', out_shape=jax.ShapeDtypeStru...]
    pallas_call x2, Pallas kernels: 8.8 us -> 11.2 us  [slots_of_tokens(): pl.pallas_call(functools.partial(pick_kernel, experts, chunk), name='pick...]
where the time goes in v12:
time: 227 us; the launch traced here: 226 us
  waiting for transfers between devices  117 us (52%)
  Pallas kernels  85 us (37%)
  starting transfers between devices  23.9 us (11%)
    all_to_all x4, waiting for transfers between devices, exchange(): lax.all_to_all(split, 'ep', split_axis=0, concat_axis=0, tiled=True)  110 us
    pallas_call x2, Pallas kernels, expert(): pl.pallas_call(functools.partial(expert_kernel, steps), name='expert_rows...  59.3 us
    all_to_all x4, starting transfers between devices, exchange(): lax.all_to_all(split, 'ep', split_axis=0, concat_axis=0, tiled=True)  23.3 us
    pallas_call x2, Pallas kernels, mix(): pl.pallas_call(mix_kernel, name='mix_slots', out_shape=jax.ShapeDtypeStru...  12.6 us
    pallas_call x2, Pallas kernels, slots_of_tokens(): pl.pallas_call(functools.partial(pick_kernel, experts, chunk), name='pick...  11.2 us
    ppermute x1, waiting for transfers between devices, on_device(): downs = (w_down, lax.ppermute(late, 'ep', pairs))  7.12 us
  transfers between devices with their start and end apart: 7, of which 5 were waited for; matrix products, arithmetic and copies ran while one was open for 0% of the time, Pallas kernels for 32%

profile of v12, /device:TPU:0, one launch (start us, length us, event | category | flops | bytes accessed | tf_op | source)
XLA Modules:
  0.0 226.1 jit_solution(1920669733470539585)
XLA Ops:
  0.0 5.5 %pick_slots.2 = bf16[256,7168]{1,0:T(8,128)(2,1)} custom-call(s32[2,128]{1,0:T(2,128)} %bitcast.14, bf16[128,7168]{1,0:T(8,128)(2,1)} %tokens_ref.3), custom_call_target="tpu_custom_call" | custom-call | tf_op jit(solution)/shard_map/pick_slots/pallas_call | solution.py:103
  5.5 8.7 %all-to-all-start = ((bf16[32,8,7168]{2,1,0:T(8,128)(2,1)}), bf16[32,8,7168]{2,1,0:T(8,128)(2,1)}, u32[]{:S(2)}, u32[]{:S(2)}) async-start(bf16[32,8,7168]{2,1,0:T(8,128)(2,1)} %bitcast.13), calls=%async_computation | async-start | bytes 7340032 | tf_op jit(solution)/shard_map/all_to_all | solution.py:315
  14.2 0.3 collective-permute-start
  14.5 0.3 collective-permute-start.1
  14.8 5.7 %pick_slots.3 = bf16[256,7168]{1,0:T(8,128)(2,1)} custom-call(s32[2,128]{1,0:T(2,128)} %bitcast.15, bf16[128,7168]{1,0:T(8,128)(2,1)} %tokens_ref.3), custom_call_target="tpu_custom_call" | custom-call | tf_op jit(solution)/shard_map/pick_slots/pallas_call | solution.py:103
  20.4 41.4 %all-to-all-done = bf16[32,8,7168]{2,1,0:T(8,128)(2,1)} async-done(((bf16[32,8,7168]{2,1,0:T(8,128)(2,1)}), bf16[32,8,7168]{2,1,0:T(8,128)(2,1)}, u32[]{:S(2)}, u32[]{:S(2)}) %all-to-all-start) | async-done | bytes 3670048 | tf_op jit(solution)/shard_map/all_to_all | solution.py:315
  61.8 0.0 collective-permute-start.2
  61.8 4.8 %all-to-all-start.1 = ((bf16[32,8,7168]{2,1,0:T(8,128)(2,1)}), bf16[32,8,7168]{2,1,0:T(8,128)(2,1)}, u32[]{:S(2)}, u32[]{:S(2)}) async-start(bf16[32,8,7168]{2,1,0:T(8,128)(2,1)} %bitcast.12), calls=%async_computation.1 | async-start | bytes 7340032 | tf_op jit(solution)/shard_map/all_to_all | solution.py:315
  66.7 0.0 collective-permute-done.g1
  66.7 0.0 collective-permute-done.1.u1
  66.7 7.1 %collective-permute-done.2.d1 = bf16[1,512,7168]{2,1,0:T(8,128)(2,1)} collective-permute-done((bf16[1,512,7168]{2,1,0:T(8,128)(2,1)}, bf16[1,512,7168]{2,1,0:T(8,128)(2,1)}, u32[]{:S(2)}, u32[]{:S(2)}) %collective-permute-start.2) | collective-permute-done | bytes 7340064 | tf_op jit(solution)/shard_map/ppermute | solution.py:333
  73.8 29.6 %expert_rows.3 = bf16[256,7168]{1,0:T(8,128)(2,1)} custom-call(bf16[256,7168]{1,0:T(8,128)(2,1)} %bitcast.3.x_ref, bf16[1,7168,512]{2,1,0:T(8,128)(2,1)} %g0.3, bf16[1,7168,512]{2,1,0:T(8,128)(2,1)} %collective-permute-done.g1, bf16[1,7168,512]{2,1,0:T(8,128)(2,1)} %u0.3, bf16[1,7168,512]{2,1,0:T(8,128)(2,1)} %collective-permute-done.1.u1, ...), custom_call_target="tpu_custom_call" | custom-call | flops 11274289152 | bytes 51380224 | tf_op jit(solution)/shard_map/expert_rows/pallas_call | solution.py:184
  103.5 10.9 %all-to-all-done.1 = bf16[32,8,7168]{2,1,0:T(8,128)(2,1)} async-done(((bf16[32,8,7168]{2,1,0:T(8,128)(2,1)}), bf16[32,8,7168]{2,1,0:T(8,128)(2,1)}, u32[]{:S(2)}, u32[]{:S(2)}) %all-to-all-start.1) | async-done | bytes 3670048 | tf_op jit(solution)/shard_map/all_to_all | solution.py:315
  114.4 4.8 %all-to-all-start.3 = ((bf16[32,8,7168]{2,1,0:T(8,128)(2,1)}), bf16[32,8,7168]{2,1,0:T(8,128)(2,1)}, u32[]{:S(2)}, u32[]{:S(2)}) async-start(bf16[32,8,7168]{2,1,0:T(8,128)(2,1)} %bitcast.11), calls=%async_computation.3 | async-start | bytes 7340032 | tf_op jit(solution)/shard_map/all_to_all | solution.py:315
  119.2 29.6 %expert_rows.2 = bf16[256,7168]{1,0:T(8,128)(2,1)} custom-call(bf16[256,7168]{1,0:T(8,128)(2,1)} %bitcast.5.x_ref, bf16[1,7168,512]{2,1,0:T(8,128)(2,1)} %g0.3, bf16[1,7168,512]{2,1,0:T(8,128)(2,1)} %collective-permute-done.g1, bf16[1,7168,512]{2,1,0:T(8,128)(2,1)} %u0.3, bf16[1,7168,512]{2,1,0:T(8,128)(2,1)} %collective-permute-done.1.u1, ...), custom_call_target="tpu_custom_call" | custom-call | flops 11274289152 | bytes 51380224 | tf_op jit(solution)/shard_map/expert_rows/pallas_call | solution.py:184
  148.9 18.0 %all-to-all-done.3 = bf16[32,8,7168]{2,1,0:T(8,128)(2,1)} async-done(((bf16[32,8,7168]{2,1,0:T(8,128)(2,1)}), bf16[32,8,7168]{2,1,0:T(8,128)(2,1)}, u32[]{:S(2)}, u32[]{:S(2)}) %all-to-all-start.3) | async-done | bytes 3670048 | tf_op jit(solution)/shard_map/all_to_all | solution.py:315
  166.9 5.0 %all-to-all-start.2 = ((bf16[32,8,7168]{2,1,0:T(8,128)(2,1)}), bf16[32,8,7168]{2,1,0:T(8,128)(2,1)}, u32[]{:S(2)}, u32[]{:S(2)}) async-start(bf16[32,8,7168]{2,1,0:T(8,128)(2,1)} %bitcast.10), calls=%async_computation.2 | async-start | bytes 7340032 | tf_op jit(solution)/shard_map/all_to_all | solution.py:315
  171.9 2.0 slot_weights.1
  173.8 6.1 %mix_slots.2.rest_0_ = bf16[128,7168]{1,0:T(8,128)(2,1)} custom-call(bf16[256,256]{1,0:T(8,128)(2,1)} %get-tuple-element.13.table_ref, bf16[256,7168]{1,0:T(8,128)(2,1)} %bitcast.9.in_ref), custom_call_target="tpu_custom_call" | custom-call | flops 939524096 | bytes 3670016 | tf_op jit(solution)/shard_map/mix_slots/pallas_call | solution.py:291
  179.9 39.5 %all-to-all-done.2 = bf16[32,8,7168]{2,1,0:T(8,128)(2,1)} async-done(((bf16[32,8,7168]{2,1,0:T(8,128)(2,1)}), bf16[32,8,7168]{2,1,0:T(8,128)(2,1)}, u32[]{:S(2)}, u32[]{:S(2)}) %all-to-all-start.2) | async-done | bytes 3670048 | tf_op jit(solution)/shard_map/all_to_all | solution.py:315
  219.4 6.5 %mix_slots.3 = bf16[128,7168]{1,0:T(8,128)(2,1)} custom-call(bf16[256,256]{1,0:T(8,128)(2,1)} %get-tuple-element.10.table_ref, bf16[256,7168]{1,0:T(8,128)(2,1)} %bitcast.7.in_ref, bf16[128,7168]{1,0:T(8,128)(2,1)} %mix_slots.2.rest_0_), custom_call_target="tpu_custom_call" | custom-call | flops 939524096 | bytes 3670016 | tf_op jit(solution)/shard_map/mix_slots/pallas_call | solution.py:291
Async XLA Ops:
  5.5 56.3 %all-to-all-start = ((bf16[32,8,7168]{2,1,0:T(8,128)(2,1)}), bf16[32,8,7168]{2,1,0:T(8,128)(2,1)}, u32[]{:S(2)}, u32[]{:S(2)}) async-start(bf16[32,8,7168]{2,1,0:T(8,128)(2,1)} %bitcast.13), calls=%async_computation | async-start | bytes 7340032 | tf_op jit(solution)/shard_map/all_to_all | solution.py:315
  14.2 52.5 %collective-permute-start = (bf16[1,7168,512]{2,1,0:T(8,128)(2,1)}, bf16[1,7168,512]{2,1,0:T(8,128)(2,1)}, u32[]{:S(2)}, u32[]{:S(2)}) collective-permute-start(bf16[1,7168,512]{2,1,0:T(8,128)(2,1)} %g0.3), channel_id=1, source_target_pairs={{0,4},{4,0},{8,12},{12,8},{16,20},{20,16},{24,28},{28,24},{32,36},... | collective-permute-start | bytes 22020104 | tf_op jit(solution)/shard_map/ppermute | solution.py:325
  14.5 52.3 %collective-permute-start.1 = (bf16[1,7168,512]{2,1,0:T(8,128)(2,1)}, bf16[1,7168,512]{2,1,0:T(8,128)(2,1)}, u32[]{:S(2)}, u32[]{:S(2)}) collective-permute-start(bf16[1,7168,512]{2,1,0:T(8,128)(2,1)} %u0.3), channel_id=1, source_target_pairs={{0,4},{4,0},{8,12},{12,8},{16,20},{20,16},{24,28},{28,24},{32,36},... | collective-permute-start | bytes 22020104 | tf_op jit(solution)/shard_map/ppermute | solution.py:325
  61.8 12.0 %collective-permute-start.2 = (bf16[1,512,7168]{2,1,0:T(8,128)(2,1)}, bf16[1,512,7168]{2,1,0:T(8,128)(2,1)}, u32[]{:S(2)}, u32[]{:S(2)}) collective-permute-start(bf16[1,512,7168]{2,1,0:T(8,128)(2,1)} %d0.3), channel_id=1, source_target_pairs={{0,4},{4,0},{8,12},{12,8},{16,20},{20,16},{24,28},{28,24},{32,36},... | collective-permute-start | bytes 22020104 | tf_op jit(solution)/shard_map/ppermute | solution.py:333
  61.8 52.5 %all-to-all-start.1 = ((bf16[32,8,7168]{2,1,0:T(8,128)(2,1)}), bf16[32,8,7168]{2,1,0:T(8,128)(2,1)}, u32[]{:S(2)}, u32[]{:S(2)}) async-start(bf16[32,8,7168]{2,1,0:T(8,128)(2,1)} %bitcast.12), calls=%async_computation.1 | async-start | bytes 7340032 | tf_op jit(solution)/shard_map/all_to_all | solution.py:315
  114.4 52.5 %all-to-all-start.3 = ((bf16[32,8,7168]{2,1,0:T(8,128)(2,1)}), bf16[32,8,7168]{2,1,0:T(8,128)(2,1)}, u32[]{:S(2)}, u32[]{:S(2)}) async-start(bf16[32,8,7168]{2,1,0:T(8,128)(2,1)} %bitcast.11), calls=%async_computation.3 | async-start | bytes 7340032 | tf_op jit(solution)/shard_map/all_to_all | solution.py:315
  166.9 52.5 %all-to-all-start.2 = ((bf16[32,8,7168]{2,1,0:T(8,128)(2,1)}), bf16[32,8,7168]{2,1,0:T(8,128)(2,1)}, u32[]{:S(2)}, u32[]{:S(2)}) async-start(bf16[32,8,7168]{2,1,0:T(8,128)(2,1)} %bitcast.10), calls=%async_computation.2 | async-start | bytes 7340032 | tf_op jit(solution)/shard_map/all_to_all | solution.py:315

commit v13 on v12

--- a/solution.py
+++ b/solution.py
@@ -10,7 +10,7 @@
 BLOCK = 16
 LANES = 128
 CHUNKS = 2
-PIECES = 14
+PIECES = 4
 VMEM_BYTES = 56 * 1024 * 1024
 
 

time: 227 us -> 224 us (0.987)
  Pallas kernels: 85 us -> 79.2 us
  waiting for transfers between devices: 117 us -> 120 us
    all_to_all x4, waiting for transfers between devices: 110 us -> 113 us  [exchange(): lax.all_to_all(split, 'ep', split_axis=0, concat_axis=0, tiled=True)]
    pallas_call x2, Pallas kernels: 11.2 us -> 8.27 us  [slots_of_tokens(): pl.pallas_call(functools.partial(pick_kernel, experts, chunk), name='pick...]
    pallas_call x2, Pallas kernels: 12.6 us -> 9.74 us  [mix(): pl.pallas_call(mix_kernel, name='mix_slots', out_shape=jax.ShapeDtypeStru...]
  transfers between devices with their start and end apart: 7 -> 7, of which waited for: 5 -> 5; matrix products, arithmetic and copies ran while one was open for 0% -> 0% of each run, Pallas kernels for 32% -> 31%
where the time goes in v13:
time: 224 us; the launch traced here: 223 us
  waiting for transfers between devices  120 us (54%)
  Pallas kernels  79.2 us (35%)
  starting transfers between devices  23.8 us (11%)
    all_to_all x4, waiting for transfers between devices, exchange(): lax.all_to_all(split, 'ep', split_axis=0, concat_axis=0, tiled=True)  113 us
    pallas_call x2, Pallas kernels, expert(): pl.pallas_call(functools.partial(expert_kernel, steps), name='expert_rows...  59.3 us
    all_to_all x4, starting transfers between devices, exchange(): lax.all_to_all(split, 'ep', split_axis=0, concat_axis=0, tiled=True)  23.2 us
    pallas_call x2, Pallas kernels, mix(): pl.pallas_call(mix_kernel, name='mix_slots', out_shape=jax.ShapeDtypeStru...  9.74 us
    pallas_call x2, Pallas kernels, slots_of_tokens(): pl.pallas_call(functools.partial(pick_kernel, experts, chunk), name='pick...  8.27 us
    ppermute x1, waiting for transfers between devices, on_device(): downs = (w_down, lax.ppermute(late, 'ep', pairs))  7.12 us
  transfers between devices with their start and end apart: 7, of which 5 were waited for; matrix products, arithmetic and copies ran while one was open for 0% of the time, Pallas kernels for 31%

profile of v13, /device:TPU:0, one launch (start us, length us, event | category | flops | bytes accessed | tf_op | source)
XLA Modules:
  0.0 223.1 jit_solution(871254658656066723)
XLA Ops:
  0.0 4.2 %pick_slots.2 = bf16[256,7168]{1,0:T(8,128)(2,1)} custom-call(s32[2,128]{1,0:T(2,128)} %bitcast.14, bf16[128,7168]{1,0:T(8,128)(2,1)} %tokens_ref.3), custom_call_target="tpu_custom_call" | custom-call | tf_op jit(solution)/shard_map/pick_slots/pallas_call | solution.py:103
  4.2 8.5 %all-to-all-start = ((bf16[32,8,7168]{2,1,0:T(8,128)(2,1)}), bf16[32,8,7168]{2,1,0:T(8,128)(2,1)}, u32[]{:S(2)}, u32[]{:S(2)}) async-start(bf16[32,8,7168]{2,1,0:T(8,128)(2,1)} %bitcast.13), calls=%async_computation | async-start | bytes 7340032 | tf_op jit(solution)/shard_map/all_to_all | solution.py:315
  12.7 0.3 collective-permute-start
  13.0 0.3 collective-permute-start.1
  13.3 4.1 %pick_slots.3 = bf16[256,7168]{1,0:T(8,128)(2,1)} custom-call(s32[2,128]{1,0:T(2,128)} %bitcast.15, bf16[128,7168]{1,0:T(8,128)(2,1)} %tokens_ref.3), custom_call_target="tpu_custom_call" | custom-call | tf_op jit(solution)/shard_map/pick_slots/pallas_call | solution.py:103
  17.4 43.0 %all-to-all-done = bf16[32,8,7168]{2,1,0:T(8,128)(2,1)} async-done(((bf16[32,8,7168]{2,1,0:T(8,128)(2,1)}), bf16[32,8,7168]{2,1,0:T(8,128)(2,1)}, u32[]{:S(2)}, u32[]{:S(2)}) %all-to-all-start) | async-done | bytes 3670048 | tf_op jit(solution)/shard_map/all_to_all | solution.py:315
  60.4 0.0 collective-permute-start.2
  60.4 4.8 %all-to-all-start.1 = ((bf16[32,8,7168]{2,1,0:T(8,128)(2,1)}), bf16[32,8,7168]{2,1,0:T(8,128)(2,1)}, u32[]{:S(2)}, u32[]{:S(2)}) async-start(bf16[32,8,7168]{2,1,0:T(8,128)(2,1)} %bitcast.12), calls=%async_computation.1 | async-start | bytes 7340032 | tf_op jit(solution)/shard_map/all_to_all | solution.py:315
  65.2 0.0 collective-permute-done.g1
  65.3 0.0 collective-permute-done.1.u1
  65.3 7.1 %collective-permute-done.2.d1 = bf16[1,512,7168]{2,1,0:T(8,128)(2,1)} collective-permute-done((bf16[1,512,7168]{2,1,0:T(8,128)(2,1)}, bf16[1,512,7168]{2,1,0:T(8,128)(2,1)}, u32[]{:S(2)}, u32[]{:S(2)}) %collective-permute-start.2) | collective-permute-done | bytes 7340064 | tf_op jit(solution)/shard_map/ppermute | solution.py:333
  72.4 29.6 %expert_rows.3 = bf16[256,7168]{1,0:T(8,128)(2,1)} custom-call(bf16[256,7168]{1,0:T(8,128)(2,1)} %bitcast.3.x_ref, bf16[1,7168,512]{2,1,0:T(8,128)(2,1)} %g0.3, bf16[1,7168,512]{2,1,0:T(8,128)(2,1)} %collective-permute-done.g1, bf16[1,7168,512]{2,1,0:T(8,128)(2,1)} %u0.3, bf16[1,7168,512]{2,1,0:T(8,128)(2,1)} %collective-permute-done.1.u1, ...), custom_call_target="tpu_custom_call" | custom-call | flops 11274289152 | bytes 51380224 | tf_op jit(solution)/shard_map/expert_rows/pallas_call | solution.py:184
  102.0 10.9 %all-to-all-done.1 = bf16[32,8,7168]{2,1,0:T(8,128)(2,1)} async-done(((bf16[32,8,7168]{2,1,0:T(8,128)(2,1)}), bf16[32,8,7168]{2,1,0:T(8,128)(2,1)}, u32[]{:S(2)}, u32[]{:S(2)}) %all-to-all-start.1) | async-done | bytes 3670048 | tf_op jit(solution)/shard_map/all_to_all | solution.py:315
  112.9 4.8 %all-to-all-start.3 = ((bf16[32,8,7168]{2,1,0:T(8,128)(2,1)}), bf16[32,8,7168]{2,1,0:T(8,128)(2,1)}, u32[]{:S(2)}, u32[]{:S(2)}) async-start(bf16[32,8,7168]{2,1,0:T(8,128)(2,1)} %bitcast.11), calls=%async_computation.3 | async-start | bytes 7340032 | tf_op jit(solution)/shard_map/all_to_all | solution.py:315
  117.8 29.6 %expert_rows.2 = bf16[256,7168]{1,0:T(8,128)(2,1)} custom-call(bf16[256,7168]{1,0:T(8,128)(2,1)} %bitcast.5.x_ref, bf16[1,7168,512]{2,1,0:T(8,128)(2,1)} %g0.3, bf16[1,7168,512]{2,1,0:T(8,128)(2,1)} %collective-permute-done.g1, bf16[1,7168,512]{2,1,0:T(8,128)(2,1)} %u0.3, bf16[1,7168,512]{2,1,0:T(8,128)(2,1)} %collective-permute-done.1.u1, ...), custom_call_target="tpu_custom_call" | custom-call | flops 11274289152 | bytes 51380224 | tf_op jit(solution)/shard_map/expert_rows/pallas_call | solution.py:184
  147.4 18.0 %all-to-all-done.3 = bf16[32,8,7168]{2,1,0:T(8,128)(2,1)} async-done(((bf16[32,8,7168]{2,1,0:T(8,128)(2,1)}), bf16[32,8,7168]{2,1,0:T(8,128)(2,1)}, u32[]{:S(2)}, u32[]{:S(2)}) %all-to-all-start.3) | async-done | bytes 3670048 | tf_op jit(solution)/shard_map/all_to_all | solution.py:315
  165.4 5.0 %all-to-all-start.2 = ((bf16[32,8,7168]{2,1,0:T(8,128)(2,1)}), bf16[32,8,7168]{2,1,0:T(8,128)(2,1)}, u32[]{:S(2)}, u32[]{:S(2)}) async-start(bf16[32,8,7168]{2,1,0:T(8,128)(2,1)} %bitcast.10), calls=%async_computation.2 | async-start | bytes 7340032 | tf_op jit(solution)/shard_map/all_to_all | solution.py:315
  170.4 2.0 slot_weights.1
  172.4 4.7 %mix_slots.2.rest_0_ = bf16[128,7168]{1,0:T(8,128)(2,1)} custom-call(bf16[256,256]{1,0:T(8,128)(2,1)} %get-tuple-element.13.table_ref, bf16[256,7168]{1,0:T(8,128)(2,1)} %bitcast.9.in_ref), custom_call_target="tpu_custom_call" | custom-call | flops 939524096 | bytes 3670016 | tf_op jit(solution)/shard_map/mix_slots/pallas_call | solution.py:291
  177.1 40.8 %all-to-all-done.2 = bf16[32,8,7168]{2,1,0:T(8,128)(2,1)} async-done(((bf16[32,8,7168]{2,1,0:T(8,128)(2,1)}), bf16[32,8,7168]{2,1,0:T(8,128)(2,1)}, u32[]{:S(2)}, u32[]{:S(2)}) %all-to-all-start.2) | async-done | bytes 3670048 | tf_op jit(solution)/shard_map/all_to_all | solution.py:315
  217.9 5.0 %mix_slots.3 = bf16[128,7168]{1,0:T(8,128)(2,1)} custom-call(bf16[256,256]{1,0:T(8,128)(2,1)} %get-tuple-element.10.table_ref, bf16[256,7168]{1,0:T(8,128)(2,1)} %bitcast.7.in_ref, bf16[128,7168]{1,0:T(8,128)(2,1)} %mix_slots.2.rest_0_), custom_call_target="tpu_custom_call" | custom-call | flops 939524096 | bytes 3670016 | tf_op jit(solution)/shard_map/mix_slots/pallas_call | solution.py:291
Async XLA Ops:
  4.2 56.2 %all-to-all-start = ((bf16[32,8,7168]{2,1,0:T(8,128)(2,1)}), bf16[32,8,7168]{2,1,0:T(8,128)(2,1)}, u32[]{:S(2)}, u32[]{:S(2)}) async-start(bf16[32,8,7168]{2,1,0:T(8,128)(2,1)} %bitcast.13), calls=%async_computation | async-start | bytes 7340032 | tf_op jit(solution)/shard_map/all_to_all | solution.py:315
  12.7 52.5 %collective-permute-start = (bf16[1,7168,512]{2,1,0:T(8,128)(2,1)}, bf16[1,7168,512]{2,1,0:T(8,128)(2,1)}, u32[]{:S(2)}, u32[]{:S(2)}) collective-permute-start(bf16[1,7168,512]{2,1,0:T(8,128)(2,1)} %g0.3), channel_id=1, source_target_pairs={{0,4},{4,0},{8,12},{12,8},{16,20},{20,16},{24,28},{28,24},{32,36},... | collective-permute-start | bytes 22020104 | tf_op jit(solution)/shard_map/ppermute | solution.py:325
  13.0 52.3 %collective-permute-start.1 = (bf16[1,7168,512]{2,1,0:T(8,128)(2,1)}, bf16[1,7168,512]{2,1,0:T(8,128)(2,1)}, u32[]{:S(2)}, u32[]{:S(2)}) collective-permute-start(bf16[1,7168,512]{2,1,0:T(8,128)(2,1)} %u0.3), channel_id=1, source_target_pairs={{0,4},{4,0},{8,12},{12,8},{16,20},{20,16},{24,28},{28,24},{32,36},... | collective-permute-start | bytes 22020104 | tf_op jit(solution)/shard_map/ppermute | solution.py:325
  60.4 12.0 %collective-permute-start.2 = (bf16[1,512,7168]{2,1,0:T(8,128)(2,1)}, bf16[1,512,7168]{2,1,0:T(8,128)(2,1)}, u32[]{:S(2)}, u32[]{:S(2)}) collective-permute-start(bf16[1,512,7168]{2,1,0:T(8,128)(2,1)} %d0.3), channel_id=1, source_target_pairs={{0,4},{4,0},{8,12},{12,8},{16,20},{20,16},{24,28},{28,24},{32,36},... | collective-permute-start | bytes 22020104 | tf_op jit(solution)/shard_map/ppermute | solution.py:333
  60.4 52.5 %all-to-all-start.1 = ((bf16[32,8,7168]{2,1,0:T(8,128)(2,1)}), bf16[32,8,7168]{2,1,0:T(8,128)(2,1)}, u32[]{:S(2)}, u32[]{:S(2)}) async-start(bf16[32,8,7168]{2,1,0:T(8,128)(2,1)} %bitcast.12), calls=%async_computation.1 | async-start | bytes 7340032 | tf_op jit(solution)/shard_map/all_to_all | solution.py:315
  112.9 52.5 %all-to-all-start.3 = ((bf16[32,8,7168]{2,1,0:T(8,128)(2,1)}), bf16[32,8,7168]{2,1,0:T(8,128)(2,1)}, u32[]{:S(2)}, u32[]{:S(2)}) async-start(bf16[32,8,7168]{2,1,0:T(8,128)(2,1)} %bitcast.11), calls=%async_computation.3 | async-start | bytes 7340032 | tf_op jit(solution)/shard_map/all_to_all | solution.py:315
  165.4 52.5 %all-to-all-start.2 = ((bf16[32,8,7168]{2,1,0:T(8,128)(2,1)}), bf16[32,8,7168]{2,1,0:T(8,128)(2,1)}, u32[]{:S(2)}, u32[]{:S(2)}) async-start(bf16[32,8,7168]{2,1,0:T(8,128)(2,1)} %bitcast.10), calls=%async_computation.2 | async-start | bytes 7340032 | tf_op jit(solution)/shard_map/all_to_all | solution.py:315
